TPU v7x, 1024 devices: a whole 4x8x16 slice. The times are simulated.
1024 devices in a mesh: lat: 128 (over z_lo, x, y), lon: 8 (over z_hi, core).
Axes of the slice: x: 4, y: 8, z: 16 (z_hi: 4, z_lo: 4; z = z_hi * 4 + z_lo), core: 2. Of those that a mesh axis runs over, the one named last changes fastest.
Arguments:
- fields: bfloat16 [512, 576, 256], P('lat', 'lon'), may hold values from -6 to 6
- basis: bfloat16 [512, 25, 9, 25], P('lat'), may hold values from -0.375 to 0.375
- spans: int32 [512, 25], P('lat'), may hold values from 0 to 12, as said below
- weight: bfloat16 [256, 2304], P('lat'), may hold values from -0.125 to 0.125
- cotangent: bfloat16 [512, 576, 256], P('lat', 'lon'), may hold values from -24 to 24
Outputs:
- output: bfloat16 [512, 576, 256], P('lat', 'lon')
- grad_weight: float32 [256, 2304], P('lat')
Inputs may be any that keep to these rules, and one draw needn't show every extreme that they name: Rows near the two ends of the band have wider spans.
All inputs are finite; a program needn't handle non-finite values.
Results may differ from a plain program's by a relative error of at most 0.013.
Values may be sent and summed in bfloat16 or wider, within the bound.
No kernel may reach another device: no remote copies, remote signals or barrier semaphores. Data moves between devices by JAX's collectives and lax.ppermute only.
A program may use at most 32 MiB of HBM per device.

v0:
```python
import math

import jax
import jax.numpy as jnp
from jax import lax
from jax.sharding import PartitionSpec as P

TILE = 12


def passed_along(shard, axis, by):
    count = lax.axis_size(axis)
    pairs = [(i, i + by) for i in range(count) if 0 <= i + by < count]
    return lax.ppermute(shard, axis, pairs)


def padded(block, sides, width):
    for axis, dim in sides:
        count = lax.axis_size(axis)
        forward = [(i, i + 1) for i in range(count - 1)]
        forward.append((count - 1, 0))
        backward = [(target, source) for source, target in forward]
        low = lax.ppermute(
            lax.slice_in_dim(block, block.shape[dim] - width, None, axis=dim), axis, forward
        )
        high = lax.ppermute(lax.slice_in_dim(block, 0, width, axis=dim), axis, backward)
        block = jnp.concatenate([low, block, high], axis=dim)
    return block


def shards(fields, basis, spans, weight, cotangent):
    row_count, col_count, channel_count_total = fields.shape
    row_extent = basis.shape[1]
    nbasis = basis.shape[2]
    col_span = basis.shape[3]
    lat_reach = (row_extent - 1) // 2
    lon_reach = (col_span - 1) // 2
    offsets = jnp.arange(col_span) - lon_reach
    validity = jnp.abs(offsets)[None, None, :] <= spans[:, :, None]
    masked = jnp.where(validity[:, :, None, :], basis, jnp.zeros_like(basis))
    band_count = (lat_reach + row_count - 1) // row_count
    shifted_rows = {}
    for distance in range(1, band_count + 1):
        for direction in (1, -1):
            shifted_rows[direction * distance] = passed_along(fields, "lat", direction * distance)
    upper_rows = [shifted_rows[distance] for distance in range(band_count, 0, -1)]
    lower_rows = [shifted_rows[-distance] for distance in range(1, band_count + 1)]
    stacked = jnp.concatenate(upper_rows + [fields] + lower_rows, axis=0)
    extended = padded(stacked, (("lon", 1),), lon_reach)
    tile_columns = TILE
    tile_count = col_count // tile_columns
    tile_span = tile_columns + 2 * lon_reach
    selector = (
        jnp.arange(tile_span)[None, :, None] - jnp.arange(tile_columns)[:, None, None]
        == jnp.arange(col_span)[None, None, :]
    ).astype(jnp.bfloat16)

    def row_features(row_index):
        row_basis = lax.dynamic_index_in_dim(masked, row_index, 0, keepdims=False)
        latitude_band_block = jnp.einsum(
            "rkw,jvw->jkrv", row_basis, selector, preferred_element_type=jnp.float32
        ).astype(jnp.bfloat16)
        latitude_band_block = latitude_band_block.reshape(
            tile_columns * nbasis, row_extent * tile_span
        )
        window = lax.dynamic_slice_in_dim(extended, row_index, row_extent, 0)
        sliding_windows = jnp.stack(
            [
                lax.slice_in_dim(
                    window, tile_index * tile_columns, tile_index * tile_columns + tile_span, axis=1
                )
                for tile_index in range(tile_count)
            ]
        )
        sliding_windows = sliding_windows.reshape(
            tile_count, row_extent * tile_span, channel_count_total
        )
        reduced_total = jnp.einsum(
            "hz,qzk->qhk", latitude_band_block, sliding_windows, preferred_element_type=jnp.float32
        )
        return reduced_total.reshape(col_count, nbasis, channel_count_total).astype(jnp.bfloat16)

    features = lax.map(row_features, jnp.arange(row_count))
    cell_count = row_count * col_count
    flat_features = features.reshape(cell_count, nbasis * channel_count_total)
    grads_flat = cotangent.reshape(cell_count, channel_count_total)
    scale = 1.0 / math.sqrt(row_count * lax.axis_size("lat") * col_count * lax.axis_size("lon"))
    mixed = lax.dot_general(
        flat_features,
        lax.all_gather(weight, "lat", axis=0, tiled=True),
        (((1,), (1,)), ((), ())),
        preferred_element_type=jnp.float32,
    )
    output = mixed.astype(jnp.bfloat16)
    output = output.reshape(row_count, col_count, channel_count_total)
    term = lax.dot_general(
        grads_flat, flat_features, (((0,), (0,)), ((), ())), preferred_element_type=jnp.float32
    )
    local_grad = lax.psum_scatter(term * scale, "lat", scatter_dimension=0, tiled=True)
    grad_weight = lax.psum(local_grad, "lon")
    return (output, grad_weight)


def solution(mesh):
    return jax.shard_map(
        shards,
        mesh=mesh,
        in_specs=(
            P("lat", "lon", None),
            P("lat", None, None, None),
            P("lat", None),
            P("lat", None),
            P("lat", "lon", None),
        ),
        out_specs=(P("lat", "lon", None), P("lat", None)),
        check_vma=False,
    )
```

profile of v0, /device:TPU:1, one launch (start us, length us, event | category | flops | bytes accessed | tf_op | source)
XLA Modules:
  0.0 2185.9 jit_solution(17344223361845571116)
XLA Ops:
  7.2 6.2 collective-permute-start
  13.4 4.5 collective-permute-start.1
  18.0 2.3 collective-permute-start.2
  25.1 4.5 collective-permute-done.2
  31.8 1.8 collective-permute-done.5
  33.6 27.7 %collective-permute-start.6 = (bf16[28,12,256]{2,1,0:T(8,128)(2,1)S(1)}, bf16[28,12,256]{2,1,0:T(8,128)(2,1)S(1)}, u32[]{:S(2)}, u32[]{:S(2)}) collective-permute-start(bf16[28,12,256]{2,1,0:T(8,128)(2,1)S(1)} %get-tuple-element.74), channel_id=1, source_target_pairs={{0,1},{1,2},{2,3},{3,4},{4,5},{5,6},{6,7},{7,0},{8,9},{9,10},{10,1... | collective-permute-start | bytes 516104 | tf_op jit(solution)/shard_map/ppermute | solution.py:23
  61.4 1.9 collective-permute-start.7
  64.4 15.5 collective-permute-done.7
  80.6 80.1 %while.11 = (s32[]{:T(128)}, bf16[4,72,9,256]{3,2,1,0:T(8,128)(2,1)}, s32[4]{0:T(128)S(1)}, bf16[28,96,256]{2,1,0:T(8,128)(2,1)S(1)}, bf16[4,25,9,25]{3,1,2,0:T(...) while((s32[]{:T(128)}, ...), condition=%wide.region_1.2_spmd.clone, body=%wide.region_0.1_spmd.clone.sunk | while | flops 303743104 | bytes 22525484 | solution.py:83
  83.1 1.7 constant_dynamic-slice_fusion.8
  97.2 2.4 fusion.30
  103.2 1.7 constant_dynamic-slice_fusion.8
  117.3 2.4 fusion.30
  123.2 1.7 constant_dynamic-slice_fusion.8
  137.3 2.3 fusion.30
  143.2 1.7 constant_dynamic-slice_fusion.8
  157.3 2.4 fusion.30
  160.6 2.3 copy.18
  162.9 2.2 fusion.11
  167.1 467.7 %all-gather.3.cloned.1.call-done = bf16[128,2,2304]{2,1,0:T(2,128)(2,1)} async-done(((bf16[1,2,2304]{2,1,0:T(2,128)(2,1)}), bf16[128,2,2304]{2,1,0:T(2,128)(2,1)}) %all-gather.3.cloned.1.call-update) | async-done | bytes 1179664 | tf_op jit(solution)/shard_map/all_gather | solution.py:90
  634.9 2.9 reshape.67
  639.0 1387.8 %all-reduce.3.cloned.1.call-done = f32[256,2304]{0,1:T(8,128)} async-done(((f32[256,2304]{0,1:T(8,128)}), f32[256,2304]{0,1:T(8,128)}) %all-reduce.3.cloned.1.call-update) | async-done | bytes 2359312
  2026.8 1.6 constant_dynamic-slice_fusion.6
  2028.4 149.7 %psum.7 = f32[2,2304]{0,1:T(8,128)S(1)} all-reduce(f32[2,2304]{0,1:T(8,128)S(1)} %constant_dynamic-slice_fusion.6), channel_id=1, replica_groups=mesh['lat'=128,'lon'=8] {'lon'}, use_global_device_ids=true, to_apply=%region_3.4 | all-reduce | flops 4608 | bytes 36864 | tf_op jit(solution)/shard_map/psum | solution.py:100
  (106 shorter events, 62.6 us)
Async XLA Ops:
  7.2 155.8 %copy-start = (bf16[4,72,256]{2,1,0:T(8,128)(2,1)S(1)}, bf16[4,72,256]{2,1,0:T(8,128)(2,1)}, u32[]{:S(2)}) copy-start(bf16[4,72,256]{2,1,0:T(8,128)(2,1)} %param.11) | copy-start | bytes 442372
  7.2 56.2 %copy-start.1 = (bf16[4,25,9,25]{3,0,2,1:T(4,128)(2,1)S(1)}, bf16[4,25,9,25]{3,0,2,1:T(4,128)(2,1)}, u32[]{:S(2)}) copy-start(bf16[4,25,9,25]{3,0,2,1:T(4,128)(2,1)} %param.8) | copy-start | bytes 135004
  7.2 627.7 %all-gather.3.cloned.1.call-start = ((), (), s32[]{:S(2)}) async-start(), calls=%async_computation | async-start | bytes 1188864 | tf_op jit(solution)/shard_map/all_gather | solution.py:90
  7.2 16.5 collective-permute-start
  13.4 11.7 collective-permute-start.1
  18.0 11.7 collective-permute-start.2
  20.3 10.3 collective-permute-start.3
  21.6 10.2 collective-permute-start.4
  22.9 2003.8 %all-reduce.3.cloned.1.call-start = ((), (), s32[]{:S(2)}) async-start(), calls=%async_computation.1 | async-start | bytes 4718592
  23.8 9.8 collective-permute-start.5
  33.6 30.8 %collective-permute-start.6 = (bf16[28,12,256]{2,1,0:T(8,128)(2,1)S(1)}, bf16[28,12,256]{2,1,0:T(8,128)(2,1)S(1)}, u32[]{:S(2)}, u32[]{:S(2)}) collective-permute-start(bf16[28,12,256]{2,1,0:T(8,128)(2,1)S(1)} %get-tuple-element.74), channel_id=1, source_target_pairs={{0,1},{1,2},{2,3},{3,4},{4,5},{5,6},{6,7},{7,0},{8,9},{9,10},{10,1... | collective-permute-start | bytes 516104 | tf_op jit(solution)/shard_map/ppermute | solution.py:23
  61.4 18.5 collective-permute-start.7
Sparse Core Ops, SparseCore 0:
  23.0 611.7 all-gather.2
  638.4 1388.3 all-reduce.2
where the time goes:
time: 2190 us
  waiting for transfers between devices  1880 us (86%)
  blocking collectives  150 us (7%)
  local copies, waits for them, and re-layouts  62.6 us (3%)
  starting transfers between devices  46.7 us (2%)
    unnamed x3, waiting for transfers between devices  1390 us
    all_gather x1, waiting for transfers between devices, shards(): lax.all_gather(weight, 'lat', axis=0, tiled=True)  468 us
    psum x1, blocking collectives, shards(): grad_weight = lax.psum(local_grad, 'lon')  150 us
  transfers between devices with their start and end apart: 10, of which 7 were waited for; matrix products, arithmetic and copies ran while one was open for 4% of the time, Pallas kernels for 0%

commit v1 on v0

v1 whole, which is shorter than its diff:
```python
import math

import jax
import jax.numpy as jnp
from jax import lax
from jax.experimental import pallas as pl
from jax.experimental.pallas import tpu as pltpu
from jax.sharding import PartitionSpec as P

FACTORS = {128: (4, 4, 8), 8: (2, 2, 2)}
TILE = 8


def dot(a, b, contract):
    return lax.dot_general(a, b, (contract, ((), ())), preferred_element_type=jnp.float32)


def lat_index(z, x, y, factors):
    return (z * factors[1] + x) * factors[2] + y


def lat_coords(index, factors):
    return index // (factors[1] * factors[2]), index // factors[2] % factors[1], index % factors[2]


def along(block, dim, step, factors):
    pairs = []
    for source in range(factors[0] * factors[1] * factors[2]):
        coords = list(lat_coords(source, factors))
        coords[dim] = (coords[dim] + step) % factors[dim]
        pairs.append((source, lat_index(*coords, factors)))
    return lax.ppermute(block, "lat", pairs)


def swapped_lat(block, bit):
    return lax.ppermute(block, "lat", [(i, i ^ bit) for i in range(lax.axis_size("lat"))])


def swapped_core(block):
    return lax.ppermute(block, "lon", [(i, i ^ 1) for i in range(lax.axis_size("lon"))])


def along_lon(block, step):
    count = lax.axis_size("lon")
    return lax.ppermute(block, "lon", [(i, (i + step) % count) for i in range(count)])


def passed_along(block, by):
    count = lax.axis_size("lat")
    return lax.ppermute(block, "lat", [(i, i + by) for i in range(count) if 0 <= i + by < count])


def band_kernel(rows_ref, band_ref):
    count, width = rows_ref.shape
    for start in range(0, count, 2):
        pair = []
        for row in (start, start + 1):
            spread = jnp.broadcast_to(rows_ref[row : row + 1, :], (TILE, width))
            pair.append(pltpu.roll(spread, 0, 1, stride=1, stride_axis=0))
        both = jnp.concatenate(pair, axis=0).astype(jnp.bfloat16)
        band_ref[start * TILE : (start + 2) * TILE, :] = both


def feature_kernel(nbasis, tile_count, *refs):
    band_ref, cot_ref = refs[0], refs[1]
    window_refs = refs[2:9]
    features_ref, keep_ref, send_ref = refs[9:]
    rows = window_refs[0].shape[0]
    reach = band_ref.shape[1] // (7 * rows)
    per_tile = rows * TILE
    band = band_ref[...]
    for tile in range(tile_count):
        pieces = []
        for ref in window_refs:
            for row in range(rows):
                pieces.append(ref[row, tile * TILE : tile * TILE + reach, :])
        window = jnp.concatenate(pieces, axis=0)
        summed = dot(band, window, ((1,), (0,))).astype(jnp.bfloat16)
        for k in range(nbasis):
            features_ref[k, tile * per_tile : (tile + 1) * per_tile, :] = summed[
                k * per_tile : (k + 1) * per_tile
            ]
    half = cot_ref.shape[0] // 2
    channels = features_ref.shape[2]
    for k in range(nbasis):
        term = dot(cot_ref[...], features_ref[k], ((1,), (0,)))
        span = slice(k * channels, (k + 1) * channels)
        keep_ref[:, span] = term[:half].astype(keep_ref.dtype)
        send_ref[:, span] = term[half:].astype(send_ref.dtype)


def output_kernel(tile_count, features_ref, weight_ref, order_ref, output_ref):
    nbasis, cells, channels = features_ref.shape
    rows = output_ref.shape[0]
    total = jnp.zeros((cells, weight_ref.shape[0]), jnp.float32)
    for k in range(nbasis):
        piece = weight_ref[:, k * channels : (k + 1) * channels]
        total = total + dot(features_ref[k], piece, ((1,), (1,)))
    mixed = dot(total.astype(jnp.bfloat16), order_ref[...], ((1,), (0,))).astype(jnp.bfloat16)
    for tile in range(tile_count):
        for row in range(rows):
            start = (tile * rows + row) * TILE
            output_ref[row, tile * TILE : (tile + 1) * TILE, :] = mixed[start : start + TILE]


def vmem(count):
    return [pl.BlockSpec(memory_space=pltpu.VMEM)] * count


def shards(fields, basis, spans, weight, cotangent):
    rows, cols, channels = fields.shape
    extent, nbasis, width = basis.shape[1:]
    outs = cotangent.shape[2]
    reach = (width - 1) // 2
    factors = FACTORS[lax.axis_size("lat")]
    lat = lax.axis_index("lat")
    lon = lax.axis_index("lon")
    core = lon % 2
    z_at, x_at, y_at = lat_coords(lat, factors)
    tile_count = cols // TILE
    window_rows = extent + rows - 1
    window_cols = TILE + width - 1
    cells = rows * cols
    bf16 = jnp.bfloat16

    left = along_lon(fields[:, cols - reach :], 1)
    right = along_lon(fields[:, :reach], -1)
    own = jnp.concatenate([left, fields, right], axis=1)
    below, above = [own], [own]
    for _ in range(3):
        below.append(passed_along(below[-1], 1))
        above.append(passed_along(above[-1], -1))
    windows = below[:0:-1] + [own] + above[1:]

    gathered = lax.dynamic_slice_in_dim(weight, core, 1, 0)
    bit = 1
    while bit < lax.axis_size("lat"):
        gathered = jnp.concatenate([gathered, swapped_lat(gathered, bit)], axis=0)
        bit *= 2
    all_weight = jnp.concatenate([gathered, swapped_core(gathered)], axis=0)
    position = jnp.arange(outs)
    half = outs // 2
    weight_row = 2 * (lat ^ (position % half)) + (core ^ (position // half))
    weight_order = (weight_row[:, None] == jnp.arange(outs)[None, :]).astype(bf16)

    offsets = jnp.arange(width) - reach
    validity = jnp.abs(offsets)[None, None, :] <= spans[:, :, None]
    masked = jnp.where(validity[:, :, None, :], basis, jnp.zeros_like(basis))
    masked = jnp.transpose(masked, (2, 0, 1, 3)).astype(jnp.float32)
    band_rows = jnp.stack(
        [
            jnp.pad(masked[:, row], ((0, 0), (row, rows - 1 - row), (0, window_cols - width)))
            for row in range(rows)
        ],
        axis=1,
    ).reshape(nbasis * rows, window_rows * window_cols)
    band = pl.pallas_call(
        band_kernel,
        out_shape=jax.ShapeDtypeStruct((nbasis * rows * TILE, window_rows * window_cols), bf16),
        in_specs=vmem(1),
        out_specs=pl.BlockSpec(memory_space=pltpu.VMEM),
    )(band_rows)

    zs, xs, ys = factors
    away = (
        2
        * lat_index(
            (z_at + position // ys % zs) % zs,
            (x_at + position // (ys * zs) % xs) % xs,
            (y_at + position % ys) % ys,
            factors,
        )
        + (core ^ (position // half))
    )
    cot_order = (away[:, None] == jnp.arange(outs)[None, :]).astype(bf16)
    cot_cells = jnp.transpose(cotangent.reshape(rows, tile_count, TILE, outs), (1, 0, 2, 3))
    cot = dot(cot_order, cot_cells.reshape(cells, outs), ((1,), (1,))).astype(bf16)

    features, keep, send = pl.pallas_call(
        lambda *refs: feature_kernel(nbasis, tile_count, *refs),
        out_shape=(
            jax.ShapeDtypeStruct((nbasis, cells, channels), bf16),
            jax.ShapeDtypeStruct((half, nbasis * channels), bf16),
            jax.ShapeDtypeStruct((half, nbasis * channels), bf16),
        ),
        in_specs=vmem(9),
        out_specs=tuple(vmem(3)),
        name="features",
    )(band, cot, *windows)

    output = pl.pallas_call(
        lambda *refs: output_kernel(tile_count, *refs),
        out_shape=jax.ShapeDtypeStruct((rows, cols, outs), bf16),
        in_specs=vmem(3),
        out_specs=pl.BlockSpec(memory_space=pltpu.VMEM),
        name="mixing",
    )(features, all_weight, weight_order)

    f32 = jnp.float32
    total = keep.astype(f32) + swapped_core(send).astype(f32)
    for dim in (1, 0, 2):
        count = factors[dim]
        piece = total.shape[0] // count
        moved = total if dim == 2 else total.astype(bf16)
        arrived = [
            along(moved[step * piece : (step + 1) * piece], dim, step, factors)
            for step in range(1, count)
        ]
        total = total[:piece]
        for part in arrived:
            total = total + part.astype(f32)
    hi = lax.axis_size("lon") // 2
    if hi == 4:
        one, two, three = (along_lon(total, 2 * step) for step in (1, 2, 3))
        total = (total + two) + (one + three)
    scale = 1.0 / math.sqrt(rows * lax.axis_size("lat") * cols * lax.axis_size("lon"))
    total = total * scale
    other = swapped_core(total)
    grad_weight = jnp.where(
        core == 0,
        jnp.concatenate([total, other], axis=0),
        jnp.concatenate([other, total], axis=0),
    )
    return (output, grad_weight)


def solution(mesh):
    return jax.shard_map(
        shards,
        mesh=mesh,
        in_specs=(
            P("lat", "lon", None),
            P("lat", None, None, None),
            P("lat", None),
            P("lat", None),
            P("lat", "lon", None),
        ),
        out_specs=(P("lat", "lon", None), P("lat", None)),
        check_vma=False,
    )
```

time: 2190 us -> 189 us (0.09)
  waiting for transfers between devices: 1880 us -> 11.6 us
  blocking collectives: 150 us -> 0 us
  starting transfers between devices: 46.7 us -> 150 us
  local copies, waits for them, and re-layouts: 62.6 us -> 10.1 us
    unnamed x3 -> x0, waiting for transfers between devices: 1390 us -> none
    all_gather x1 -> x0, waiting for transfers between devices: 468 us -> none  [shards(): lax.all_gather(weight, 'lat', axis=0, tiled=True)]
    psum x1 -> x0, blocking collectives: 150 us -> none  [shards(): grad_weight = lax.psum(local_grad, 'lon')]
    ppermute x8 -> x34, starting transfers between devices: 46.6 us -> 150 us  [the longest x13 51.2 us: along(): return lax.ppermute(block, 'lat', pairs)]
  transfers between devices with their start and end apart: 10 -> 34, of which waited for: 7 -> 5; matrix products, arithmetic and copies ran while one was open for 4% -> 7% of each run, Pallas kernels for 0% -> 5%
where the time goes in v1:
time: 189 us; the launch traced here: 188 us
  starting transfers between devices  150 us (79%)
  waiting for transfers between devices  11.6 us (6%)
  local copies, waits for them, and re-layouts  10.1 us (5%)
  Pallas kernels  10.1 us (5%)
  other arithmetic  4.83 us (3%)
    ppermute x13, starting transfers between devices, along(): return lax.ppermute(block, 'lat', pairs)  51.2 us
    ppermute x5, starting transfers between devices, along_lon(): lax.ppermute(block, 'lon', [(i, (i + step) % count) for i in range(count)])  38.7 us
    ppermute x3, starting transfers between devices, swapped_core(): lax.ppermute(block, 'lon', [(i, i ^ 1) for i in range(lax.axis_size('lon'...  23.1 us
    ppermute x7, starting transfers between devices, swapped_lat(): lax.ppermute(block, 'lat', [(i, i ^ bit) for i in range(lax.axis_size('la...  21.5 us
    ppermute x6, starting transfers between devices, passed_along(): lax.ppermute(block, 'lat', [(i, i + by) for i in range(count) if 0 <= i +...  15.1 us
    ppermute x6, waiting for transfers between devices, passed_along(): lax.ppermute(block, 'lat', [(i, i + by) for i in range(count) if 0 <= i +...  7.01 us
    concatenate x1, local copies, waits for them, and re-layouts, shards(): all_weight = jnp.concatenate([gathered, swapped_core(gathered)], axis=0)  6.01 us
    pallas_call x1, Pallas kernels, shards(): pl.pallas_call(lambda *refs: feature_kernel(nbasis, tile_count, *refs), o...  5.15 us
  transfers between devices with their start and end apart: 34, of which 5 were waited for; matrix products, arithmetic and copies ran while one was open for 7% of the time, Pallas kernels for 5%

profile of v1, /device:TPU:1, one launch (start us, length us, event | category | flops | bytes accessed | tf_op | source)
XLA Modules:
  0.0 188.0 jit_solution(15919017210329036247)
XLA Ops:
  1.5 12.0 %collective-permute-start = (bf16[4,12,256]{2,1,0:T(8,128)(2,1)S(1)}, bf16[4,12,256]{2,1,0:T(8,128)(2,1)S(1)}, u32[]{:S(2)}, u32[]{:S(2)}) collective-permute-start(bf16[4,12,256]{2,1,0:T(8,128)(2,1)S(1)} %get-tuple-element.22), channel_id=1, source_target_pairs={{0,1},{1,2},{2,3},{3,4},{4,5},{5,6},{6,7},{7,0},{8,9},{9,10},{10,1... | collective-permute-start | bytes 73736 | tf_op jit(solution)/shard_map/ppermute | solution.py:45
  13.5 6.0 %collective-permute-start.1 = (bf16[4,12,256]{2,1,0:T(8,128)(2,1)S(1)}, bf16[4,12,256]{2,1,0:T(8,128)(2,1)S(1)}, u32[]{:S(2)}, u32[]{:S(2)}) collective-permute-start(bf16[4,12,256]{2,1,0:T(8,128)(2,1)S(1)} %get-tuple-element.23), channel_id=1, source_target_pairs={{0,7},{1,0},{2,1},{3,2},{4,3},{5,4},{6,5},{7,6},{8,15},{9,8},{10,9... | collective-permute-start | bytes 73736 | tf_op jit(solution)/shard_map/ppermute | solution.py:45
  23.5 3.4 %collective-permute-start.2 = (bf16[4,96,256]{2,1,0:T(8,128)(2,1)S(1)}, bf16[4,96,256]{2,1,0:T(8,128)(2,1)S(1)}, u32[]{:S(2)}, u32[]{:S(2)}) collective-permute-start(bf16[4,96,256]{2,1,0:T(8,128)(2,1)S(1)} %pad_maximum_fusion.1.refs_5_), channel_id=1, source_target_pairs={{0,8},{8,16},{16,24},{24,32},{32,40},{40,48},{48,56},{56,64},{64,7... | collective-permute-start | bytes 589832 | tf_op jit(solution)/shard_map/ppermute | solution.py:50
  29.6 3.8 %collective-permute-start.3 = (bf16[4,96,256]{2,1,0:T(8,128)(2,1)S(1)}, bf16[4,96,256]{2,1,0:T(8,128)(2,1)S(1)}, u32[]{:S(2)}, u32[]{:S(2)}) collective-permute-start(bf16[4,96,256]{2,1,0:T(8,128)(2,1)S(1)} %collective-permute-done.2.refs_4_), channel_id=1, source_target_pairs={{0,8},{8,16},{16,24},{24,32},{32,40},{40,48},{48,56},{56,64},{64,7... | collective-permute-start | bytes 589832 | tf_op jit(solution)/shard_map/ppermute | solution.py:50
  38.1 4.0 %collective-permute-start.4 = (bf16[4,96,256]{2,1,0:T(8,128)(2,1)S(1)}, bf16[4,96,256]{2,1,0:T(8,128)(2,1)S(1)}, u32[]{:S(2)}, u32[]{:S(2)}) collective-permute-start(bf16[4,96,256]{2,1,0:T(8,128)(2,1)S(1)} %collective-permute-done.3.refs_3_), channel_id=1, source_target_pairs={{0,8},{8,16},{16,24},{24,32},{32,40},{40,48},{48,56},{56,64},{64,7... | collective-permute-start | bytes 589832 | tf_op jit(solution)/shard_map/ppermute | solution.py:50
  50.6 5.2 %features.1 = (bf16[9,288,256]{2,1,0:T(8,128)(2,1)}, bf16[128,2304]{1,0:T(8,128)(2,1)}, bf16[128,2304]{1,0:T(8,128)(2,1)}) custom-call(bf16[288,896]{1,0:T(8,128)(2,1)} %shard_map.68.refs_0_, bf16[256,288]{1,0:T(8,128)(2,1)} %copy.23.refs_1_, bf16[4,96,256]{2,1,0:T(8,128)(2,1)} %copy-done.7, bf16[4,96,256]{2,1,0:T(8,128)(2,1)} %copy-done.5, ...), custom_call_target="tpu_custom_call" | custom-call | tf_op jit(solution)/shard_map/features/pallas_call | solution.py:179
  55.8 11.1 %collective-permute-start.16 = (bf16[128,2304]{1,0:T(8,128)(2,1)}, bf16[128,2304]{1,0:T(8,128)(2,1)S(1)}, u32[]{:S(2)}, u32[]{:S(2)}) collective-permute-start(bf16[128,2304]{1,0:T(8,128)(2,1)} %get-tuple-element.7), channel_id=1, source_target_pairs={{0,1},{1,0},{2,3},{3,2},{4,5},{5,4},{6,7},{7,6},{8,9},{9,8},{10,11... | collective-permute-start | bytes 1769480 | tf_op jit(solution)/shard_map/ppermute | solution.py:40
  72.3 5.6 %collective-permute-start.10 = (bf16[4,2304]{1,0:T(4,128)(2,1)S(1)}, bf16[4,2304]{1,0:T(4,128)(2,1)S(1)}, u32[]{:S(2)}, u32[]{:S(2)}) collective-permute-start(bf16[4,2304]{1,0:T(4,128)(2,1)S(1)} %pad_maximum_fusion.3), channel_id=1, source_target_pairs={{0,32},{8,40},{16,48},{24,56},{32,0},{40,8},{48,16},{56,24},{64,96... | collective-permute-start | bytes 55304 | tf_op jit(solution)/shard_map/ppermute | solution.py:36
  82.3 5.7 %collective-permute-start.18 = (bf16[32,2304]{1,0:T(8,128)(2,1)S(1)}, bf16[32,2304]{1,0:T(8,128)(2,1)S(1)}, u32[]{:S(2)}, u32[]{:S(2)}) collective-permute-start(bf16[32,2304]{1,0:T(8,128)(2,1)S(1)} %get-tuple-element.14), channel_id=1, source_target_pairs={{0,128},{8,136},{16,144},{24,152},{32,160},{40,168},{48,176},{56,1... | collective-permute-start | bytes 442376 | tf_op jit(solution)/shard_map/ppermute | solution.py:32
  90.0 3.4 %collective-permute-start.11 = (bf16[8,2304]{1,0:T(8,128)(2,1)S(1)}, bf16[8,2304]{1,0:T(8,128)(2,1)S(1)}, u32[]{:S(2)}, u32[]{:S(2)}) collective-permute-start(bf16[8,2304]{1,0:T(8,128)(2,1)S(1)} %pad_maximum_fusion.2), channel_id=1, source_target_pairs={{0,64},{8,72},{16,80},{24,88},{32,96},{40,104},{48,112},{56,120},{... | collective-permute-start | bytes 110600 | tf_op jit(solution)/shard_map/ppermute | solution.py:36
  95.2 3.3 %collective-permute-start.12 = (bf16[16,2304]{1,0:T(8,128)(2,1)S(1)}, bf16[16,2304]{1,0:T(8,128)(2,1)S(1)}, u32[]{:S(2)}, u32[]{:S(2)}) collective-permute-start(bf16[16,2304]{1,0:T(8,128)(2,1)S(1)} %concatenate.44), channel_id=1, source_target_pairs={{0,128},{8,136},{16,144},{24,152},{32,160},{40,168},{48,176},{56,1... | collective-permute-start | bytes 221192 | tf_op jit(solution)/shard_map/ppermute | solution.py:36
  98.7 4.7 %collective-permute-start.20 = (bf16[8,2304]{1,0:T(8,128)(2,1)S(1)}, bf16[8,2304]{1,0:T(8,128)(2,1)S(1)}, u32[]{:S(2)}, u32[]{:S(2)}) collective-permute-start(bf16[8,2304]{1,0:T(8,128)(2,1)S(1)} %get-tuple-element.19), channel_id=1, source_target_pairs={{0,256},{8,264},{16,272},{24,280},{32,288},{40,296},{48,304},{56,3... | collective-permute-start | bytes 110600 | tf_op jit(solution)/shard_map/ppermute | solution.py:32
  103.4 4.0 %collective-permute-start.21 = (bf16[8,2304]{1,0:T(8,128)(2,1)S(1)}, bf16[8,2304]{1,0:T(8,128)(2,1)S(1)}, u32[]{:S(2)}, u32[]{:S(2)}) collective-permute-start(bf16[8,2304]{1,0:T(8,128)(2,1)S(1)} %get-tuple-element.21), channel_id=1, source_target_pairs={{0,512},{8,520},{16,528},{24,536},{32,544},{40,552},{48,560},{56,5... | collective-permute-start | bytes 110600 | tf_op jit(solution)/shard_map/ppermute | solution.py:32
  112.9 5.7 %collective-permute-start.23 = (f32[1,2304]{1,0:T(1,128)S(1)}, f32[1,2304]{1,0:T(1,128)S(1)}, u32[]{:S(2)}, u32[]{:S(2)}) collective-permute-start(f32[1,2304]{1,0:T(1,128)S(1)} %get-tuple-element.24), channel_id=1, source_target_pairs={{0,8},{8,16},{16,24},{24,32},{32,40},{40,48},{48,56},{56,0},{64,72... | collective-permute-start | bytes 27656 | tf_op jit(solution)/shard_map/ppermute | solution.py:32
  118.7 4.5 %collective-permute-start.24 = (f32[1,2304]{1,0:T(1,128)S(1)}, f32[1,2304]{1,0:T(1,128)S(1)}, u32[]{:S(2)}, u32[]{:S(2)}) collective-permute-start(f32[1,2304]{1,0:T(1,128)S(1)} %get-tuple-element.30), channel_id=1, source_target_pairs={{0,16},{8,24},{16,32},{24,40},{32,48},{40,56},{48,0},{56,8},{64,80... | collective-permute-start | bytes 27656 | tf_op jit(solution)/shard_map/ppermute | solution.py:32
  125.1 4.7 %collective-permute-start.26 = (f32[1,2304]{1,0:T(1,128)S(1)}, f32[1,2304]{1,0:T(1,128)S(1)}, u32[]{:S(2)}, u32[]{:S(2)}) collective-permute-start(f32[1,2304]{1,0:T(1,128)S(1)} %get-tuple-element.28), channel_id=1, source_target_pairs={{0,32},{8,40},{16,48},{24,56},{32,0},{40,8},{48,16},{56,24},{64,96... | collective-permute-start | bytes 27656 | tf_op jit(solution)/shard_map/ppermute | solution.py:32
  129.8 3.6 %collective-permute-start.27 = (f32[1,2304]{1,0:T(1,128)S(1)}, f32[1,2304]{1,0:T(1,128)S(1)}, u32[]{:S(2)}, u32[]{:S(2)}) collective-permute-start(f32[1,2304]{1,0:T(1,128)S(1)} %get-tuple-element.27), channel_id=1, source_target_pairs={{0,40},{8,48},{16,56},{24,0},{32,8},{40,16},{48,24},{56,32},{64,10... | collective-permute-start | bytes 27656 | tf_op jit(solution)/shard_map/ppermute | solution.py:32
  133.4 5.2 %collective-permute-start.28 = (f32[1,2304]{1,0:T(1,128)S(1)}, f32[1,2304]{1,0:T(1,128)S(1)}, u32[]{:S(2)}, u32[]{:S(2)}) collective-permute-start(f32[1,2304]{1,0:T(1,128)S(1)} %get-tuple-element.26), channel_id=1, source_target_pairs={{0,48},{8,56},{16,0},{24,8},{32,16},{40,24},{48,32},{56,40},{64,11... | collective-permute-start | bytes 27656 | tf_op jit(solution)/shard_map/ppermute | solution.py:32
  144.5 11.5 %collective-permute-start.30 = (f32[1,2304]{1,0:T(1,128)S(1)}, f32[1,2304]{1,0:T(1,128)S(1)}, u32[]{:S(2)}, u32[]{:S(2)}) collective-permute-start(f32[1,2304]{1,0:T(1,128)S(1)} %add_add_fusion), channel_id=1, source_target_pairs={{0,4},{1,5},{2,6},{3,7},{4,0},{5,1},{6,2},{7,3},{8,12},{9,13},{10,... | collective-permute-start | bytes 27656 | tf_op jit(solution)/shard_map/ppermute | solution.py:45
  156.0 3.3 %collective-permute-start.31 = (f32[1,2304]{1,0:T(1,128)S(1)}, f32[1,2304]{1,0:T(1,128)S(1)}, u32[]{:S(2)}, u32[]{:S(2)}) collective-permute-start(f32[1,2304]{1,0:T(1,128)S(1)} %add_add_fusion), channel_id=1, source_target_pairs={{0,2},{1,3},{2,4},{3,5},{4,6},{5,7},{6,0},{7,1},{8,10},{9,11},{10,... | collective-permute-start | bytes 27656 | tf_op jit(solution)/shard_map/ppermute | solution.py:45
  159.3 5.9 %collective-permute-start.32 = (f32[1,2304]{1,0:T(1,128)S(1)}, f32[1,2304]{1,0:T(1,128)S(1)}, u32[]{:S(2)}, u32[]{:S(2)}) collective-permute-start(f32[1,2304]{1,0:T(1,128)S(1)} %add_add_fusion), channel_id=1, source_target_pairs={{0,6},{1,7},{2,0},{3,1},{4,2},{5,3},{6,4},{7,5},{8,14},{9,15},{10,... | collective-permute-start | bytes 27656 | tf_op jit(solution)/shard_map/ppermute | solution.py:45
  165.5 8.8 %collective-permute-start.15 = (bf16[128,2304]{1,0:T(8,128)(2,1)S(1)}, bf16[128,2304]{1,0:T(8,128)(2,1)S(1)}, u32[]{:S(2)}, u32[]{:S(2)}) collective-permute-start(bf16[128,2304]{1,0:T(8,128)(2,1)S(1)} %concatenate.47), channel_id=1, source_target_pairs={{0,1},{1,0},{2,3},{3,2},{4,5},{5,4},{6,7},{7,6},{8,9},{9,8},{10,11... | collective-permute-start | bytes 1769480 | tf_op jit(solution)/shard_map/ppermute | solution.py:40
  174.3 3.2 %collective-permute-start.33 = (f32[1,2304]{1,0:T(1,128)S(1)}, f32[1,2304]{1,0:T(1,128)S(1)}, u32[]{:S(2)}, u32[]{:S(2)}) collective-permute-start(f32[1,2304]{1,0:T(1,128)S(1)} %add_multiply_fusion), channel_id=1, source_target_pairs={{0,1},{1,0},{2,3},{3,2},{4,5},{5,4},{6,7},{7,6},{8,9},{9,8},{10,11... | collective-permute-start | bytes 27656 | tf_op jit(solution)/shard_map/ppermute | solution.py:40
  178.3 6.0 %concatenate.48.refs_1_ = bf16[256,2304]{1,0:T(8,128)(2,1)} concatenate(bf16[1,2304]{1,0:T(2,128)(2,1)S(1)} %constant_dynamic-slice_fusion, bf16[1,2304]{1,0:T(2,128)(2,1)S(1)} %collective-permute-done.8, bf16[2,2304]{1,0:T(2,128)(2,1)S(1)} %collective-permute-done.9, bf16[4,2304]{1,0:T(4,128)(2,1)S(1)} %collective-permute-done.10, bf16[8,2304]{1,0:T(8,128)(2,1)S(1)} %collective-permute-done.11, ...), dimensions={0} | concatenate | bytes 2359296 | tf_op jit(solution)/shard_map/concatenate | solution.py:140
  (102 shorter events, 52.0 us)
Async XLA Ops:
  1.5 22.0 %collective-permute-start = (bf16[4,12,256]{2,1,0:T(8,128)(2,1)S(1)}, bf16[4,12,256]{2,1,0:T(8,128)(2,1)S(1)}, u32[]{:S(2)}, u32[]{:S(2)}) collective-permute-start(bf16[4,12,256]{2,1,0:T(8,128)(2,1)S(1)} %get-tuple-element.22), channel_id=1, source_target_pairs={{0,1},{1,2},{2,3},{3,4},{4,5},{5,6},{6,7},{7,0},{8,9},{9,10},{10,1... | collective-permute-start | bytes 73736 | tf_op jit(solution)/shard_map/ppermute | solution.py:45
  13.5 9.9 %collective-permute-start.1 = (bf16[4,12,256]{2,1,0:T(8,128)(2,1)S(1)}, bf16[4,12,256]{2,1,0:T(8,128)(2,1)S(1)}, u32[]{:S(2)}, u32[]{:S(2)}) collective-permute-start(bf16[4,12,256]{2,1,0:T(8,128)(2,1)S(1)} %get-tuple-element.23), channel_id=1, source_target_pairs={{0,7},{1,0},{2,1},{3,2},{4,3},{5,4},{6,5},{7,6},{8,15},{9,8},{10,9... | collective-permute-start | bytes 73736 | tf_op jit(solution)/shard_map/ppermute | solution.py:45
  19.5 47.4 %collective-permute-start.8 = (bf16[1,2304]{1,0:T(2,128)(2,1)S(1)}, bf16[1,2304]{1,0:T(2,128)(2,1)S(1)}, u32[]{:S(2)}, u32[]{:S(2)}) collective-permute-start(bf16[1,2304]{1,0:T(2,128)(2,1)S(1)} %constant_dynamic-slice_fusion), channel_id=1, source_target_pairs={{0,8},{8,0},{16,24},{24,16},{32,40},{40,32},{48,56},{56,48},{64,72... | collective-permute-start | bytes 13832 | tf_op jit(solution)/shard_map/ppermute | solution.py:36
  55.8 22.1 %collective-permute-start.16 = (bf16[128,2304]{1,0:T(8,128)(2,1)}, bf16[128,2304]{1,0:T(8,128)(2,1)S(1)}, u32[]{:S(2)}, u32[]{:S(2)}) collective-permute-start(bf16[128,2304]{1,0:T(8,128)(2,1)} %get-tuple-element.7), channel_id=1, source_target_pairs={{0,1},{1,0},{2,3},{3,2},{4,5},{5,4},{6,7},{7,6},{8,9},{9,8},{10,11... | collective-permute-start | bytes 1769480 | tf_op jit(solution)/shard_map/ppermute | solution.py:40
  72.3 17.6 %collective-permute-start.10 = (bf16[4,2304]{1,0:T(4,128)(2,1)S(1)}, bf16[4,2304]{1,0:T(4,128)(2,1)S(1)}, u32[]{:S(2)}, u32[]{:S(2)}) collective-permute-start(bf16[4,2304]{1,0:T(4,128)(2,1)S(1)} %pad_maximum_fusion.3), channel_id=1, source_target_pairs={{0,32},{8,40},{16,48},{24,56},{32,0},{40,8},{48,16},{56,24},{64,96... | collective-permute-start | bytes 55304 | tf_op jit(solution)/shard_map/ppermute | solution.py:36
  79.2 19.4 %collective-permute-start.17 = (bf16[32,2304]{1,0:T(8,128)(2,1)S(1)}, bf16[32,2304]{1,0:T(8,128)(2,1)S(1)}, u32[]{:S(2)}, u32[]{:S(2)}) collective-permute-start(bf16[32,2304]{1,0:T(8,128)(2,1)S(1)} %get-tuple-element.12), channel_id=1, source_target_pairs={{0,64},{8,72},{16,80},{24,88},{32,96},{40,104},{48,112},{56,120},{... | collective-permute-start | bytes 442376 | tf_op jit(solution)/shard_map/ppermute | solution.py:32
  82.3 16.3 %collective-permute-start.18 = (bf16[32,2304]{1,0:T(8,128)(2,1)S(1)}, bf16[32,2304]{1,0:T(8,128)(2,1)S(1)}, u32[]{:S(2)}, u32[]{:S(2)}) collective-permute-start(bf16[32,2304]{1,0:T(8,128)(2,1)S(1)} %get-tuple-element.14), channel_id=1, source_target_pairs={{0,128},{8,136},{16,144},{24,152},{32,160},{40,168},{48,176},{56,1... | collective-permute-start | bytes 442376 | tf_op jit(solution)/shard_map/ppermute | solution.py:32
  88.0 10.6 %collective-permute-start.19 = (bf16[32,2304]{1,0:T(8,128)(2,1)S(1)}, bf16[32,2304]{1,0:T(8,128)(2,1)S(1)}, u32[]{:S(2)}, u32[]{:S(2)}) collective-permute-start(bf16[32,2304]{1,0:T(8,128)(2,1)S(1)} %get-tuple-element.13), channel_id=1, source_target_pairs={{0,192},{8,200},{16,208},{24,216},{32,224},{40,232},{48,240},{56,2... | collective-permute-start | bytes 442376 | tf_op jit(solution)/shard_map/ppermute | solution.py:32
  95.2 15.3 %collective-permute-start.12 = (bf16[16,2304]{1,0:T(8,128)(2,1)S(1)}, bf16[16,2304]{1,0:T(8,128)(2,1)S(1)}, u32[]{:S(2)}, u32[]{:S(2)}) collective-permute-start(bf16[16,2304]{1,0:T(8,128)(2,1)S(1)} %concatenate.44), channel_id=1, source_target_pairs={{0,128},{8,136},{16,144},{24,152},{32,160},{40,168},{48,176},{56,1... | collective-permute-start | bytes 221192 | tf_op jit(solution)/shard_map/ppermute | solution.py:36
  98.7 14.1 %collective-permute-start.20 = (bf16[8,2304]{1,0:T(8,128)(2,1)S(1)}, bf16[8,2304]{1,0:T(8,128)(2,1)S(1)}, u32[]{:S(2)}, u32[]{:S(2)}) collective-permute-start(bf16[8,2304]{1,0:T(8,128)(2,1)S(1)} %get-tuple-element.19), channel_id=1, source_target_pairs={{0,256},{8,264},{16,272},{24,280},{32,288},{40,296},{48,304},{56,3... | collective-permute-start | bytes 110600 | tf_op jit(solution)/shard_map/ppermute | solution.py:32
  103.4 9.4 %collective-permute-start.21 = (bf16[8,2304]{1,0:T(8,128)(2,1)S(1)}, bf16[8,2304]{1,0:T(8,128)(2,1)S(1)}, u32[]{:S(2)}, u32[]{:S(2)}) collective-permute-start(bf16[8,2304]{1,0:T(8,128)(2,1)S(1)} %get-tuple-element.21), channel_id=1, source_target_pairs={{0,512},{8,520},{16,528},{24,536},{32,544},{40,552},{48,560},{56,5... | collective-permute-start | bytes 110600 | tf_op jit(solution)/shard_map/ppermute | solution.py:32
  110.6 19.2 %collective-permute-start.13 = (bf16[32,2304]{1,0:T(8,128)(2,1)S(1)}, bf16[32,2304]{1,0:T(8,128)(2,1)S(1)}, u32[]{:S(2)}, u32[]{:S(2)}) collective-permute-start(bf16[32,2304]{1,0:T(8,128)(2,1)S(1)} %concatenate.45), channel_id=1, source_target_pairs={{0,256},{8,264},{16,272},{24,280},{32,288},{40,296},{48,304},{56,3... | collective-permute-start | bytes 442376 | tf_op jit(solution)/shard_map/ppermute | solution.py:36
  112.9 20.5 %collective-permute-start.23 = (f32[1,2304]{1,0:T(1,128)S(1)}, f32[1,2304]{1,0:T(1,128)S(1)}, u32[]{:S(2)}, u32[]{:S(2)}) collective-permute-start(f32[1,2304]{1,0:T(1,128)S(1)} %get-tuple-element.24), channel_id=1, source_target_pairs={{0,8},{8,16},{16,24},{24,32},{32,40},{40,48},{48,56},{56,0},{64,72... | collective-permute-start | bytes 27656 | tf_op jit(solution)/shard_map/ppermute | solution.py:32
  118.7 20.0 %collective-permute-start.24 = (f32[1,2304]{1,0:T(1,128)S(1)}, f32[1,2304]{1,0:T(1,128)S(1)}, u32[]{:S(2)}, u32[]{:S(2)}) collective-permute-start(f32[1,2304]{1,0:T(1,128)S(1)} %get-tuple-element.30), channel_id=1, source_target_pairs={{0,16},{8,24},{16,32},{24,40},{32,48},{40,56},{48,0},{56,8},{64,80... | collective-permute-start | bytes 27656 | tf_op jit(solution)/shard_map/ppermute | solution.py:32
  123.2 18.7 %collective-permute-start.25 = (f32[1,2304]{1,0:T(1,128)S(1)}, f32[1,2304]{1,0:T(1,128)S(1)}, u32[]{:S(2)}, u32[]{:S(2)}) collective-permute-start(f32[1,2304]{1,0:T(1,128)S(1)} %get-tuple-element.29), channel_id=1, source_target_pairs={{0,24},{8,32},{16,40},{24,48},{32,56},{40,0},{48,8},{56,16},{64,88... | collective-permute-start | bytes 27656 | tf_op jit(solution)/shard_map/ppermute | solution.py:32
  125.1 19.3 %collective-permute-start.26 = (f32[1,2304]{1,0:T(1,128)S(1)}, f32[1,2304]{1,0:T(1,128)S(1)}, u32[]{:S(2)}, u32[]{:S(2)}) collective-permute-start(f32[1,2304]{1,0:T(1,128)S(1)} %get-tuple-element.28), channel_id=1, source_target_pairs={{0,32},{8,40},{16,48},{24,56},{32,0},{40,8},{48,16},{56,24},{64,96... | collective-permute-start | bytes 27656 | tf_op jit(solution)/shard_map/ppermute | solution.py:32
  129.8 14.6 %collective-permute-start.27 = (f32[1,2304]{1,0:T(1,128)S(1)}, f32[1,2304]{1,0:T(1,128)S(1)}, u32[]{:S(2)}, u32[]{:S(2)}) collective-permute-start(f32[1,2304]{1,0:T(1,128)S(1)} %get-tuple-element.27), channel_id=1, source_target_pairs={{0,40},{8,48},{16,56},{24,0},{32,8},{40,16},{48,24},{56,32},{64,10... | collective-permute-start | bytes 27656 | tf_op jit(solution)/shard_map/ppermute | solution.py:32
  133.4 11.0 %collective-permute-start.28 = (f32[1,2304]{1,0:T(1,128)S(1)}, f32[1,2304]{1,0:T(1,128)S(1)}, u32[]{:S(2)}, u32[]{:S(2)}) collective-permute-start(f32[1,2304]{1,0:T(1,128)S(1)} %get-tuple-element.26), channel_id=1, source_target_pairs={{0,48},{8,56},{16,0},{24,8},{32,16},{40,24},{48,32},{56,40},{64,11... | collective-permute-start | bytes 27656 | tf_op jit(solution)/shard_map/ppermute | solution.py:32
  141.9 23.3 %collective-permute-start.14 = (bf16[64,2304]{1,0:T(8,128)(2,1)S(1)}, bf16[64,2304]{1,0:T(8,128)(2,1)S(1)}, u32[]{:S(2)}, u32[]{:S(2)}) collective-permute-start(bf16[64,2304]{1,0:T(8,128)(2,1)S(1)} %concatenate.46), channel_id=1, source_target_pairs={{0,512},{8,520},{16,528},{24,536},{32,544},{40,552},{48,560},{56,5... | collective-permute-start | bytes 884744 | tf_op jit(solution)/shard_map/ppermute | solution.py:36
  144.5 29.8 %collective-permute-start.30 = (f32[1,2304]{1,0:T(1,128)S(1)}, f32[1,2304]{1,0:T(1,128)S(1)}, u32[]{:S(2)}, u32[]{:S(2)}) collective-permute-start(f32[1,2304]{1,0:T(1,128)S(1)} %add_add_fusion), channel_id=1, source_target_pairs={{0,4},{1,5},{2,6},{3,7},{4,0},{5,1},{6,2},{7,3},{8,12},{9,13},{10,... | collective-permute-start | bytes 27656 | tf_op jit(solution)/shard_map/ppermute | solution.py:45
  156.0 18.3 %collective-permute-start.31 = (f32[1,2304]{1,0:T(1,128)S(1)}, f32[1,2304]{1,0:T(1,128)S(1)}, u32[]{:S(2)}, u32[]{:S(2)}) collective-permute-start(f32[1,2304]{1,0:T(1,128)S(1)} %add_add_fusion), channel_id=1, source_target_pairs={{0,2},{1,3},{2,4},{3,5},{4,6},{5,7},{6,0},{7,1},{8,10},{9,11},{10,... | collective-permute-start | bytes 27656 | tf_op jit(solution)/shard_map/ppermute | solution.py:45
  159.3 15.0 %collective-permute-start.32 = (f32[1,2304]{1,0:T(1,128)S(1)}, f32[1,2304]{1,0:T(1,128)S(1)}, u32[]{:S(2)}, u32[]{:S(2)}) collective-permute-start(f32[1,2304]{1,0:T(1,128)S(1)} %add_add_fusion), channel_id=1, source_target_pairs={{0,6},{1,7},{2,0},{3,1},{4,2},{5,3},{6,4},{7,5},{8,14},{9,15},{10,... | collective-permute-start | bytes 27656 | tf_op jit(solution)/shard_map/ppermute | solution.py:45
  165.5 12.8 %collective-permute-start.15 = (bf16[128,2304]{1,0:T(8,128)(2,1)S(1)}, bf16[128,2304]{1,0:T(8,128)(2,1)S(1)}, u32[]{:S(2)}, u32[]{:S(2)}) collective-permute-start(bf16[128,2304]{1,0:T(8,128)(2,1)S(1)} %concatenate.47), channel_id=1, source_target_pairs={{0,1},{1,0},{2,3},{3,2},{4,5},{5,4},{6,7},{7,6},{8,9},{9,8},{10,11... | collective-permute-start | bytes 1769480 | tf_op jit(solution)/shard_map/ppermute | solution.py:40
  174.3 13.0 %collective-permute-start.33 = (f32[1,2304]{1,0:T(1,128)S(1)}, f32[1,2304]{1,0:T(1,128)S(1)}, u32[]{:S(2)}, u32[]{:S(2)}) collective-permute-start(f32[1,2304]{1,0:T(1,128)S(1)} %add_multiply_fusion), channel_id=1, source_target_pairs={{0,1},{1,0},{2,3},{3,2},{4,5},{5,4},{6,7},{7,6},{8,9},{9,8},{10,11... | collective-permute-start | bytes 27656 | tf_op jit(solution)/shard_map/ppermute | solution.py:40
  (20 other events, 169.0 us)

commit v2 on v1

--- a/solution.py
+++ b/solution.py
@@ -9,6 +9,7 @@
 
 FACTORS = {128: (4, 4, 8), 8: (2, 2, 2)}
 TILE = 8
+MASKS = {128: (8, 16, 32, 64, 1, 2, 7), 8: (2, 4, 1)}
 
 
 def dot(a, b, contract):
@@ -23,13 +24,13 @@
     return index // (factors[1] * factors[2]), index // factors[2] % factors[1], index % factors[2]
 
 
-def along(block, dim, step, factors):
-    pairs = []
-    for source in range(factors[0] * factors[1] * factors[2]):
-        coords = list(lat_coords(source, factors))
-        coords[dim] = (coords[dim] + step) % factors[dim]
-        pairs.append((source, lat_index(*coords, factors)))
-    return lax.ppermute(block, "lat", pairs)
+def groups(dims, factors):
+    members = {}
+    for index in range(factors[0] * factors[1] * factors[2]):
+        coords = lat_coords(index, factors)
+        fixed = tuple(coords[d] for d in range(3) if d not in dims)
+        members.setdefault(fixed, []).append(index)
+    return [members[fixed] for fixed in sorted(members)]
 
 
 def swapped_lat(block, bit):
@@ -40,14 +41,17 @@
     return lax.ppermute(block, "lon", [(i, i ^ 1) for i in range(lax.axis_size("lon"))])
 
 
-def along_lon(block, step):
-    count = lax.axis_size("lon")
-    return lax.ppermute(block, "lon", [(i, (i + step) % count) for i in range(count)])
-
-
-def passed_along(block, by):
-    count = lax.axis_size("lat")
-    return lax.ppermute(block, "lat", [(i, i + by) for i in range(count) if 0 <= i + by < count])
+def paired(block, axis, first, loop):
+    count = lax.axis_size(axis)
+    pairs = []
+    for low in range(first, count, 2):
+        high = low + 1
+        if high == count:
+            if not loop:
+                continue
+            high = 0
+        pairs += [(low, high), (high, low)]
+    return lax.ppermute(block, axis, pairs)
 
 
 def band_kernel(rows_ref, band_ref):
@@ -89,12 +93,13 @@
         send_ref[:, span] = term[half:].astype(send_ref.dtype)
 
 
-def output_kernel(tile_count, features_ref, weight_ref, order_ref, output_ref):
+def output_kernel(tile_count, features_ref, mine_ref, other_ref, order_ref, output_ref):
     nbasis, cells, channels = features_ref.shape
     rows = output_ref.shape[0]
-    total = jnp.zeros((cells, weight_ref.shape[0]), jnp.float32)
+    total = jnp.zeros((cells, order_ref.shape[0]), jnp.float32)
     for k in range(nbasis):
-        piece = weight_ref[:, k * channels : (k + 1) * channels]
+        span = slice(k * channels, (k + 1) * channels)
+        piece = jnp.concatenate([mine_ref[:, span], other_ref[:, span]], axis=0)
         total = total + dot(features_ref[k], piece, ((1,), (1,)))
     mixed = dot(total.astype(jnp.bfloat16), order_ref[...], ((1,), (0,))).astype(jnp.bfloat16)
     for tile in range(tile_count):
@@ -116,31 +121,49 @@
     lat = lax.axis_index("lat")
     lon = lax.axis_index("lon")
     core = lon % 2
-    z_at, x_at, y_at = lat_coords(lat, factors)
     tile_count = cols // TILE
     window_rows = extent + rows - 1
     window_cols = TILE + width - 1
     cells = rows * cols
     bf16 = jnp.bfloat16
 
-    left = along_lon(fields[:, cols - reach :], 1)
-    right = along_lon(fields[:, :reach], -1)
+    masks = MASKS[lax.axis_size("lat")]
+    owners = [0]
+    for mask in masks:
+        owners = owners + [owner ^ mask for owner in owners]
+
+    def doubled(block, turn):
+        if turn >= len(masks):
+            return block
+        return jnp.concatenate([block, swapped_lat(block, masks[turn])], axis=0)
+
+    gathered = doubled(lax.dynamic_slice_in_dim(weight, core, 1, 0), 0)
+
+    edges = jnp.where(core == 0, fields[:, cols - reach :], fields[:, :reach])
+    other_edges = jnp.where(core == 0, fields[:, :reach], fields[:, cols - reach :])
+    near_edge = paired(edges, "lon", 0, True)
+    far_edge = paired(other_edges, "lon", 1, True)
+    left = jnp.where(core == 0, far_edge, near_edge)
+    right = jnp.where(core == 0, near_edge, far_edge)
     own = jnp.concatenate([left, fields, right], axis=1)
-    below, above = [own], [own]
-    for _ in range(3):
-        below.append(passed_along(below[-1], 1))
-        above.append(passed_along(above[-1], -1))
-    windows = below[:0:-1] + [own] + above[1:]
-
-    gathered = lax.dynamic_slice_in_dim(weight, core, 1, 0)
-    bit = 1
-    while bit < lax.axis_size("lat"):
-        gathered = jnp.concatenate([gathered, swapped_lat(gathered, bit)], axis=0)
-        bit *= 2
-    all_weight = jnp.concatenate([gathered, swapped_core(gathered)], axis=0)
+    near, far = own, own
+    nears, fars = [], []
+    for turn in range(3):
+        near, far, gathered = lax.optimization_barrier((near, far, gathered))
+        near, far = paired(far, "lat", 0, False), paired(near, "lat", 1, False)
+        gathered = doubled(gathered, turn + 1)
+        nears.append(near)
+        fars.append(far)
+    windows = nears[::-1] + [own] + fars
+
+    near, gathered = lax.optimization_barrier((near, gathered))
+    nears[-1] = near
+    for turn in range(4, len(masks)):
+        gathered = doubled(gathered, turn)
+    other_weight = swapped_core(gathered)
     position = jnp.arange(outs)
     half = outs // 2
-    weight_row = 2 * (lat ^ (position % half)) + (core ^ (position // half))
+    weight_row = 2 * (lat ^ jnp.array(owners + owners, jnp.int32)) + (core ^ (position // half))
     weight_order = (weight_row[:, None] == jnp.arange(outs)[None, :]).astype(bf16)
 
     offsets = jnp.arange(width) - reach
@@ -153,7 +176,9 @@
             for row in range(rows)
         ],
         axis=1,
-    ).reshape(nbasis * rows, window_rows * window_cols)
+    ).reshape(nbasis * rows, window_rows // rows, rows * window_cols)
+    band_rows = jnp.where(lat % 2 == 0, band_rows[:, ::-1], band_rows)
+    band_rows = band_rows.reshape(nbasis * rows, window_rows * window_cols)
     band = pl.pallas_call(
         band_kernel,
         out_shape=jax.ShapeDtypeStruct((nbasis * rows * TILE, window_rows * window_cols), bf16),
@@ -165,10 +190,7 @@
     away = (
         2
         * lat_index(
-            (z_at + position // ys % zs) % zs,
-            (x_at + position // (ys * zs) % xs) % xs,
-            (y_at + position % ys) % ys,
-            factors,
+            position // ys % zs, position // (ys * zs) % xs, position % ys, factors
         )
         + (core ^ (position // half))
     )
@@ -191,36 +213,24 @@
     output = pl.pallas_call(
         lambda *refs: output_kernel(tile_count, *refs),
         out_shape=jax.ShapeDtypeStruct((rows, cols, outs), bf16),
-        in_specs=vmem(3),
+        in_specs=vmem(4),
         out_specs=pl.BlockSpec(memory_space=pltpu.VMEM),
         name="mixing",
-    )(features, all_weight, weight_order)
+    )(features, gathered, other_weight, weight_order)
 
     f32 = jnp.float32
     total = keep.astype(f32) + swapped_core(send).astype(f32)
     for dim in (1, 0, 2):
         count = factors[dim]
-        piece = total.shape[0] // count
         moved = total if dim == 2 else total.astype(bf16)
-        arrived = [
-            along(moved[step * piece : (step + 1) * piece], dim, step, factors)
-            for step in range(1, count)
-        ]
-        total = total[:piece]
-        for part in arrived:
-            total = total + part.astype(f32)
-    hi = lax.axis_size("lon") // 2
-    if hi == 4:
-        one, two, three = (along_lon(total, 2 * step) for step in (1, 2, 3))
-        total = (total + two) + (one + three)
+        moved = moved.reshape(count, -1, moved.shape[1])
+        arrived = lax.all_to_all(moved, "lat", 0, 0, axis_index_groups=groups((dim,), factors))
+        total = jnp.sum(arrived.astype(f32), axis=0)
     scale = 1.0 / math.sqrt(rows * lax.axis_size("lat") * cols * lax.axis_size("lon"))
-    total = total * scale
-    other = swapped_core(total)
-    grad_weight = jnp.where(
-        core == 0,
-        jnp.concatenate([total, other], axis=0),
-        jnp.concatenate([other, total], axis=0),
-    )
+    lon_size = lax.axis_size("lon")
+    spread = jnp.broadcast_to(total * scale, (lon_size,) + total.shape)
+    arrived = lax.all_to_all(spread, "lon", 0, 0)
+    grad_weight = jnp.sum(arrived.reshape(lon_size // 2, 2, nbasis * channels), axis=0)
     return (output, grad_weight)
 
 

time: 189 us -> 158 us (0.84)
  starting transfers between devices: 150 us -> 95.5 us
  waiting for transfers between devices: 11.6 us -> 36.7 us
  local copies, waits for them, and re-layouts: 10.1 us -> 6.09 us
  other arithmetic: 4.83 us -> 7.27 us
    ppermute x24 -> x8, starting transfers between devices: 105 us -> 34.7 us  [paired(): return lax.ppermute(block, axis, pairs)]
    all_to_all x0 -> x4, waiting for transfers between devices: none -> 19.5 us  [the longest x3 10.3 us: shards(): lax.all_to_all(moved, 'lat', 0, 0, axis_index_groups=groups((dim,), facto...]
    all_to_all x0 -> x4, starting transfers between devices: none -> 17.1 us  [the longest x3 10.2 us: shards(): lax.all_to_all(moved, 'lat', 0, 0, axis_index_groups=groups((dim,), facto...]
    ppermute x3 -> x2, starting transfers between devices: 23.1 us -> 9.53 us  [swapped_core(): lax.ppermute(block, 'lon', [(i, i ^ 1) for i in range(lax.axis_size('lon'...]
    ppermute x7, starting transfers between devices: 21.5 us -> 34.2 us  [swapped_lat(): lax.ppermute(block, 'lat', [(i, i ^ bit) for i in range(lax.axis_size('la...]
    concatenate x5 -> x1, local copies, waits for them, and re-layouts: 6.54 us -> 0.02 us  [doubled(): return jnp.concatenate([block, swapped_lat(block, masks[turn])], axis=0)]
    ppermute x7, waiting for transfers between devices: 4.52 us -> 9.56 us  [swapped_lat(): lax.ppermute(block, 'lat', [(i, i ^ bit) for i in range(lax.axis_size('la...]
    unnamed x20 -> x31, local copies, waits for them, and re-layouts: 0.72 us -> 3.43 us
  transfers between devices with their start and end apart: 34 -> 21, of which waited for: 5 -> 6; matrix products, arithmetic and copies ran while one was open for 7% -> 6% of each run, Pallas kernels for 5% -> 6%
where the time goes in v2:
time: 158 us; the launch traced here: 157 us
  starting transfers between devices  95.5 us (60%)
  waiting for transfers between devices  36.7 us (23%)
  Pallas kernels  10.1 us (6%)
  other arithmetic  7.27 us (5%)
  local copies, waits for them, and re-layouts  6.09 us (4%)
    ppermute x8, starting transfers between devices, paired(): return lax.ppermute(block, axis, pairs)  34.7 us
    ppermute x7, starting transfers between devices, swapped_lat(): lax.ppermute(block, 'lat', [(i, i ^ bit) for i in range(lax.axis_size('la...  34.2 us
    all_to_all x3, waiting for transfers between devices, shards(): lax.all_to_all(moved, 'lat', 0, 0, axis_index_groups=groups((dim,), facto...  10.3 us
    all_to_all x3, starting transfers between devices, shards(): lax.all_to_all(moved, 'lat', 0, 0, axis_index_groups=groups((dim,), facto...  10.2 us
    ppermute x7, waiting for transfers between devices, swapped_lat(): lax.ppermute(block, 'lat', [(i, i ^ bit) for i in range(lax.axis_size('la...  9.56 us
    ppermute x2, starting transfers between devices, swapped_core(): lax.ppermute(block, 'lon', [(i, i ^ 1) for i in range(lax.axis_size('lon'...  9.53 us
    all_to_all x1, waiting for transfers between devices, shards(): arrived = lax.all_to_all(spread, 'lon', 0, 0)  9.2 us
    ppermute x8, waiting for transfers between devices, paired(): return lax.ppermute(block, axis, pairs)  7.62 us
  transfers between devices with their start and end apart: 21, of which 6 were waited for; matrix products, arithmetic and copies ran while one was open for 6% of the time, Pallas kernels for 6%

profile of v2, /device:TPU:1, one launch (start us, length us, event | category | flops | bytes accessed | tf_op | source)
XLA Modules:
  0.0 157.1 jit_solution(10070765508000186513)
XLA Ops:
  1.5 12.0 %collective-permute-start = (bf16[4,12,256]{2,1,0:T(8,128)(2,1)S(1)}, bf16[4,12,256]{2,1,0:T(8,128)(2,1)S(1)}, u32[]{:S(2)}, u32[]{:S(2)}) collective-permute-start(bf16[4,12,256]{2,1,0:T(8,128)(2,1)S(1)} %get-tuple-element.32), channel_id=1, source_target_pairs={{1,2},{2,1},{3,4},{4,3},{5,6},{6,5},{7,0},{0,7},{9,10},{10,9},{11,... | collective-permute-start | bytes 73736 | tf_op jit(solution)/shard_map/ppermute | solution.py:54
  13.5 9.0 %collective-permute-start.1 = (bf16[4,12,256]{2,1,0:T(8,128)(2,1)S(1)}, bf16[4,12,256]{2,1,0:T(8,128)(2,1)S(1)}, u32[]{:S(2)}, u32[]{:S(2)}) collective-permute-start(bf16[4,12,256]{2,1,0:T(8,128)(2,1)S(1)} %get-tuple-element.33), channel_id=1, source_target_pairs={{0,1},{1,0},{2,3},{3,2},{4,5},{5,4},{6,7},{7,6},{8,9},{9,8},{10,11... | collective-permute-start | bytes 73736 | tf_op jit(solution)/shard_map/ppermute | solution.py:54
  22.6 3.1 %collective-permute-start.2 = (bf16[1,2304]{1,0:T(2,128)(2,1)S(1)}, bf16[1,2304]{1,0:T(2,128)(2,1)S(1)}, u32[]{:S(2)}, u32[]{:S(2)}) collective-permute-start(bf16[1,2304]{1,0:T(2,128)(2,1)S(1)} %constant_dynamic-slice_fusion), channel_id=1, source_target_pairs={{0,64},{8,72},{16,80},{24,88},{32,96},{40,104},{48,112},{56,120},{... | collective-permute-start | bytes 13832 | tf_op jit(solution)/shard_map/ppermute | solution.py:37
  28.7 4.4 %collective-permute-start.5 = (bf16[2,2304]{1,0:T(2,128)(2,1)S(1)}, bf16[2,2304]{1,0:T(2,128)(2,1)S(1)}, u32[]{:S(2)}, u32[]{:S(2)}) collective-permute-start(bf16[2,2304]{1,0:T(2,128)(2,1)S(1)} %pad_maximum_fusion.7), channel_id=1, source_target_pairs={{0,128},{8,136},{16,144},{24,152},{32,160},{40,168},{48,176},{56,1... | collective-permute-start | bytes 27656 | tf_op jit(solution)/shard_map/ppermute | solution.py:37
  33.1 3.2 %collective-permute-start.3 = (bf16[4,96,256]{2,1,0:T(8,128)(2,1)S(1)}, bf16[4,96,256]{2,1,0:T(8,128)(2,1)S(1)}, u32[]{:S(2)}, u32[]{:S(2)}) collective-permute-start(bf16[4,96,256]{2,1,0:T(8,128)(2,1)S(1)} %pad_maximum_fusion.2.refs_5_), channel_id=1, source_target_pairs={{0,8},{8,0},{16,24},{24,16},{32,40},{40,32},{48,56},{56,48},{64,72... | collective-permute-start | bytes 589832 | tf_op jit(solution)/shard_map/ppermute | solution.py:54
  37.0 3.8 %collective-permute-done.3.refs_4_ = bf16[4,96,256]{2,1,0:T(8,128)(2,1)S(1)} collective-permute-done((bf16[4,96,256]{2,1,0:T(8,128)(2,1)S(1)}, bf16[4,96,256]{2,1,0:T(8,128)(2,1)S(1)}, u32[]{:S(2)}, u32[]{:S(2)}) %collective-permute-start.3) | collective-permute-done | bytes 196640 | tf_op jit(solution)/shard_map/ppermute | solution.py:54
  40.8 10.2 %collective-permute-start.8 = (bf16[4,2304]{1,0:T(4,128)(2,1)S(1)}, bf16[4,2304]{1,0:T(4,128)(2,1)S(1)}, u32[]{:S(2)}, u32[]{:S(2)}) collective-permute-start(bf16[4,2304]{1,0:T(4,128)(2,1)S(1)} %pad_maximum_fusion.6), channel_id=1, source_target_pairs={{0,256},{8,264},{16,272},{24,280},{32,288},{40,296},{48,304},{56,3... | collective-permute-start | bytes 55304 | tf_op jit(solution)/shard_map/ppermute | solution.py:37
  53.7 3.8 %collective-permute-done.6.refs_3_ = bf16[4,96,256]{2,1,0:T(8,128)(2,1)S(1)} collective-permute-done((bf16[4,96,256]{2,1,0:T(8,128)(2,1)S(1)}, bf16[4,96,256]{2,1,0:T(8,128)(2,1)S(1)}, u32[]{:S(2)}, u32[]{:S(2)}) %collective-permute-start.6) | collective-permute-done | bytes 196640 | tf_op jit(solution)/shard_map/ppermute | solution.py:54
  58.2 6.5 %collective-permute-start.9 = (bf16[4,96,256]{2,1,0:T(8,128)(2,1)S(1)}, bf16[4,96,256]{2,1,0:T(8,128)(2,1)S(1)}, u32[]{:S(2)}, u32[]{:S(2)}) collective-permute-start(bf16[4,96,256]{2,1,0:T(8,128)(2,1)S(1)} %collective-permute-done.7.refs_7_), channel_id=1, source_target_pairs={{0,8},{8,0},{16,24},{24,16},{32,40},{40,32},{48,56},{56,48},{64,72... | collective-permute-start | bytes 589832 | tf_op jit(solution)/shard_map/ppermute | solution.py:54
  64.7 8.4 %collective-permute-start.11 = (bf16[8,2304]{1,0:T(8,128)(2,1)S(1)}, bf16[8,2304]{1,0:T(8,128)(2,1)S(1)}, u32[]{:S(2)}, u32[]{:S(2)}) collective-permute-start(bf16[8,2304]{1,0:T(8,128)(2,1)S(1)} %pad_maximum_fusion.5), channel_id=1, source_target_pairs={{0,512},{8,520},{16,528},{24,536},{32,544},{40,552},{48,560},{56,5... | collective-permute-start | bytes 110600 | tf_op jit(solution)/shard_map/ppermute | solution.py:37
  78.3 5.1 %features.1 = (bf16[9,288,256]{2,1,0:T(8,128)(2,1)}, bf16[128,2304]{1,0:T(8,128)(2,1)}, bf16[128,2304]{1,0:T(8,128)(2,1)}) custom-call(bf16[288,896]{1,0:T(8,128)(2,1)} %shard_map.77.refs_0_, bf16[256,288]{1,0:T(8,128)(2,1)} %copy.44.refs_1_, bf16[4,96,256]{2,1,0:T(8,128)(2,1)} %copy-done.10, bf16[4,96,256]{2,1,0:T(8,128)(2,1)} %copy-done.7, ...), custom_call_target="tpu_custom_call" | custom-call | tf_op jit(solution)/shard_map/features/pallas_call | solution.py:201
  83.4 5.9 %collective-permute-start.16 = (bf16[128,2304]{1,0:T(8,128)(2,1)}, bf16[128,2304]{1,0:T(8,128)(2,1)S(1)}, u32[]{:S(2)}, u32[]{:S(2)}) collective-permute-start(bf16[128,2304]{1,0:T(8,128)(2,1)} %get-tuple-element.27), channel_id=1, source_target_pairs={{0,1},{1,0},{2,3},{3,2},{4,5},{5,4},{6,7},{7,6},{8,9},{9,8},{10,11... | collective-permute-start | bytes 1769480 | tf_op jit(solution)/shard_map/ppermute | solution.py:41
  89.4 3.6 %collective-permute-start.12 = (bf16[16,2304]{1,0:T(8,128)(2,1)S(1)}, bf16[16,2304]{1,0:T(8,128)(2,1)S(1)}, u32[]{:S(2)}, u32[]{:S(2)}) collective-permute-start(bf16[16,2304]{1,0:T(8,128)(2,1)S(1)} %pad_maximum_fusion.4), channel_id=1, source_target_pairs={{0,8},{8,0},{16,24},{24,16},{32,40},{40,32},{48,56},{56,48},{64,72... | collective-permute-start | bytes 221192 | tf_op jit(solution)/shard_map/ppermute | solution.py:37
  95.1 3.5 %all-to-all-start = ((bf16[4,32,2304]{2,1,0:T(8,128)(2,1)}), bf16[4,32,2304]{2,1,0:T(8,128)(2,1)S(1)}, u32[]{:S(2)}, u32[]{:S(2)}) async-start(bf16[4,32,2304]{2,1,0:T(8,128)(2,1)} %bitcast.12), calls=%async_computation | async-start | bytes 1179648 | tf_op jit(solution)/shard_map/all_to_all | solution.py:227
  100.5 8.0 %all-to-all-done = bf16[4,32,2304]{2,1,0:T(8,128)(2,1)S(1)} async-done(((bf16[4,32,2304]{2,1,0:T(8,128)(2,1)}), bf16[4,32,2304]{2,1,0:T(8,128)(2,1)S(1)}, u32[]{:S(2)}, u32[]{:S(2)}) %all-to-all-start) | async-done | bytes 589856 | tf_op jit(solution)/shard_map/all_to_all | solution.py:227
  109.3 3.4 %all-to-all-start.1 = ((bf16[4,8,2304]{2,1,0:T(8,128)(2,1)}), bf16[4,8,2304]{2,1,0:T(8,128)(2,1)S(1)}, u32[]{:S(2)}, u32[]{:S(2)}) async-start(bf16[4,8,2304]{2,1,0:T(8,128)(2,1)} %bitcast.13), calls=%async_computation.1 | async-start | bytes 294912 | tf_op jit(solution)/shard_map/all_to_all | solution.py:227
  112.7 2.5 %collective-permute-start.14 = (bf16[64,2304]{1,0:T(8,128)(2,1)S(1)}, bf16[64,2304]{1,0:T(8,128)(2,1)S(1)}, u32[]{:S(2)}, u32[]{:S(2)}) collective-permute-start(bf16[64,2304]{1,0:T(8,128)(2,1)S(1)} %pad_maximum_fusion.1), channel_id=1, source_target_pairs={{0,56},{8,48},{16,40},{24,32},{32,24},{40,16},{48,8},{56,0},{64,12... | collective-permute-start | bytes 884744 | tf_op jit(solution)/shard_map/ppermute | solution.py:37
  115.3 2.3 %all-to-all-done.1 = bf16[4,8,2304]{2,1,0:T(8,128)(2,1)S(1)} async-done(((bf16[4,8,2304]{2,1,0:T(8,128)(2,1)}), bf16[4,8,2304]{2,1,0:T(8,128)(2,1)S(1)}, u32[]{:S(2)}, u32[]{:S(2)}) %all-to-all-start.1) | async-done | bytes 147488 | tf_op jit(solution)/shard_map/all_to_all | solution.py:227
  118.2 3.4 %all-to-all-start.2 = ((f32[8,1,2304]{2,1,0:T(1,128)}), f32[8,1,2304]{2,1,0:T(1,128)S(1)}, u32[]{:S(2)}, u32[]{:S(2)}) async-start(f32[8,1,2304]{2,1,0:T(1,128)} %copy.45), calls=%async_computation.2 | async-start | bytes 147456 | tf_op jit(solution)/shard_map/all_to_all | solution.py:227
  121.6 9.5 %collective-permute-done.14 = bf16[64,2304]{1,0:T(8,128)(2,1)S(1)} collective-permute-done((bf16[64,2304]{1,0:T(8,128)(2,1)S(1)}, bf16[64,2304]{1,0:T(8,128)(2,1)S(1)}, u32[]{:S(2)}, u32[]{:S(2)}) %collective-permute-start.14) | collective-permute-done | bytes 294944 | tf_op jit(solution)/shard_map/ppermute | solution.py:37
  131.2 3.6 %collective-permute-start.15 = (bf16[128,2304]{1,0:T(8,128)(2,1)S(1)}, bf16[128,2304]{1,0:T(8,128)(2,1)S(1)}, u32[]{:S(2)}, u32[]{:S(2)}) collective-permute-start(bf16[128,2304]{1,0:T(8,128)(2,1)S(1)} %constant_dynamic-update-slice_fusion.refs_1_), channel_id=1, source_target_pairs={{0,1},{1,0},{2,3},{3,2},{4,5},{5,4},{6,7},{7,6},{8,9},{9,8},{10,11... | collective-permute-start | bytes 1769480 | tf_op jit(solution)/shard_map/ppermute | solution.py:41
  135.5 6.9 %all-to-all-start.3 = ((f32[8,1,2304]{2,1,0:T(1,128)}), f32[8,1,2304]{2,1,0:T(1,128)S(1)}, u32[]{:S(2)}, u32[]{:S(2)}) async-start(f32[8,1,2304]{2,1,0:T(1,128)} %broadcast_in_dim.14), calls=%async_computation.3 | async-start | bytes 147456 | tf_op jit(solution)/shard_map/all_to_all | solution.py:232
  144.1 3.0 %mixing.1 = bf16[4,72,256]{2,1,0:T(8,128)(2,1)} custom-call(bf16[9,288,256]{2,1,0:T(8,128)(2,1)} %get-tuple-element.23.refs_0_, bf16[128,2304]{1,0:T(8,128)(2,1)} %copy-done.2, bf16[128,2304]{1,0:T(8,128)(2,1)} %copy-done.3, bf16[256,256]{1,0:T(8,128)(2,1)} %fusion.refs_3_), custom_call_target="tpu_custom_call" | custom-call | tf_op jit(solution)/shard_map/mixing/pallas_call | solution.py:213
  147.1 9.2 %all-to-all-done.3 = f32[8,1,2304]{2,1,0:T(1,128)S(1)} async-done(((f32[8,1,2304]{2,1,0:T(1,128)}), f32[8,1,2304]{2,1,0:T(1,128)S(1)}, u32[]{:S(2)}, u32[]{:S(2)}) %all-to-all-start.3) | async-done | bytes 73760 | tf_op jit(solution)/shard_map/all_to_all | solution.py:232
  (90 shorter events, 21.5 us)
Async XLA Ops:
  1.5 26.6 %collective-permute-start = (bf16[4,12,256]{2,1,0:T(8,128)(2,1)S(1)}, bf16[4,12,256]{2,1,0:T(8,128)(2,1)S(1)}, u32[]{:S(2)}, u32[]{:S(2)}) collective-permute-start(bf16[4,12,256]{2,1,0:T(8,128)(2,1)S(1)} %get-tuple-element.32), channel_id=1, source_target_pairs={{1,2},{2,1},{3,4},{4,3},{5,6},{6,5},{7,0},{0,7},{9,10},{10,9},{11,... | collective-permute-start | bytes 73736 | tf_op jit(solution)/shard_map/ppermute | solution.py:54
  13.5 14.6 %collective-permute-start.1 = (bf16[4,12,256]{2,1,0:T(8,128)(2,1)S(1)}, bf16[4,12,256]{2,1,0:T(8,128)(2,1)S(1)}, u32[]{:S(2)}, u32[]{:S(2)}) collective-permute-start(bf16[4,12,256]{2,1,0:T(8,128)(2,1)S(1)} %get-tuple-element.33), channel_id=1, source_target_pairs={{0,1},{1,0},{2,3},{3,2},{4,5},{5,4},{6,7},{7,6},{8,9},{9,8},{10,11... | collective-permute-start | bytes 73736 | tf_op jit(solution)/shard_map/ppermute | solution.py:54
  22.6 5.4 %collective-permute-start.2 = (bf16[1,2304]{1,0:T(2,128)(2,1)S(1)}, bf16[1,2304]{1,0:T(2,128)(2,1)S(1)}, u32[]{:S(2)}, u32[]{:S(2)}) collective-permute-start(bf16[1,2304]{1,0:T(2,128)(2,1)S(1)} %constant_dynamic-slice_fusion), channel_id=1, source_target_pairs={{0,64},{8,72},{16,80},{24,88},{32,96},{40,104},{48,112},{56,120},{... | collective-permute-start | bytes 13832 | tf_op jit(solution)/shard_map/ppermute | solution.py:37
  28.6 47.4 %copy-start.1 = (bf16[4,96,256]{2,1,0:T(8,128)(2,1)}, bf16[4,96,256]{2,1,0:T(8,128)(2,1)S(1)}, u32[]{:S(2)}) copy-start(bf16[4,96,256]{2,1,0:T(8,128)(2,1)S(1)} %pad_maximum_fusion.2.refs_5_) | copy-start | bytes 589828
  28.7 8.3 %collective-permute-start.5 = (bf16[2,2304]{1,0:T(2,128)(2,1)S(1)}, bf16[2,2304]{1,0:T(2,128)(2,1)S(1)}, u32[]{:S(2)}, u32[]{:S(2)}) collective-permute-start(bf16[2,2304]{1,0:T(2,128)(2,1)S(1)} %pad_maximum_fusion.7), channel_id=1, source_target_pairs={{0,128},{8,136},{16,144},{24,152},{32,160},{40,168},{48,176},{56,1... | collective-permute-start | bytes 27656 | tf_op jit(solution)/shard_map/ppermute | solution.py:37
  33.1 7.8 %collective-permute-start.3 = (bf16[4,96,256]{2,1,0:T(8,128)(2,1)S(1)}, bf16[4,96,256]{2,1,0:T(8,128)(2,1)S(1)}, u32[]{:S(2)}, u32[]{:S(2)}) collective-permute-start(bf16[4,96,256]{2,1,0:T(8,128)(2,1)S(1)} %pad_maximum_fusion.2.refs_5_), channel_id=1, source_target_pairs={{0,8},{8,0},{16,24},{24,16},{32,40},{40,32},{48,56},{56,48},{64,72... | collective-permute-start | bytes 589832 | tf_op jit(solution)/shard_map/ppermute | solution.py:54
  36.3 4.6 %collective-permute-start.4 = (bf16[4,96,256]{2,1,0:T(8,128)(2,1)S(1)}, bf16[4,96,256]{2,1,0:T(8,128)(2,1)S(1)}, u32[]{:S(2)}, u32[]{:S(2)}) collective-permute-start(bf16[4,96,256]{2,1,0:T(8,128)(2,1)S(1)} %pad_maximum_fusion.2.refs_5_), channel_id=1, source_target_pairs={{8,16},{16,8},{24,32},{32,24},{40,48},{48,40},{56,64},{64,56},{72,... | collective-permute-start | bytes 589832 | tf_op jit(solution)/shard_map/ppermute | solution.py:54
  40.8 36.1 %copy-start.5 = (bf16[4,96,256]{2,1,0:T(8,128)(2,1)}, bf16[4,96,256]{2,1,0:T(8,128)(2,1)S(1)}, u32[]{:S(2)}) copy-start(bf16[4,96,256]{2,1,0:T(8,128)(2,1)S(1)} %collective-permute-done.3.refs_4_) | copy-start | bytes 589828
  40.8 36.1 %copy-start.6 = (bf16[4,96,256]{2,1,0:T(8,128)(2,1)}, bf16[4,96,256]{2,1,0:T(8,128)(2,1)S(1)}, u32[]{:S(2)}) copy-start(bf16[4,96,256]{2,1,0:T(8,128)(2,1)S(1)} %collective-permute-done.4.refs_6_) | copy-start | bytes 589828
  40.8 12.9 %collective-permute-start.8 = (bf16[4,2304]{1,0:T(4,128)(2,1)S(1)}, bf16[4,2304]{1,0:T(4,128)(2,1)S(1)}, u32[]{:S(2)}, u32[]{:S(2)}) collective-permute-start(bf16[4,2304]{1,0:T(4,128)(2,1)S(1)} %pad_maximum_fusion.6), channel_id=1, source_target_pairs={{0,256},{8,264},{16,272},{24,280},{32,288},{40,296},{48,304},{56,3... | collective-permute-start | bytes 55304 | tf_op jit(solution)/shard_map/ppermute | solution.py:37
  51.1 6.4 %collective-permute-start.6 = (bf16[4,96,256]{2,1,0:T(8,128)(2,1)S(1)}, bf16[4,96,256]{2,1,0:T(8,128)(2,1)S(1)}, u32[]{:S(2)}, u32[]{:S(2)}) collective-permute-start(bf16[4,96,256]{2,1,0:T(8,128)(2,1)S(1)} %collective-permute-done.4.refs_6_), channel_id=1, source_target_pairs={{0,8},{8,0},{16,24},{24,16},{32,40},{40,32},{48,56},{56,48},{64,72... | collective-permute-start | bytes 589832 | tf_op jit(solution)/shard_map/ppermute | solution.py:54
  53.0 4.5 %collective-permute-start.7 = (bf16[4,96,256]{2,1,0:T(8,128)(2,1)S(1)}, bf16[4,96,256]{2,1,0:T(8,128)(2,1)S(1)}, u32[]{:S(2)}, u32[]{:S(2)}) collective-permute-start(bf16[4,96,256]{2,1,0:T(8,128)(2,1)S(1)} %collective-permute-done.3.refs_4_), channel_id=1, source_target_pairs={{8,16},{16,8},{24,32},{32,24},{40,48},{48,40},{56,64},{64,56},{72,... | collective-permute-start | bytes 589832 | tf_op jit(solution)/shard_map/ppermute | solution.py:54
  57.5 19.4 %collective-permute-start.10 = (bf16[4,96,256]{2,1,0:T(8,128)(2,1)S(1)}, bf16[4,96,256]{2,1,0:T(8,128)(2,1)S(1)}, u32[]{:S(2)}, u32[]{:S(2)}) collective-permute-start(bf16[4,96,256]{2,1,0:T(8,128)(2,1)S(1)} %collective-permute-done.6.refs_3_), channel_id=1, source_target_pairs={{8,16},{16,8},{24,32},{32,24},{40,48},{48,40},{56,64},{64,56},{72,... | collective-permute-start | bytes 589832 | tf_op jit(solution)/shard_map/ppermute | solution.py:54
  58.2 18.7 %collective-permute-start.9 = (bf16[4,96,256]{2,1,0:T(8,128)(2,1)S(1)}, bf16[4,96,256]{2,1,0:T(8,128)(2,1)S(1)}, u32[]{:S(2)}, u32[]{:S(2)}) collective-permute-start(bf16[4,96,256]{2,1,0:T(8,128)(2,1)S(1)} %collective-permute-done.7.refs_7_), channel_id=1, source_target_pairs={{0,8},{8,0},{16,24},{24,16},{32,40},{40,32},{48,56},{56,48},{64,72... | collective-permute-start | bytes 589832 | tf_op jit(solution)/shard_map/ppermute | solution.py:54
  64.7 24.6 %collective-permute-start.11 = (bf16[8,2304]{1,0:T(8,128)(2,1)S(1)}, bf16[8,2304]{1,0:T(8,128)(2,1)S(1)}, u32[]{:S(2)}, u32[]{:S(2)}) collective-permute-start(bf16[8,2304]{1,0:T(8,128)(2,1)S(1)} %pad_maximum_fusion.5), channel_id=1, source_target_pairs={{0,512},{8,520},{16,528},{24,536},{32,544},{40,552},{48,560},{56,5... | collective-permute-start | bytes 110600 | tf_op jit(solution)/shard_map/ppermute | solution.py:37
  83.4 9.6 %collective-permute-start.16 = (bf16[128,2304]{1,0:T(8,128)(2,1)}, bf16[128,2304]{1,0:T(8,128)(2,1)S(1)}, u32[]{:S(2)}, u32[]{:S(2)}) collective-permute-start(bf16[128,2304]{1,0:T(8,128)(2,1)} %get-tuple-element.27), channel_id=1, source_target_pairs={{0,1},{1,0},{2,3},{3,2},{4,5},{5,4},{6,7},{7,6},{8,9},{9,8},{10,11... | collective-permute-start | bytes 1769480 | tf_op jit(solution)/shard_map/ppermute | solution.py:41
  89.4 9.2 %collective-permute-start.12 = (bf16[16,2304]{1,0:T(8,128)(2,1)S(1)}, bf16[16,2304]{1,0:T(8,128)(2,1)S(1)}, u32[]{:S(2)}, u32[]{:S(2)}) collective-permute-start(bf16[16,2304]{1,0:T(8,128)(2,1)S(1)} %pad_maximum_fusion.4), channel_id=1, source_target_pairs={{0,8},{8,0},{16,24},{24,16},{32,40},{40,32},{48,56},{56,48},{64,72... | collective-permute-start | bytes 221192 | tf_op jit(solution)/shard_map/ppermute | solution.py:37
  95.1 13.5 %all-to-all-start = ((bf16[4,32,2304]{2,1,0:T(8,128)(2,1)}), bf16[4,32,2304]{2,1,0:T(8,128)(2,1)S(1)}, u32[]{:S(2)}, u32[]{:S(2)}) async-start(bf16[4,32,2304]{2,1,0:T(8,128)(2,1)} %bitcast.12), calls=%async_computation | async-start | bytes 1179648 | tf_op jit(solution)/shard_map/all_to_all | solution.py:227
  98.6 14.1 %collective-permute-start.13 = (bf16[32,2304]{1,0:T(8,128)(2,1)S(1)}, bf16[32,2304]{1,0:T(8,128)(2,1)S(1)}, u32[]{:S(2)}, u32[]{:S(2)}) collective-permute-start(bf16[32,2304]{1,0:T(8,128)(2,1)S(1)} %pad_maximum_fusion.3), channel_id=1, source_target_pairs={{0,16},{8,24},{16,0},{24,8},{32,48},{40,56},{48,32},{56,40},{64,80... | collective-permute-start | bytes 442376 | tf_op jit(solution)/shard_map/ppermute | solution.py:37
  109.3 8.2 %all-to-all-start.1 = ((bf16[4,8,2304]{2,1,0:T(8,128)(2,1)}), bf16[4,8,2304]{2,1,0:T(8,128)(2,1)S(1)}, u32[]{:S(2)}, u32[]{:S(2)}) async-start(bf16[4,8,2304]{2,1,0:T(8,128)(2,1)} %bitcast.13), calls=%async_computation.1 | async-start | bytes 294912 | tf_op jit(solution)/shard_map/all_to_all | solution.py:227
  112.7 18.5 %collective-permute-start.14 = (bf16[64,2304]{1,0:T(8,128)(2,1)S(1)}, bf16[64,2304]{1,0:T(8,128)(2,1)S(1)}, u32[]{:S(2)}, u32[]{:S(2)}) collective-permute-start(bf16[64,2304]{1,0:T(8,128)(2,1)S(1)} %pad_maximum_fusion.1), channel_id=1, source_target_pairs={{0,56},{8,48},{16,40},{24,32},{32,24},{40,16},{48,8},{56,0},{64,12... | collective-permute-start | bytes 884744 | tf_op jit(solution)/shard_map/ppermute | solution.py:37
  118.2 16.5 %all-to-all-start.2 = ((f32[8,1,2304]{2,1,0:T(1,128)}), f32[8,1,2304]{2,1,0:T(1,128)S(1)}, u32[]{:S(2)}, u32[]{:S(2)}) async-start(f32[8,1,2304]{2,1,0:T(1,128)} %copy.45), calls=%async_computation.2 | async-start | bytes 147456 | tf_op jit(solution)/shard_map/all_to_all | solution.py:227
  131.2 12.1 %collective-permute-start.15 = (bf16[128,2304]{1,0:T(8,128)(2,1)S(1)}, bf16[128,2304]{1,0:T(8,128)(2,1)S(1)}, u32[]{:S(2)}, u32[]{:S(2)}) collective-permute-start(bf16[128,2304]{1,0:T(8,128)(2,1)S(1)} %constant_dynamic-update-slice_fusion.refs_1_), channel_id=1, source_target_pairs={{0,1},{1,0},{2,3},{3,2},{4,5},{5,4},{6,7},{7,6},{8,9},{9,8},{10,11... | collective-permute-start | bytes 1769480 | tf_op jit(solution)/shard_map/ppermute | solution.py:41
  135.5 20.7 %all-to-all-start.3 = ((f32[8,1,2304]{2,1,0:T(1,128)}), f32[8,1,2304]{2,1,0:T(1,128)S(1)}, u32[]{:S(2)}, u32[]{:S(2)}) async-start(f32[8,1,2304]{2,1,0:T(1,128)} %broadcast_in_dim.14), calls=%async_computation.3 | async-start | bytes 147456 | tf_op jit(solution)/shard_map/all_to_all | solution.py:232
  (10 other events, 129.0 us)

commit v3 on v2

--- a/solution.py
+++ b/solution.py
@@ -9,7 +9,6 @@
 
 FACTORS = {128: (4, 4, 8), 8: (2, 2, 2)}
 TILE = 8
-MASKS = {128: (8, 16, 32, 64, 1, 2, 7), 8: (2, 4, 1)}
 
 
 def dot(a, b, contract):
@@ -33,12 +32,13 @@
     return [members[fixed] for fixed in sorted(members)]
 
 
-def swapped_lat(block, bit):
-    return lax.ppermute(block, "lat", [(i, i ^ bit) for i in range(lax.axis_size("lat"))])
-
-
 def swapped_core(block):
     return lax.ppermute(block, "lon", [(i, i ^ 1) for i in range(lax.axis_size("lon"))])
+
+
+def passed_along(block, by):
+    count = lax.axis_size("lat")
+    return lax.ppermute(block, "lat", [(i, i + by) for i in range(count) if 0 <= i + by < count])
 
 
 def paired(block, axis, first, loop):
@@ -54,6 +54,18 @@
     return lax.ppermute(block, axis, pairs)
 
 
+def spread_over(block, dim, factors):
+    copies = jnp.broadcast_to(block, (factors[dim],) + block.shape)
+    joined = lax.all_to_all(copies, "lat", 0, 0, axis_index_groups=groups((dim,), factors))
+    return joined.reshape(-1, block.shape[1])
+
+
+def doubled(block, mask, factors):
+    mask = mask * factors[1] * factors[2]
+    pairs = [(i, i ^ mask) for i in range(lax.axis_size("lat"))]
+    return jnp.concatenate([block, lax.ppermute(block, "lat", pairs)], axis=0)
+
+
 def band_kernel(rows_ref, band_ref):
     count, width = rows_ref.shape
     for start in range(0, count, 2):
@@ -65,20 +77,24 @@
         band_ref[start * TILE : (start + 2) * TILE, :] = both
 
 
-def feature_kernel(nbasis, tile_count, *refs):
-    band_ref, cot_ref = refs[0], refs[1]
-    window_refs = refs[2:9]
-    features_ref, keep_ref, send_ref = refs[9:]
-    rows = window_refs[0].shape[0]
-    reach = band_ref.shape[1] // (7 * rows)
+def feature_kernel(nbasis, tile_count, core_ref, band_ref, cot_ref, near_ref, far_ref, *refs):
+    piece_refs = refs[:7]
+    features_ref, keep_ref, send_ref, window_ref = refs[7:]
+    rows, cols, _ = piece_refs[0].shape
+    window_rows = window_ref.shape[0]
+    reach = near_ref.shape[1]
+    span = band_ref.shape[1] // window_rows
     per_tile = rows * TILE
+    first = core_ref[0] == 0
+    for row in range(window_rows):
+        near, far = near_ref[row], far_ref[row]
+        window_ref[row, :reach, :] = jnp.where(first, far, near)
+        window_ref[row, reach : reach + cols, :] = piece_refs[row // rows][row % rows]
+        window_ref[row, reach + cols :, :] = jnp.where(first, near, far)
     band = band_ref[...]
     for tile in range(tile_count):
-        pieces = []
-        for ref in window_refs:
-            for row in range(rows):
-                pieces.append(ref[row, tile * TILE : tile * TILE + reach, :])
-        window = jnp.concatenate(pieces, axis=0)
+        window = window_ref[:, tile * TILE : tile * TILE + span, :]
+        window = window.reshape(window_rows * span, window.shape[2])
         summed = dot(band, window, ((1,), (0,))).astype(jnp.bfloat16)
         for k in range(nbasis):
             features_ref[k, tile * per_tile : (tile + 1) * per_tile, :] = summed[
@@ -127,44 +143,10 @@
     cells = rows * cols
     bf16 = jnp.bfloat16
 
-    masks = MASKS[lax.axis_size("lat")]
-    owners = [0]
-    for mask in masks:
-        owners = owners + [owner ^ mask for owner in owners]
-
-    def doubled(block, turn):
-        if turn >= len(masks):
-            return block
-        return jnp.concatenate([block, swapped_lat(block, masks[turn])], axis=0)
-
-    gathered = doubled(lax.dynamic_slice_in_dim(weight, core, 1, 0), 0)
-
-    edges = jnp.where(core == 0, fields[:, cols - reach :], fields[:, :reach])
-    other_edges = jnp.where(core == 0, fields[:, :reach], fields[:, cols - reach :])
-    near_edge = paired(edges, "lon", 0, True)
-    far_edge = paired(other_edges, "lon", 1, True)
-    left = jnp.where(core == 0, far_edge, near_edge)
-    right = jnp.where(core == 0, near_edge, far_edge)
-    own = jnp.concatenate([left, fields, right], axis=1)
-    near, far = own, own
-    nears, fars = [], []
-    for turn in range(3):
-        near, far, gathered = lax.optimization_barrier((near, far, gathered))
-        near, far = paired(far, "lat", 0, False), paired(near, "lat", 1, False)
-        gathered = doubled(gathered, turn + 1)
-        nears.append(near)
-        fars.append(far)
-    windows = nears[::-1] + [own] + fars
-
-    near, gathered = lax.optimization_barrier((near, gathered))
-    nears[-1] = near
-    for turn in range(4, len(masks)):
-        gathered = doubled(gathered, turn)
-    other_weight = swapped_core(gathered)
-    position = jnp.arange(outs)
-    half = outs // 2
-    weight_row = 2 * (lat ^ jnp.array(owners + owners, jnp.int32)) + (core ^ (position // half))
-    weight_order = (weight_row[:, None] == jnp.arange(outs)[None, :]).astype(bf16)
+    gathered = lax.dynamic_slice_in_dim(weight, core, 1, 0)
+    gathered = spread_over(gathered, 2, factors)
+    gathered = doubled(gathered, 1, factors)
+    gathered = spread_over(gathered, 1, factors)
 
     offsets = jnp.arange(width) - reach
     validity = jnp.abs(offsets)[None, None, :] <= spans[:, :, None]
@@ -176,9 +158,7 @@
             for row in range(rows)
         ],
         axis=1,
-    ).reshape(nbasis * rows, window_rows // rows, rows * window_cols)
-    band_rows = jnp.where(lat % 2 == 0, band_rows[:, ::-1], band_rows)
-    band_rows = band_rows.reshape(nbasis * rows, window_rows * window_cols)
+    ).reshape(nbasis * rows, window_rows * window_cols)
     band = pl.pallas_call(
         band_kernel,
         out_shape=jax.ShapeDtypeStruct((nbasis * rows * TILE, window_rows * window_cols), bf16),
@@ -187,6 +167,9 @@
     )(band_rows)
 
     zs, xs, ys = factors
+    z_at = lat // (xs * ys)
+    position = jnp.arange(outs)
+    half = outs // 2
     away = (
         2
         * lat_index(
@@ -198,6 +181,21 @@
     cot_cells = jnp.transpose(cotangent.reshape(rows, tile_count, TILE, outs), (1, 0, 2, 3))
     cot = dot(cot_order, cot_cells.reshape(cells, outs), ((1,), (1,))).astype(bf16)
 
+    shifts = (3, 2, 1, -1, -2, -3)
+    windows = {0: fields}
+    for by in shifts:
+        windows[by] = passed_along(fields, by)
+    pieces = [windows[by] for by in (3, 2, 1, 0, -1, -2, -3)]
+    low = jnp.concatenate([piece[:, :reach] for piece in pieces], axis=0)
+    high = jnp.concatenate([piece[:, cols - reach :] for piece in pieces], axis=0)
+    to_near = jnp.where(core == 0, high, low)
+    to_far = jnp.where(core == 0, low, high)
+    to_near, to_far, band, cot, gathered = lax.optimization_barrier(
+        (to_near, to_far, band, cot, gathered)
+    )
+    far_edge = paired(to_far, "lon", 1, True)
+    near_edge = paired(to_near, "lon", 0, True)
+
     features, keep, send = pl.pallas_call(
         lambda *refs: feature_kernel(nbasis, tile_count, *refs),
         out_shape=(
@@ -205,11 +203,31 @@
             jax.ShapeDtypeStruct((half, nbasis * channels), bf16),
             jax.ShapeDtypeStruct((half, nbasis * channels), bf16),
         ),
-        in_specs=vmem(9),
+        in_specs=[pl.BlockSpec(memory_space=pltpu.SMEM)] + vmem(11),
         out_specs=tuple(vmem(3)),
+        scratch_shapes=[pltpu.VMEM((window_rows, cols + 2 * reach, channels), bf16)],
         name="features",
-    )(band, cot, *windows)
-
+    )(core.reshape(1).astype(jnp.int32), band, cot, near_edge, far_edge, *pieces)
+
+    if zs == 4:
+        gathered = doubled(gathered, 2, factors)
+    place = position % half
+    from_z = z_at ^ (place // ys % 2 + place // (2 * ys * xs) * 2)
+    weight_row = 2 * lat_index(from_z, place // (2 * ys) % xs, place % ys, factors)
+    weight_row = weight_row + (core ^ (position // half))
+    weight_order = (weight_row[:, None] == jnp.arange(outs)[None, :]).astype(bf16)
+
+    f32 = jnp.float32
+    total = keep.astype(f32) + swapped_core(send).astype(f32)
+    for dim in (1, 0, 2):
+        count = factors[dim]
+        if dim == 0:
+            total, gathered = lax.optimization_barrier((total, gathered))
+        moved = total if dim == 2 else total.astype(bf16)
+        moved = moved.reshape(count, -1, moved.shape[1])
+        arrived = lax.all_to_all(moved, "lat", 0, 0, axis_index_groups=groups((dim,), factors))
+        total = jnp.sum(arrived.astype(f32), axis=0)
+    other_weight = swapped_core(gathered)
     output = pl.pallas_call(
         lambda *refs: output_kernel(tile_count, *refs),
         out_shape=jax.ShapeDtypeStruct((rows, cols, outs), bf16),
@@ -218,14 +236,6 @@
         name="mixing",
     )(features, gathered, other_weight, weight_order)
 
-    f32 = jnp.float32
-    total = keep.astype(f32) + swapped_core(send).astype(f32)
-    for dim in (1, 0, 2):
-        count = factors[dim]
-        moved = total if dim == 2 else total.astype(bf16)
-        moved = moved.reshape(count, -1, moved.shape[1])
-        arrived = lax.all_to_all(moved, "lat", 0, 0, axis_index_groups=groups((dim,), factors))
-        total = jnp.sum(arrived.astype(f32), axis=0)
     scale = 1.0 / math.sqrt(rows * lax.axis_size("lat") * cols * lax.axis_size("lon"))
     lon_size = lax.axis_size("lon")
     spread = jnp.broadcast_to(total * scale, (lon_size,) + total.shape)

time: 158 us -> 168 us (1.063)
  waiting for transfers between devices: 36.7 us -> 47.5 us
  starting transfers between devices: 95.5 us -> 87 us
  blocking collectives: 0 us -> 7.97 us
    ppermute x8 -> x2, starting transfers between devices: 34.7 us -> 19 us  [paired(): return lax.ppermute(block, axis, pairs)]
    ppermute x7 -> x8, waiting for transfers between devices: 9.56 us -> 19.9 us  [the longest x6 11.7 us: passed_along(): lax.ppermute(block, 'lat', [(i, i + by) for i in range(count) if 0 <= i +...]
    all_to_all x0 -> x2, starting transfers between devices: none -> 10.3 us  [spread_over(): lax.all_to_all(copies, 'lat', 0, 0, axis_index_groups=groups((dim,), fact...]
    all_to_all x0 -> x1, blocking collectives: none -> 7.97 us  [shards(): lax.all_to_all(moved, 'lat', 0, 0, axis_index_groups=groups((dim,), facto...]
    all_to_all x3 -> x2, waiting for transfers between devices: 10.3 us -> 4.92 us  [shards(): lax.all_to_all(moved, 'lat', 0, 0, axis_index_groups=groups((dim,), facto...]
    all_to_all x0 -> x2, waiting for transfers between devices: none -> 3.85 us  [spread_over(): lax.all_to_all(copies, 'lat', 0, 0, axis_index_groups=groups((dim,), fact...]
    ppermute x8 -> x2, waiting for transfers between devices: 7.62 us -> 11.4 us  [paired(): return lax.ppermute(block, axis, pairs)]
    all_to_all x1, starting transfers between devices: 6.94 us -> 10.4 us  [shards(): arrived = lax.all_to_all(spread, 'lon', 0, 0)]
  transfers between devices with their start and end apart: 21 -> 17, of which waited for: 6 -> 8; matrix products, arithmetic and copies ran while one was open for 6% -> 6% of each run, Pallas kernels for 6% -> 3%
where the time goes in v3:
time: 168 us; the launch traced here: 167 us
  starting transfers between devices  87 us (52%)
  waiting for transfers between devices  47.5 us (28%)
  Pallas kernels  10.1 us (6%)
  blocking collectives  7.97 us (5%)
  other arithmetic  6.55 us (4%)
  local copies, waits for them, and re-layouts  6.08 us (4%)
    ppermute x2, starting transfers between devices, paired(): return lax.ppermute(block, axis, pairs)  19 us
    ppermute x6, starting transfers between devices, passed_along(): lax.ppermute(block, 'lat', [(i, i + by) for i in range(count) if 0 <= i +...  16.8 us
    ppermute x2, starting transfers between devices, doubled(): return jnp.concatenate([block, lax.ppermute(block, 'lat', pairs)], axis=0)  15.9 us
    ppermute x6, waiting for transfers between devices, passed_along(): lax.ppermute(block, 'lat', [(i, i + by) for i in range(count) if 0 <= i +...  11.7 us
    ppermute x2, waiting for transfers between devices, paired(): return lax.ppermute(block, axis, pairs)  11.4 us
    all_to_all x1, starting transfers between devices, shards(): arrived = lax.all_to_all(spread, 'lon', 0, 0)  10.4 us
    all_to_all x2, starting transfers between devices, spread_over(): lax.all_to_all(copies, 'lat', 0, 0, axis_index_groups=groups((dim,), fact...  10.3 us
    ppermute x2, waiting for transfers between devices, doubled(): return jnp.concatenate([block, lax.ppermute(block, 'lat', pairs)], axis=0)  8.16 us
  transfers between devices with their start and end apart: 17, of which 8 were waited for; matrix products, arithmetic and copies ran while one was open for 6% of the time, Pallas kernels for 3%

profile of v3, /device:TPU:1, one launch (start us, length us, event | category | flops | bytes accessed | tf_op | source)
XLA Modules:
  0.0 167.4 jit_solution(3196247966864090315)
XLA Ops:
  0.6 6.1 %collective-permute-start = (bf16[4,72,256]{2,1,0:T(8,128)(2,1)}, bf16[4,72,256]{2,1,0:T(8,128)(2,1)S(1)}, u32[]{:S(2)}, u32[]{:S(2)}) collective-permute-start(bf16[4,72,256]{2,1,0:T(8,128)(2,1)} %refs_8_.1), channel_id=1, source_target_pairs={{0,24},{8,32},{16,40},{24,48},{32,56},{40,64},{48,72},{56,80},{64,... | collective-permute-start | bytes 442376 | tf_op jit(solution)/shard_map/ppermute | solution.py:41
  6.7 4.5 %collective-permute-start.1 = (bf16[4,72,256]{2,1,0:T(8,128)(2,1)}, bf16[4,72,256]{2,1,0:T(8,128)(2,1)S(1)}, u32[]{:S(2)}, u32[]{:S(2)}) collective-permute-start(bf16[4,72,256]{2,1,0:T(8,128)(2,1)} %refs_8_.1), channel_id=1, source_target_pairs={{0,16},{8,24},{16,32},{24,40},{32,48},{40,56},{48,64},{56,72},{64,... | collective-permute-start | bytes 442376 | tf_op jit(solution)/shard_map/ppermute | solution.py:41
  11.3 2.3 %collective-permute-start.2 = (bf16[4,72,256]{2,1,0:T(8,128)(2,1)}, bf16[4,72,256]{2,1,0:T(8,128)(2,1)S(1)}, u32[]{:S(2)}, u32[]{:S(2)}) collective-permute-start(bf16[4,72,256]{2,1,0:T(8,128)(2,1)} %refs_8_.1), channel_id=1, source_target_pairs={{0,8},{8,16},{16,24},{24,32},{32,40},{40,48},{48,56},{56,64},{64,7... | collective-permute-start | bytes 442376 | tf_op jit(solution)/shard_map/ppermute | solution.py:41
  17.0 6.2 %all-to-all-start = ((bf16[8,2,1152]{2,1,0:T(2,128)(2,1)}), bf16[8,2,1152]{2,1,0:T(2,128)(2,1)S(1)}, u32[]{:S(2)}, u32[]{:S(2)}) async-start(bf16[8,2,1152]{2,1,0:T(2,128)(2,1)} %reshape.212), calls=%async_computation | async-start | bytes 73728 | tf_op jit(solution)/shard_map/all_to_all | solution.py:59
  26.1 3.8 %all-to-all-done = bf16[8,2,1152]{2,1,0:T(2,128)(2,1)S(1)} async-done(((bf16[8,2,1152]{2,1,0:T(2,128)(2,1)}), bf16[8,2,1152]{2,1,0:T(2,128)(2,1)S(1)}, u32[]{:S(2)}, u32[]{:S(2)}) %all-to-all-start) | async-done | bytes 36896 | tf_op jit(solution)/shard_map/all_to_all | solution.py:59
  30.0 7.2 %collective-permute-start.6 = (bf16[8,2304]{1,0:T(8,128)(2,1)S(1)}, bf16[8,2304]{1,0:T(8,128)(2,1)S(1)}, u32[]{:S(2)}, u32[]{:S(2)}) collective-permute-start(bf16[8,2304]{1,0:T(8,128)(2,1)S(1)} %bitcast.39), channel_id=1, source_target_pairs={{0,256},{8,264},{16,272},{24,280},{32,288},{40,296},{48,304},{56,3... | collective-permute-start | bytes 110600 | tf_op jit(solution)/shard_map/ppermute | solution.py:66
  42.1 4.1 %all-to-all-start.1 = ((bf16[4,16,2304]{2,1,0:T(8,128)(2,1)}), bf16[4,16,2304]{2,1,0:T(8,128)(2,1)S(1)}, u32[]{:S(2)}, u32[]{:S(2)}) async-start(bf16[4,16,2304]{2,1,0:T(8,128)(2,1)} %broadcast_in_dim.30), calls=%async_computation.1 | async-start | bytes 589824 | tf_op jit(solution)/shard_map/all_to_all | solution.py:59
  48.5 11.0 %collective-permute-done.5.refs_11_ = bf16[4,72,256]{2,1,0:T(8,128)(2,1)S(1)} collective-permute-done((bf16[4,72,256]{2,1,0:T(8,128)(2,1)S(1)}, bf16[4,72,256]{2,1,0:T(8,128)(2,1)S(1)}, u32[]{:S(2)}, u32[]{:S(2)}) %collective-permute-start.5) | collective-permute-done | bytes 147488 | tf_op jit(solution)/shard_map/ppermute | solution.py:41
  59.5 8.4 %collective-permute-start.7 = (bf16[28,12,256]{2,1,0:T(8,128)(2,1)S(1)}, bf16[28,12,256]{2,1,0:T(8,128)(2,1)S(1)}, u32[]{:S(2)}, u32[]{:S(2)}) collective-permute-start(bf16[28,12,256]{2,1,0:T(8,128)(2,1)S(1)} %get-tuple-element.14), channel_id=1, source_target_pairs={{0,1},{1,0},{2,3},{3,2},{4,5},{5,4},{6,7},{7,6},{8,9},{9,8},{10,11... | collective-permute-start | bytes 516104 | tf_op jit(solution)/shard_map/ppermute | solution.py:54
  67.9 10.5 %collective-permute-start.8 = (bf16[28,12,256]{2,1,0:T(8,128)(2,1)S(1)}, bf16[28,12,256]{2,1,0:T(8,128)(2,1)S(1)}, u32[]{:S(2)}, u32[]{:S(2)}) collective-permute-start(bf16[28,12,256]{2,1,0:T(8,128)(2,1)S(1)} %get-tuple-element.15), channel_id=1, source_target_pairs={{1,2},{2,1},{3,4},{4,3},{5,6},{6,5},{7,0},{0,7},{9,10},{10,9},{11,... | collective-permute-start | bytes 516104 | tf_op jit(solution)/shard_map/ppermute | solution.py:54
  78.5 11.4 %collective-permute-done.8.refs_4_ = bf16[28,12,256]{2,1,0:T(8,128)(2,1)S(1)} collective-permute-done((bf16[28,12,256]{2,1,0:T(8,128)(2,1)S(1)}, bf16[28,12,256]{2,1,0:T(8,128)(2,1)S(1)}, u32[]{:S(2)}, u32[]{:S(2)}) %collective-permute-start.8) | collective-permute-done | bytes 172064 | tf_op jit(solution)/shard_map/ppermute | solution.py:54
  90.6 5.2 %features.1 = (bf16[9,288,256]{2,1,0:T(8,128)(2,1)}, bf16[128,2304]{1,0:T(8,128)(2,1)}, bf16[128,2304]{1,0:T(8,128)(2,1)}) custom-call(s32[1]{0:T(128)} %bitcast.refs_0_, bf16[288,896]{1,0:T(8,128)(2,1)} %shard_map.68.refs_1_, bf16[256,288]{1,0:T(8,128)(2,1)} %convolution_convert_fusion.refs_2_, bf16[28,12,256]{2,1,0:T(8,128)(2,1)} %copy-done.10, ...), custom_call_target="tpu_custom_call" | custom-call | tf_op jit(solution)/shard_map/features/pallas_call | solution.py:199
  95.8 3.8 %collective-permute-start.9 = (bf16[128,2304]{1,0:T(8,128)(2,1)}, bf16[128,2304]{1,0:T(8,128)(2,1)S(1)}, u32[]{:S(2)}, u32[]{:S(2)}) collective-permute-start(bf16[128,2304]{1,0:T(8,128)(2,1)} %get-tuple-element.18), channel_id=1, source_target_pairs={{0,1},{1,0},{2,3},{3,2},{4,5},{5,4},{6,7},{7,6},{8,9},{9,8},{10,11... | collective-permute-start | bytes 1769480 | tf_op jit(solution)/shard_map/ppermute | solution.py:36
  99.6 8.7 %collective-permute-start.10 = (bf16[64,2304]{1,0:T(8,128)(2,1)S(1)}, bf16[64,2304]{1,0:T(8,128)(2,1)S(1)}, u32[]{:S(2)}, u32[]{:S(2)}) collective-permute-start(bf16[64,2304]{1,0:T(8,128)(2,1)S(1)} %bitcast.33), channel_id=1, source_target_pairs={{0,512},{8,520},{16,528},{24,536},{32,544},{40,552},{48,560},{56,5... | collective-permute-start | bytes 884744 | tf_op jit(solution)/shard_map/ppermute | solution.py:66
  108.3 2.0 %add_convert_fusion = bf16[128,2304]{1,0:T(8,128)(2,1)} fusion(bf16[128,2304]{1,0:T(8,128)(2,1)S(1)} %collective-permute-done.9, bf16[128,2304]{1,0:T(8,128)(2,1)} %get-tuple-element.17), kind=kLoop, calls=%fused_computation.1 | loop fusion | flops 1179648 | bytes 1769472 | tf_op jit(solution)/shard_map/convert_element_type | solution.py:226
  110.3 3.5 %all-to-all-start.2 = ((bf16[4,32,2304]{2,1,0:T(8,128)(2,1)}), bf16[4,32,2304]{2,1,0:T(8,128)(2,1)S(1)}, u32[]{:S(2)}, u32[]{:S(2)}) async-start(bf16[4,32,2304]{2,1,0:T(8,128)(2,1)} %bitcast.14), calls=%async_computation.2 | async-start | bytes 1179648 | tf_op jit(solution)/shard_map/all_to_all | solution.py:228
  113.8 8.2 %collective-permute-done.10 = bf16[64,2304]{1,0:T(8,128)(2,1)S(1)} collective-permute-done((bf16[64,2304]{1,0:T(8,128)(2,1)S(1)}, bf16[64,2304]{1,0:T(8,128)(2,1)S(1)}, u32[]{:S(2)}, u32[]{:S(2)}) %collective-permute-start.10) | collective-permute-done | bytes 294944 | tf_op jit(solution)/shard_map/ppermute | solution.py:66
  123.9 8.0 %all_to_all.30 = bf16[4,8,2304]{2,1,0:T(8,128)(2,1)S(1)} all-to-all(bf16[4,8,2304]{2,1,0:T(8,128)(2,1)S(1)} %bitcast.36), channel_id=1, replica_groups={{0,256,512,768},{8,264,520,776},{16,272,528,784},{24,280,536,792},{32,2..., dimensions={0} | all-to-all | bytes 294912 | tf_op jit(solution)/shard_map/all_to_all | solution.py:228
  132.6 3.4 %all-to-all-start.4 = ((f32[8,1,2304]{2,1,0:T(1,128)}), f32[8,1,2304]{2,1,0:T(1,128)S(1)}, u32[]{:S(2)}, u32[]{:S(2)}) async-start(f32[8,1,2304]{2,1,0:T(1,128)} %copy.43), calls=%async_computation.4 | async-start | bytes 147456 | tf_op jit(solution)/shard_map/all_to_all | solution.py:228
  135.9 4.1 %collective-permute-start.11 = (bf16[128,2304]{1,0:T(8,128)(2,1)S(1)}, bf16[128,2304]{1,0:T(8,128)(2,1)S(1)}, u32[]{:S(2)}, u32[]{:S(2)}) collective-permute-start(bf16[128,2304]{1,0:T(8,128)(2,1)S(1)} %pad_maximum_fusion.1.refs_1_), channel_id=1, source_target_pairs={{0,1},{1,0},{2,3},{3,2},{4,5},{5,4},{6,7},{7,6},{8,9},{9,8},{10,11... | collective-permute-start | bytes 1769480 | tf_op jit(solution)/shard_map/ppermute | solution.py:36
  140.0 3.1 %all-to-all-done.4 = f32[8,1,2304]{2,1,0:T(1,128)S(1)} async-done(((f32[8,1,2304]{2,1,0:T(1,128)}), f32[8,1,2304]{2,1,0:T(1,128)S(1)}, u32[]{:S(2)}, u32[]{:S(2)}) %all-to-all-start.4) | async-done | bytes 73760 | tf_op jit(solution)/shard_map/all_to_all | solution.py:228
  143.9 10.4 %all-to-all-start.5 = ((f32[8,1,2304]{2,1,0:T(1,128)}), f32[8,1,2304]{2,1,0:T(1,128)S(1)}, u32[]{:S(2)}, u32[]{:S(2)}) async-start(f32[8,1,2304]{2,1,0:T(1,128)} %broadcast_in_dim.31), calls=%async_computation.5 | async-start | bytes 147456 | tf_op jit(solution)/shard_map/all_to_all | solution.py:242
  156.0 3.0 %mixing.1 = bf16[4,72,256]{2,1,0:T(8,128)(2,1)} custom-call(bf16[9,288,256]{2,1,0:T(8,128)(2,1)} %get-tuple-element.16.refs_0_, bf16[128,2304]{1,0:T(8,128)(2,1)} %copy-done.1, bf16[128,2304]{1,0:T(8,128)(2,1)} %copy-done.2, bf16[256,256]{1,0:T(8,128)(2,1)} %fusion.refs_3_), custom_call_target="tpu_custom_call" | custom-call | tf_op jit(solution)/shard_map/mixing/pallas_call | solution.py:231
  159.0 7.5 %all-to-all-done.5 = f32[8,1,2304]{2,1,0:T(1,128)S(1)} async-done(((f32[8,1,2304]{2,1,0:T(1,128)}), f32[8,1,2304]{2,1,0:T(1,128)S(1)}, u32[]{:S(2)}, u32[]{:S(2)}) %all-to-all-start.5) | async-done | bytes 73760 | tf_op jit(solution)/shard_map/all_to_all | solution.py:242
  (82 shorter events, 19.9 us)
Async XLA Ops:
  0.6 45.6 %collective-permute-start = (bf16[4,72,256]{2,1,0:T(8,128)(2,1)}, bf16[4,72,256]{2,1,0:T(8,128)(2,1)S(1)}, u32[]{:S(2)}, u32[]{:S(2)}) collective-permute-start(bf16[4,72,256]{2,1,0:T(8,128)(2,1)} %refs_8_.1), channel_id=1, source_target_pairs={{0,24},{8,32},{16,40},{24,48},{32,56},{40,64},{48,72},{56,80},{64,... | collective-permute-start | bytes 442376 | tf_op jit(solution)/shard_map/ppermute | solution.py:41
  6.7 40.8 %collective-permute-start.1 = (bf16[4,72,256]{2,1,0:T(8,128)(2,1)}, bf16[4,72,256]{2,1,0:T(8,128)(2,1)S(1)}, u32[]{:S(2)}, u32[]{:S(2)}) collective-permute-start(bf16[4,72,256]{2,1,0:T(8,128)(2,1)} %refs_8_.1), channel_id=1, source_target_pairs={{0,16},{8,24},{16,32},{24,40},{32,48},{40,56},{48,64},{56,72},{64,... | collective-permute-start | bytes 442376 | tf_op jit(solution)/shard_map/ppermute | solution.py:41
  11.3 36.3 %collective-permute-start.2 = (bf16[4,72,256]{2,1,0:T(8,128)(2,1)}, bf16[4,72,256]{2,1,0:T(8,128)(2,1)S(1)}, u32[]{:S(2)}, u32[]{:S(2)}) collective-permute-start(bf16[4,72,256]{2,1,0:T(8,128)(2,1)} %refs_8_.1), channel_id=1, source_target_pairs={{0,8},{8,16},{16,24},{24,32},{32,40},{40,48},{48,56},{56,64},{64,7... | collective-permute-start | bytes 442376 | tf_op jit(solution)/shard_map/ppermute | solution.py:41
  13.6 34.1 %collective-permute-start.3 = (bf16[4,72,256]{2,1,0:T(8,128)(2,1)}, bf16[4,72,256]{2,1,0:T(8,128)(2,1)S(1)}, u32[]{:S(2)}, u32[]{:S(2)}) collective-permute-start(bf16[4,72,256]{2,1,0:T(8,128)(2,1)} %refs_8_.1), channel_id=1, source_target_pairs={{8,0},{16,8},{24,16},{32,24},{40,32},{48,40},{56,48},{64,56},{72,6... | collective-permute-start | bytes 442376 | tf_op jit(solution)/shard_map/ppermute | solution.py:41
  17.0 12.9 %all-to-all-start = ((bf16[8,2,1152]{2,1,0:T(2,128)(2,1)}), bf16[8,2,1152]{2,1,0:T(2,128)(2,1)S(1)}, u32[]{:S(2)}, u32[]{:S(2)}) async-start(bf16[8,2,1152]{2,1,0:T(2,128)(2,1)} %reshape.212), calls=%async_computation | async-start | bytes 73728 | tf_op jit(solution)/shard_map/all_to_all | solution.py:59
  30.0 10.1 %collective-permute-start.6 = (bf16[8,2304]{1,0:T(8,128)(2,1)S(1)}, bf16[8,2304]{1,0:T(8,128)(2,1)S(1)}, u32[]{:S(2)}, u32[]{:S(2)}) collective-permute-start(bf16[8,2304]{1,0:T(8,128)(2,1)S(1)} %bitcast.39), channel_id=1, source_target_pairs={{0,256},{8,264},{16,272},{24,280},{32,288},{40,296},{48,304},{56,3... | collective-permute-start | bytes 110600 | tf_op jit(solution)/shard_map/ppermute | solution.py:66
  40.1 8.4 %collective-permute-start.4 = (bf16[4,72,256]{2,1,0:T(8,128)(2,1)S(1)}, bf16[4,72,256]{2,1,0:T(8,128)(2,1)S(1)}, u32[]{:S(2)}, u32[]{:S(2)}) collective-permute-start(bf16[4,72,256]{2,1,0:T(8,128)(2,1)S(1)} %copy-done.3), channel_id=1, source_target_pairs={{16,0},{24,8},{32,16},{40,24},{48,32},{56,40},{64,48},{72,56},{80,... | collective-permute-start | bytes 442376 | tf_op jit(solution)/shard_map/ppermute | solution.py:41
  42.1 17.4 %all-to-all-start.1 = ((bf16[4,16,2304]{2,1,0:T(8,128)(2,1)}), bf16[4,16,2304]{2,1,0:T(8,128)(2,1)S(1)}, u32[]{:S(2)}, u32[]{:S(2)}) async-start(bf16[4,16,2304]{2,1,0:T(8,128)(2,1)} %broadcast_in_dim.30), calls=%async_computation.1 | async-start | bytes 589824 | tf_op jit(solution)/shard_map/all_to_all | solution.py:59
  46.2 43.6 %copy-start.4 = (bf16[4,72,256]{2,1,0:T(8,128)(2,1)}, bf16[4,72,256]{2,1,0:T(8,128)(2,1)S(1)}, u32[]{:S(2)}) copy-start(bf16[4,72,256]{2,1,0:T(8,128)(2,1)S(1)} %collective-permute-done.refs_5_) | copy-start | bytes 442372
  46.2 13.2 %collective-permute-start.5 = (bf16[4,72,256]{2,1,0:T(8,128)(2,1)S(1)}, bf16[4,72,256]{2,1,0:T(8,128)(2,1)S(1)}, u32[]{:S(2)}, u32[]{:S(2)}) collective-permute-start(bf16[4,72,256]{2,1,0:T(8,128)(2,1)S(1)} %copy-done.3), channel_id=1, source_target_pairs={{24,0},{32,8},{40,16},{48,24},{56,32},{64,40},{72,48},{80,56},{88,... | collective-permute-start | bytes 442376 | tf_op jit(solution)/shard_map/ppermute | solution.py:41
  47.6 42.3 %copy-start.5 = (bf16[4,72,256]{2,1,0:T(8,128)(2,1)}, bf16[4,72,256]{2,1,0:T(8,128)(2,1)S(1)}, u32[]{:S(2)}) copy-start(bf16[4,72,256]{2,1,0:T(8,128)(2,1)S(1)} %collective-permute-done.1.refs_6_) | copy-start | bytes 442372
  47.6 42.3 %copy-start.6 = (bf16[4,72,256]{2,1,0:T(8,128)(2,1)}, bf16[4,72,256]{2,1,0:T(8,128)(2,1)S(1)}, u32[]{:S(2)}) copy-start(bf16[4,72,256]{2,1,0:T(8,128)(2,1)S(1)} %collective-permute-done.2.refs_7_) | copy-start | bytes 442372
  47.7 42.2 %copy-start.7 = (bf16[4,72,256]{2,1,0:T(8,128)(2,1)}, bf16[4,72,256]{2,1,0:T(8,128)(2,1)S(1)}, u32[]{:S(2)}) copy-start(bf16[4,72,256]{2,1,0:T(8,128)(2,1)S(1)} %collective-permute-done.3.refs_9_) | copy-start | bytes 442372
  48.4 41.5 %copy-start.8 = (bf16[4,72,256]{2,1,0:T(8,128)(2,1)}, bf16[4,72,256]{2,1,0:T(8,128)(2,1)S(1)}, u32[]{:S(2)}) copy-start(bf16[4,72,256]{2,1,0:T(8,128)(2,1)S(1)} %collective-permute-done.4.refs_10_) | copy-start | bytes 442372
  59.4 30.5 %copy-start.9 = (bf16[4,72,256]{2,1,0:T(8,128)(2,1)}, bf16[4,72,256]{2,1,0:T(8,128)(2,1)S(1)}, u32[]{:S(2)}) copy-start(bf16[4,72,256]{2,1,0:T(8,128)(2,1)S(1)} %collective-permute-done.5.refs_11_) | copy-start | bytes 442372
  59.5 19.0 %collective-permute-start.7 = (bf16[28,12,256]{2,1,0:T(8,128)(2,1)S(1)}, bf16[28,12,256]{2,1,0:T(8,128)(2,1)S(1)}, u32[]{:S(2)}, u32[]{:S(2)}) collective-permute-start(bf16[28,12,256]{2,1,0:T(8,128)(2,1)S(1)} %get-tuple-element.14), channel_id=1, source_target_pairs={{0,1},{1,0},{2,3},{3,2},{4,5},{5,4},{6,7},{7,6},{8,9},{9,8},{10,11... | collective-permute-start | bytes 516104 | tf_op jit(solution)/shard_map/ppermute | solution.py:54
  67.9 21.9 %collective-permute-start.8 = (bf16[28,12,256]{2,1,0:T(8,128)(2,1)S(1)}, bf16[28,12,256]{2,1,0:T(8,128)(2,1)S(1)}, u32[]{:S(2)}, u32[]{:S(2)}) collective-permute-start(bf16[28,12,256]{2,1,0:T(8,128)(2,1)S(1)} %get-tuple-element.15), channel_id=1, source_target_pairs={{1,2},{2,1},{3,4},{4,3},{5,6},{6,5},{7,0},{0,7},{9,10},{10,9},{11,... | collective-permute-start | bytes 516104 | tf_op jit(solution)/shard_map/ppermute | solution.py:54
  95.8 12.5 %collective-permute-start.9 = (bf16[128,2304]{1,0:T(8,128)(2,1)}, bf16[128,2304]{1,0:T(8,128)(2,1)S(1)}, u32[]{:S(2)}, u32[]{:S(2)}) collective-permute-start(bf16[128,2304]{1,0:T(8,128)(2,1)} %get-tuple-element.18), channel_id=1, source_target_pairs={{0,1},{1,0},{2,3},{3,2},{4,5},{5,4},{6,7},{7,6},{8,9},{9,8},{10,11... | collective-permute-start | bytes 1769480 | tf_op jit(solution)/shard_map/ppermute | solution.py:36
  99.6 22.4 %collective-permute-start.10 = (bf16[64,2304]{1,0:T(8,128)(2,1)S(1)}, bf16[64,2304]{1,0:T(8,128)(2,1)S(1)}, u32[]{:S(2)}, u32[]{:S(2)}) collective-permute-start(bf16[64,2304]{1,0:T(8,128)(2,1)S(1)} %bitcast.33), channel_id=1, source_target_pairs={{0,512},{8,520},{16,528},{24,536},{32,544},{40,552},{48,560},{56,5... | collective-permute-start | bytes 884744 | tf_op jit(solution)/shard_map/ppermute | solution.py:66
  110.3 13.5 %all-to-all-start.2 = ((bf16[4,32,2304]{2,1,0:T(8,128)(2,1)}), bf16[4,32,2304]{2,1,0:T(8,128)(2,1)S(1)}, u32[]{:S(2)}, u32[]{:S(2)}) async-start(bf16[4,32,2304]{2,1,0:T(8,128)(2,1)} %bitcast.14), calls=%async_computation.2 | async-start | bytes 1179648 | tf_op jit(solution)/shard_map/all_to_all | solution.py:228
  122.0 33.1 %copy-start.1 = (bf16[128,2304]{1,0:T(8,128)(2,1)}, bf16[128,2304]{1,0:T(8,128)(2,1)S(1)}, u32[]{:S(2)}) copy-start(bf16[128,2304]{1,0:T(8,128)(2,1)S(1)} %pad_maximum_fusion.1.refs_1_) | copy-start | bytes 1769476
  132.6 10.6 %all-to-all-start.4 = ((f32[8,1,2304]{2,1,0:T(1,128)}), f32[8,1,2304]{2,1,0:T(1,128)S(1)}, u32[]{:S(2)}, u32[]{:S(2)}) async-start(f32[8,1,2304]{2,1,0:T(1,128)} %copy.43), calls=%async_computation.4 | async-start | bytes 147456 | tf_op jit(solution)/shard_map/all_to_all | solution.py:228
  135.9 19.2 %collective-permute-start.11 = (bf16[128,2304]{1,0:T(8,128)(2,1)S(1)}, bf16[128,2304]{1,0:T(8,128)(2,1)S(1)}, u32[]{:S(2)}, u32[]{:S(2)}) collective-permute-start(bf16[128,2304]{1,0:T(8,128)(2,1)S(1)} %pad_maximum_fusion.1.refs_1_), channel_id=1, source_target_pairs={{0,1},{1,0},{2,3},{3,2},{4,5},{5,4},{6,7},{7,6},{8,9},{9,8},{10,11... | collective-permute-start | bytes 1769480 | tf_op jit(solution)/shard_map/ppermute | solution.py:36
  143.9 22.6 %all-to-all-start.5 = ((f32[8,1,2304]{2,1,0:T(1,128)}), f32[8,1,2304]{2,1,0:T(1,128)S(1)}, u32[]{:S(2)}, u32[]{:S(2)}) async-start(f32[8,1,2304]{2,1,0:T(1,128)} %broadcast_in_dim.31), calls=%async_computation.5 | async-start | bytes 147456 | tf_op jit(solution)/shard_map/all_to_all | solution.py:242
  (6 other events, 40.2 us)

commit v4 on v2

--- a/solution.py
+++ b/solution.py
@@ -7,9 +7,8 @@
 from jax.experimental.pallas import tpu as pltpu
 from jax.sharding import PartitionSpec as P
 
-FACTORS = {128: (4, 4, 8), 8: (2, 2, 2)}
+FACTORS = {128: (4, 4, 8), 16: (2, 2, 4)}
 TILE = 8
-MASKS = {128: (8, 16, 32, 64, 1, 2, 7), 8: (2, 4, 1)}
 
 
 def dot(a, b, contract):
@@ -31,10 +30,6 @@
         fixed = tuple(coords[d] for d in range(3) if d not in dims)
         members.setdefault(fixed, []).append(index)
     return [members[fixed] for fixed in sorted(members)]
-
-
-def swapped_lat(block, bit):
-    return lax.ppermute(block, "lat", [(i, i ^ bit) for i in range(lax.axis_size("lat"))])
 
 
 def swapped_core(block):
@@ -52,6 +47,12 @@
             high = 0
         pairs += [(low, high), (high, low)]
     return lax.ppermute(block, axis, pairs)
+
+
+def spread_over(block, dim, factors):
+    copies = jnp.broadcast_to(block, (factors[dim],) + block.shape)
+    joined = lax.all_to_all(copies, "lat", 0, 0, axis_index_groups=groups((dim,), factors))
+    return joined.reshape(-1, block.shape[1])
 
 
 def band_kernel(rows_ref, band_ref):
@@ -127,44 +128,7 @@
     cells = rows * cols
     bf16 = jnp.bfloat16
 
-    masks = MASKS[lax.axis_size("lat")]
-    owners = [0]
-    for mask in masks:
-        owners = owners + [owner ^ mask for owner in owners]
-
-    def doubled(block, turn):
-        if turn >= len(masks):
-            return block
-        return jnp.concatenate([block, swapped_lat(block, masks[turn])], axis=0)
-
-    gathered = doubled(lax.dynamic_slice_in_dim(weight, core, 1, 0), 0)
-
-    edges = jnp.where(core == 0, fields[:, cols - reach :], fields[:, :reach])
-    other_edges = jnp.where(core == 0, fields[:, :reach], fields[:, cols - reach :])
-    near_edge = paired(edges, "lon", 0, True)
-    far_edge = paired(other_edges, "lon", 1, True)
-    left = jnp.where(core == 0, far_edge, near_edge)
-    right = jnp.where(core == 0, near_edge, far_edge)
-    own = jnp.concatenate([left, fields, right], axis=1)
-    near, far = own, own
-    nears, fars = [], []
-    for turn in range(3):
-        near, far, gathered = lax.optimization_barrier((near, far, gathered))
-        near, far = paired(far, "lat", 0, False), paired(near, "lat", 1, False)
-        gathered = doubled(gathered, turn + 1)
-        nears.append(near)
-        fars.append(far)
-    windows = nears[::-1] + [own] + fars
-
-    near, gathered = lax.optimization_barrier((near, gathered))
-    nears[-1] = near
-    for turn in range(4, len(masks)):
-        gathered = doubled(gathered, turn)
-    other_weight = swapped_core(gathered)
-    position = jnp.arange(outs)
-    half = outs // 2
-    weight_row = 2 * (lat ^ jnp.array(owners + owners, jnp.int32)) + (core ^ (position // half))
-    weight_order = (weight_row[:, None] == jnp.arange(outs)[None, :]).astype(bf16)
+    gathered = spread_over(lax.dynamic_slice_in_dim(weight, core, 1, 0), 1, factors)
 
     offsets = jnp.arange(width) - reach
     validity = jnp.abs(offsets)[None, None, :] <= spans[:, :, None]
@@ -187,6 +151,8 @@
     )(band_rows)
 
     zs, xs, ys = factors
+    position = jnp.arange(outs)
+    half = outs // 2
     away = (
         2
         * lat_index(
@@ -197,6 +163,23 @@
     cot_order = (away[:, None] == jnp.arange(outs)[None, :]).astype(bf16)
     cot_cells = jnp.transpose(cotangent.reshape(rows, tile_count, TILE, outs), (1, 0, 2, 3))
     cot = dot(cot_order, cot_cells.reshape(cells, outs), ((1,), (1,))).astype(bf16)
+
+    low, high = fields[:, :reach], fields[:, cols - reach :]
+    near_edge = paired(jnp.where(core == 0, high, low), "lon", 0, True)
+    far_edge = paired(jnp.where(core == 0, low, high), "lon", 1, True)
+    left = jnp.where(core == 0, far_edge, near_edge)
+    right = jnp.where(core == 0, near_edge, far_edge)
+    own = jnp.concatenate([left, fields, right], axis=1)
+    own, gathered = lax.optimization_barrier((own, gathered))
+    near, far = own, own
+    nears, fars = [], []
+    for turn in range(3):
+        if turn == 2:
+            near, far, band, cot = lax.optimization_barrier((near, far, band, cot))
+        near, far = paired(far, "lat", 0, False), paired(near, "lat", 1, False)
+        nears.append(near)
+        fars.append(far)
+    windows = nears[::-1] + [own] + fars
 
     features, keep, send = pl.pallas_call(
         lambda *refs: feature_kernel(nbasis, tile_count, *refs),
@@ -210,26 +193,56 @@
         name="features",
     )(band, cot, *windows)
 
+    f32 = jnp.float32
+    length = nbasis * channels
+
+    def exchanged(block, dim):
+        block = block.reshape(factors[dim], -1, block.shape[-1])
+        return lax.all_to_all(block, "lat", 0, 0, axis_index_groups=groups((dim,), factors))
+
+    total = (keep.astype(f32) + swapped_core(send).astype(f32)).astype(bf16)
+    total = jnp.sum(exchanged(total, 1).astype(f32), axis=0).astype(bf16)
+
+    total = total.reshape(zs, ys, length)
+    folded = jnp.concatenate([gathered[:, : length // 2], gathered[:, length // 2 :]], axis=0)
+    folded = jnp.pad(folded, ((0, ys - folded.shape[0]), (0, 0)))
+    folded = jnp.broadcast_to(folded, (zs,) + folded.shape)
+    arrived = exchanged(jnp.concatenate([total, folded], axis=2), 0)
+    total = jnp.sum(arrived[:, :, :length].astype(f32), axis=0).astype(bf16)
+    gathered = jnp.concatenate(
+        [arrived[:, :xs, length:], arrived[:, xs : 2 * xs, length:]], axis=2
+    ).reshape(zs * xs, length)
+
+    piece = zs * xs
+    column = -(-length // piece // 128) * 128
+    folded = jnp.pad(total, ((0, 0), (0, piece * column - length))).reshape(ys, piece, column)
+    whole = jnp.broadcast_to(gathered, (ys,) + gathered.shape)
+    arrived = exchanged(jnp.concatenate([whole, folded], axis=2), 2)
+    gathered = arrived.reshape(ys * piece, length + column)
+    total = jnp.sum(arrived[:, :, length:].astype(f32), axis=0).reshape(1, -1)[:, :length]
+
+    other_weight = swapped_core(gathered[:, :length])
+    place = position % half
+    weight_row = 2 * lat_index(place // xs % zs, place % xs, place // piece, factors)
+    weight_row = weight_row + (core ^ (position // half))
+    weight_order = (weight_row[:, None] == jnp.arange(outs)[None, :]).astype(bf16)
+
     output = pl.pallas_call(
         lambda *refs: output_kernel(tile_count, *refs),
         out_shape=jax.ShapeDtypeStruct((rows, cols, outs), bf16),
         in_specs=vmem(4),
         out_specs=pl.BlockSpec(memory_space=pltpu.VMEM),
+        cost_estimate=pl.CostEstimate(
+            flops=2 * cells * outs * (length + outs), bytes_accessed=8 * cells * length, transcendentals=0
+        ),
         name="mixing",
     )(features, gathered, other_weight, weight_order)
 
-    f32 = jnp.float32
-    total = keep.astype(f32) + swapped_core(send).astype(f32)
-    for dim in (1, 0, 2):
-        count = factors[dim]
-        moved = total if dim == 2 else total.astype(bf16)
-        moved = moved.reshape(count, -1, moved.shape[1])
-        arrived = lax.all_to_all(moved, "lat", 0, 0, axis_index_groups=groups((dim,), factors))
-        total = jnp.sum(arrived.astype(f32), axis=0)
     scale = 1.0 / math.sqrt(rows * lax.axis_size("lat") * cols * lax.axis_size("lon"))
     lon_size = lax.axis_size("lon")
     spread = jnp.broadcast_to(total * scale, (lon_size,) + total.shape)
     arrived = lax.all_to_all(spread, "lon", 0, 0)
+    arrived, output = lax.optimization_barrier((arrived, output))
     grad_weight = jnp.sum(arrived.reshape(lon_size // 2, 2, nbasis * channels), axis=0)
     return (output, grad_weight)
 

time: 158 us -> 159 us (level)
  blocking collectives: 0 us -> 34.5 us
  starting transfers between devices: 95.5 us -> 71 us
  waiting for transfers between devices: 36.7 us -> 27.3 us
    all_to_all x0 -> x2, blocking collectives: none -> 34.5 us  [exchanged(): lax.all_to_all(block, 'lat', 0, 0, axis_index_groups=groups((dim,), facto...]
    ppermute x7 -> x0, starting transfers between devices: 34.2 us -> none  [swapped_lat(): lax.ppermute(block, 'lat', [(i, i ^ bit) for i in range(lax.axis_size('la...]
    ppermute x7 -> x0, waiting for transfers between devices: 9.56 us -> none  [swapped_lat(): lax.ppermute(block, 'lat', [(i, i ^ bit) for i in range(lax.axis_size('la...]
    all_to_all x3 -> x2, starting transfers between devices: 10.2 us -> 14.6 us  [the longest x1 10.6 us: exchanged(): lax.all_to_all(block, 'lat', 0, 0, axis_index_groups=groups((dim,), facto...]
    ppermute x2, starting transfers between devices: 9.53 us -> 12.1 us  [swapped_core(): lax.ppermute(block, 'lon', [(i, i ^ 1) for i in range(lax.axis_size('lon'...]
    ppermute x8, waiting for transfers between devices: 7.62 us -> 5.21 us  [paired(): return lax.ppermute(block, axis, pairs)]
    ppermute x8, starting transfers between devices: 34.7 us -> 36.9 us  [paired(): return lax.ppermute(block, axis, pairs)]
    ppermute x2, waiting for transfers between devices: 0.01 us -> 1.82 us  [swapped_core(): lax.ppermute(block, 'lon', [(i, i ^ 1) for i in range(lax.axis_size('lon'...]
  transfers between devices with their start and end apart: 21 -> 13, of which waited for: 6 -> 6; matrix products, arithmetic and copies ran while one was open for 6% -> 5% of each run, Pallas kernels for 6% -> 3%
where the time goes in v4:
time: 159 us; the launch traced here: 158 us
  starting transfers between devices  71 us (45%)
  blocking collectives  34.5 us (22%)
  waiting for transfers between devices  27.3 us (17%)
  Pallas kernels  10.1 us (6%)
  other arithmetic  7.35 us (5%)
  local copies, waits for them, and re-layouts  5.4 us (3%)
    ppermute x8, starting transfers between devices, paired(): return lax.ppermute(block, axis, pairs)  36.9 us
    all_to_all x2, blocking collectives, exchanged(): lax.all_to_all(block, 'lat', 0, 0, axis_index_groups=groups((dim,), facto...  34.5 us
    ppermute x2, starting transfers between devices, swapped_core(): lax.ppermute(block, 'lon', [(i, i ^ 1) for i in range(lax.axis_size('lon'...  12.1 us
    all_to_all x1, starting transfers between devices, exchanged(): lax.all_to_all(block, 'lat', 0, 0, axis_index_groups=groups((dim,), facto...  10.6 us
    all_to_all x1, waiting for transfers between devices, exchanged(): lax.all_to_all(block, 'lat', 0, 0, axis_index_groups=groups((dim,), facto...  9.57 us
    all_to_all x1, waiting for transfers between devices, shards(): arrived = lax.all_to_all(spread, 'lon', 0, 0)  8.73 us
    all_to_all x1, starting transfers between devices, shards(): arrived = lax.all_to_all(spread, 'lon', 0, 0)  7.42 us
    ppermute x8, waiting for transfers between devices, paired(): return lax.ppermute(block, axis, pairs)  5.21 us
  transfers between devices with their start and end apart: 13, of which 6 were waited for; matrix products, arithmetic and copies ran while one was open for 5% of the time, Pallas kernels for 3%

profile of v4, /device:TPU:1, one launch (start us, length us, event | category | flops | bytes accessed | tf_op | source)
XLA Modules:
  0.0 157.6 jit_solution(1394949295454500746)
XLA Ops:
  1.5 12.0 %collective-permute-start = (bf16[4,12,256]{2,1,0:T(8,128)(2,1)S(1)}, bf16[4,12,256]{2,1,0:T(8,128)(2,1)S(1)}, u32[]{:S(2)}, u32[]{:S(2)}) collective-permute-start(bf16[4,12,256]{2,1,0:T(8,128)(2,1)S(1)} %get-tuple-element.30), channel_id=1, source_target_pairs={{1,2},{2,1},{3,4},{4,3},{5,6},{6,5},{7,0},{0,7},{9,10},{10,9},{11,... | collective-permute-start | bytes 73736 | tf_op jit(solution)/shard_map/ppermute | solution.py:49
  13.5 9.0 %collective-permute-start.1 = (bf16[4,12,256]{2,1,0:T(8,128)(2,1)S(1)}, bf16[4,12,256]{2,1,0:T(8,128)(2,1)S(1)}, u32[]{:S(2)}, u32[]{:S(2)}) collective-permute-start(bf16[4,12,256]{2,1,0:T(8,128)(2,1)S(1)} %get-tuple-element.31), channel_id=1, source_target_pairs={{0,1},{1,0},{2,3},{3,2},{4,5},{5,4},{6,7},{7,6},{8,9},{9,8},{10,11... | collective-permute-start | bytes 73736 | tf_op jit(solution)/shard_map/ppermute | solution.py:49
  24.5 4.0 %all-to-all-start = ((bf16[4,2,1152]{2,1,0:T(2,128)(2,1)}), bf16[4,2,1152]{2,1,0:T(2,128)(2,1)S(1)}, u32[]{:S(2)}, u32[]{:S(2)}) async-start(bf16[4,2,1152]{2,1,0:T(2,128)(2,1)} %reshape.192), calls=%async_computation | async-start | bytes 36864 | tf_op jit(solution)/shard_map/all_to_all | solution.py:54
  29.3 1.0 convert_bitcast_fusion
  30.8 1.9 %all-to-all-done = bf16[4,2,1152]{2,1,0:T(2,128)(2,1)S(1)} async-done(((bf16[4,2,1152]{2,1,0:T(2,128)(2,1)}), bf16[4,2,1152]{2,1,0:T(2,128)(2,1)S(1)}, u32[]{:S(2)}, u32[]{:S(2)}) %all-to-all-start) | async-done | bytes 18464 | tf_op jit(solution)/shard_map/all_to_all | solution.py:54
  33.6 5.7 %collective-permute-start.4 = (bf16[4,96,256]{2,1,0:T(8,128)(2,1)S(1)}, bf16[4,96,256]{2,1,0:T(8,128)(2,1)S(1)}, u32[]{:S(2)}, u32[]{:S(2)}) collective-permute-start(bf16[4,96,256]{2,1,0:T(8,128)(2,1)S(1)} %pad_maximum_fusion.3.refs_5_), channel_id=1, source_target_pairs={{0,8},{8,0},{16,24},{24,16},{32,40},{40,32},{48,56},{56,48},{64,72... | collective-permute-start | bytes 589832 | tf_op jit(solution)/shard_map/ppermute | solution.py:49
  40.1 1.9 %shard_map.68.refs_0_ = bf16[288,896]{1,0:T(8,128)(2,1)} custom-call(f32[36,896]{1,0:T(8,128)} %bitcast.44), custom_call_target="tpu_custom_call" | custom-call | tf_op jit(solution)/shard_map/pallas_call | solution.py:146
  42.0 1.9 %collective-permute-start.3 = (bf16[4,96,256]{2,1,0:T(8,128)(2,1)S(1)}, bf16[4,96,256]{2,1,0:T(8,128)(2,1)S(1)}, u32[]{:S(2)}, u32[]{:S(2)}) collective-permute-start(bf16[4,96,256]{2,1,0:T(8,128)(2,1)S(1)} %collective-permute-done.2.refs_6_), channel_id=1, source_target_pairs={{0,8},{8,0},{16,24},{24,16},{32,40},{40,32},{48,56},{56,48},{64,72... | collective-permute-start | bytes 589832 | tf_op jit(solution)/shard_map/ppermute | solution.py:49
  44.7 1.0 convolution_convert_fusion.refs_1_
  45.6 2.8 %collective-permute-done.3.refs_3_ = bf16[4,96,256]{2,1,0:T(8,128)(2,1)S(1)} collective-permute-done((bf16[4,96,256]{2,1,0:T(8,128)(2,1)S(1)}, bf16[4,96,256]{2,1,0:T(8,128)(2,1)S(1)}, u32[]{:S(2)}, u32[]{:S(2)}) %collective-permute-start.3) | collective-permute-done | bytes 196640 | tf_op jit(solution)/shard_map/ppermute | solution.py:49
  48.5 6.2 %collective-permute-start.6 = (bf16[4,96,256]{2,1,0:T(8,128)(2,1)S(1)}, bf16[4,96,256]{2,1,0:T(8,128)(2,1)S(1)}, u32[]{:S(2)}, u32[]{:S(2)}) collective-permute-start(bf16[4,96,256]{2,1,0:T(8,128)(2,1)S(1)} %collective-permute-done.5.refs_7_), channel_id=1, source_target_pairs={{0,8},{8,0},{16,24},{24,16},{32,40},{40,32},{48,56},{56,48},{64,72... | collective-permute-start | bytes 589832 | tf_op jit(solution)/shard_map/ppermute | solution.py:49
  55.3 2.4 %collective-permute-done.6.refs_2_ = bf16[4,96,256]{2,1,0:T(8,128)(2,1)S(1)} collective-permute-done((bf16[4,96,256]{2,1,0:T(8,128)(2,1)S(1)}, bf16[4,96,256]{2,1,0:T(8,128)(2,1)S(1)}, u32[]{:S(2)}, u32[]{:S(2)}) %collective-permute-start.6) | collective-permute-done | bytes 196640 | tf_op jit(solution)/shard_map/ppermute | solution.py:49
  59.1 5.1 %features.1 = (bf16[9,288,256]{2,1,0:T(8,128)(2,1)}, bf16[128,2304]{1,0:T(8,128)(2,1)}, bf16[128,2304]{1,0:T(8,128)(2,1)}) custom-call(bf16[288,896]{1,0:T(8,128)(2,1)} %shard_map.68.refs_0_, bf16[256,288]{1,0:T(8,128)(2,1)} %convolution_convert_fusion.refs_1_, bf16[4,96,256]{2,1,0:T(8,128)(2,1)} %copy-done.9, bf16[4,96,256]{2,1,0:T(8,128)(2,1)} %copy-done.7, ...), custom_call_target="tpu_custom_call" | custom-call | tf_op jit(solution)/shard_map/features/pallas_call | solution.py:184
  64.2 5.6 %collective-permute-start.8 = (bf16[128,2304]{1,0:T(8,128)(2,1)}, bf16[128,2304]{1,0:T(8,128)(2,1)S(1)}, u32[]{:S(2)}, u32[]{:S(2)}) collective-permute-start(bf16[128,2304]{1,0:T(8,128)(2,1)} %get-tuple-element.19), channel_id=1, source_target_pairs={{0,1},{1,0},{2,3},{3,2},{4,5},{5,4},{6,7},{7,6},{8,9},{9,8},{10,11... | collective-permute-start | bytes 1769480 | tf_op jit(solution)/shard_map/ppermute | solution.py:36
  69.9 1.8 %collective-permute-done.8 = bf16[128,2304]{1,0:T(8,128)(2,1)S(1)} collective-permute-done((bf16[128,2304]{1,0:T(8,128)(2,1)}, bf16[128,2304]{1,0:T(8,128)(2,1)S(1)}, u32[]{:S(2)}, u32[]{:S(2)}) %collective-permute-start.8) | collective-permute-done | bytes 589856 | tf_op jit(solution)/shard_map/ppermute | solution.py:36
  71.7 2.0 %add_convert_fusion = bf16[128,2304]{1,0:T(8,128)(2,1)} fusion(bf16[128,2304]{1,0:T(8,128)(2,1)S(1)} %collective-permute-done.8, bf16[128,2304]{1,0:T(8,128)(2,1)} %get-tuple-element.18), kind=kLoop, calls=%fused_computation | loop fusion | flops 1179648 | bytes 1769472 | tf_op jit(solution)/shard_map/convert_element_type | solution.py:203
  73.7 10.6 %all-to-all-start.1 = ((bf16[4,32,2304]{2,1,0:T(8,128)(2,1)}), bf16[4,32,2304]{2,1,0:T(8,128)(2,1)S(1)}, u32[]{:S(2)}, u32[]{:S(2)}) async-start(bf16[4,32,2304]{2,1,0:T(8,128)(2,1)} %bitcast.12), calls=%async_computation.1 | async-start | bytes 1179648 | tf_op jit(solution)/shard_map/all_to_all | solution.py:201
  84.3 9.6 %all-to-all-done.1 = bf16[4,32,2304]{2,1,0:T(8,128)(2,1)S(1)} async-done(((bf16[4,32,2304]{2,1,0:T(8,128)(2,1)}), bf16[4,32,2304]{2,1,0:T(8,128)(2,1)S(1)}, u32[]{:S(2)}, u32[]{:S(2)}) %all-to-all-start.1) | async-done | bytes 589856 | tf_op jit(solution)/shard_map/all_to_all | solution.py:201
  94.0 15.4 %all_to_all.25 = bf16[4,8,3456]{2,1,0:T(8,128)(2,1)S(1)} all-to-all(bf16[4,8,3456]{2,1,0:T(8,128)(2,1)S(1)} %pad_maximum_fusion.2), channel_id=1, replica_groups={{0,256,512,768},{8,264,520,776},{16,272,528,784},{24,280,536,792},{32,2..., dimensions={0} | all-to-all | bytes 442368 | tf_op jit(solution)/shard_map/all_to_all | solution.py:201
  109.6 19.1 %all_to_all.26 = bf16[8,16,2560]{2,1,0:T(8,128)(2,1)S(1)} all-to-all(bf16[8,16,2560]{2,1,0:T(8,128)(2,1)S(1)} %pad_maximum_fusion), channel_id=1, replica_groups={{0,8,16,24,32,40,48,56},{64,72,80,88,96,104,112,120},{128,136,144,152,1..., dimensions={0} | all-to-all | bytes 1310720 | tf_op jit(solution)/shard_map/all_to_all | solution.py:201
  128.8 6.4 %collective-permute-start.9 = (bf16[128,2304]{1,0:T(8,128)(2,1)S(1)}, bf16[128,2304]{1,0:T(8,128)(2,1)S(1)}, u32[]{:S(2)}, u32[]{:S(2)}) collective-permute-start(bf16[128,2304]{1,0:T(8,128)(2,1)S(1)} %slice.65), channel_id=1, source_target_pairs={{0,1},{1,0},{2,3},{3,2},{4,5},{5,4},{6,7},{7,6},{8,9},{9,8},{10,11... | collective-permute-start | bytes 1769480 | tf_op jit(solution)/shard_map/ppermute | solution.py:36
  136.0 7.4 %all-to-all-start.4 = ((f32[8,1,2304]{2,1,0:T(1,128)}), f32[8,1,2304]{2,1,0:T(1,128)S(1)}, u32[]{:S(2)}, u32[]{:S(2)}) async-start(f32[8,1,2304]{2,1,0:T(1,128)} %broadcast_in_dim.35), calls=%async_computation.4 | async-start | bytes 147456 | tf_op jit(solution)/shard_map/all_to_all | solution.py:244
  145.0 3.0 %mixing.1 = bf16[4,72,256]{2,1,0:T(8,128)(2,1)} custom-call(bf16[9,288,256]{2,1,0:T(8,128)(2,1)} %get-tuple-element.21.refs_0_, bf16[128,2560]{1,0:T(8,128)(2,1)} %bitcast.40, bf16[128,2304]{1,0:T(8,128)(2,1)} %copy-done.3, bf16[256,256]{1,0:T(8,128)(2,1)} %fusion.refs_3_), custom_call_target="tpu_custom_call" | custom-call | flops 377487360 | bytes 5308416 | tf_op jit(solution)/shard_map/mixing/pallas_call | solution.py:230
  148.0 8.7 %all-to-all-done.4 = f32[8,1,2304]{2,1,0:T(1,128)S(1)} async-done(((f32[8,1,2304]{2,1,0:T(1,128)}), f32[8,1,2304]{2,1,0:T(1,128)S(1)}, u32[]{:S(2)}, u32[]{:S(2)}) %all-to-all-start.4) | async-done | bytes 73760 | tf_op jit(solution)/shard_map/all_to_all | solution.py:244
  (81 shorter events, 11.8 us)
Async XLA Ops:
  0.6 21.9 %copy-start = (bf16[2,2304]{1,0:T(2,128)(2,1)S(1)}, bf16[2,2304]{1,0:T(2,128)(2,1)}, u32[]{:S(2)}) copy-start(bf16[2,2304]{1,0:T(2,128)(2,1)} %param.8) | copy-start | bytes 27652
  1.5 31.3 %collective-permute-start = (bf16[4,12,256]{2,1,0:T(8,128)(2,1)S(1)}, bf16[4,12,256]{2,1,0:T(8,128)(2,1)S(1)}, u32[]{:S(2)}, u32[]{:S(2)}) collective-permute-start(bf16[4,12,256]{2,1,0:T(8,128)(2,1)S(1)} %get-tuple-element.30), channel_id=1, source_target_pairs={{1,2},{2,1},{3,4},{4,3},{5,6},{6,5},{7,0},{0,7},{9,10},{10,9},{11,... | collective-permute-start | bytes 73736 | tf_op jit(solution)/shard_map/ppermute | solution.py:49
  13.5 19.3 %collective-permute-start.1 = (bf16[4,12,256]{2,1,0:T(8,128)(2,1)S(1)}, bf16[4,12,256]{2,1,0:T(8,128)(2,1)S(1)}, u32[]{:S(2)}, u32[]{:S(2)}) collective-permute-start(bf16[4,12,256]{2,1,0:T(8,128)(2,1)S(1)} %get-tuple-element.31), channel_id=1, source_target_pairs={{0,1},{1,0},{2,3},{3,2},{4,5},{5,4},{6,7},{7,6},{8,9},{9,8},{10,11... | collective-permute-start | bytes 73736 | tf_op jit(solution)/shard_map/ppermute | solution.py:49
  24.5 8.2 %all-to-all-start = ((bf16[4,2,1152]{2,1,0:T(2,128)(2,1)}), bf16[4,2,1152]{2,1,0:T(2,128)(2,1)S(1)}, u32[]{:S(2)}, u32[]{:S(2)}) async-start(bf16[4,2,1152]{2,1,0:T(2,128)(2,1)} %reshape.192), calls=%async_computation | async-start | bytes 36864 | tf_op jit(solution)/shard_map/all_to_all | solution.py:54
  30.5 2.3 %copy-start.4 = (bf16[4,72,256]{2,1,0:T(8,128)(2,1)S(1)}, bf16[4,72,256]{2,1,0:T(8,128)(2,1)}, u32[]{:S(2)}) copy-start(bf16[4,72,256]{2,1,0:T(8,128)(2,1)} %param.5) | copy-start | bytes 442372
  30.7 11.2 %copy-start.11 = (bf16[4,72,256]{2,1,0:T(8,128)(2,1)S(1)}, bf16[4,72,256]{2,1,0:T(8,128)(2,1)}, u32[]{:S(2)}) copy-start(bf16[4,72,256]{2,1,0:T(8,128)(2,1)} %param.9) | copy-start | bytes 442372
  32.9 24.8 %copy-start.2 = (bf16[4,96,256]{2,1,0:T(8,128)(2,1)}, bf16[4,96,256]{2,1,0:T(8,128)(2,1)S(1)}, u32[]{:S(2)}) copy-start(bf16[4,96,256]{2,1,0:T(8,128)(2,1)S(1)} %pad_maximum_fusion.3.refs_5_) | copy-start | bytes 589828
  32.9 9.1 %collective-permute-start.2 = (bf16[4,96,256]{2,1,0:T(8,128)(2,1)S(1)}, bf16[4,96,256]{2,1,0:T(8,128)(2,1)S(1)}, u32[]{:S(2)}, u32[]{:S(2)}) collective-permute-start(bf16[4,96,256]{2,1,0:T(8,128)(2,1)S(1)} %pad_maximum_fusion.3.refs_5_), channel_id=1, source_target_pairs={{8,16},{16,8},{24,32},{32,24},{40,48},{48,40},{56,64},{64,56},{72,... | collective-permute-start | bytes 589832 | tf_op jit(solution)/shard_map/ppermute | solution.py:49
  33.6 10.4 %collective-permute-start.4 = (bf16[4,96,256]{2,1,0:T(8,128)(2,1)S(1)}, bf16[4,96,256]{2,1,0:T(8,128)(2,1)S(1)}, u32[]{:S(2)}, u32[]{:S(2)}) collective-permute-start(bf16[4,96,256]{2,1,0:T(8,128)(2,1)S(1)} %pad_maximum_fusion.3.refs_5_), channel_id=1, source_target_pairs={{0,8},{8,0},{16,24},{24,16},{32,40},{40,32},{48,56},{56,48},{64,72... | collective-permute-start | bytes 589832 | tf_op jit(solution)/shard_map/ppermute | solution.py:49
  42.0 15.7 %copy-start.5 = (bf16[4,96,256]{2,1,0:T(8,128)(2,1)}, bf16[4,96,256]{2,1,0:T(8,128)(2,1)S(1)}, u32[]{:S(2)}) copy-start(bf16[4,96,256]{2,1,0:T(8,128)(2,1)S(1)} %collective-permute-done.2.refs_6_) | copy-start | bytes 589828
  42.0 6.4 %collective-permute-start.3 = (bf16[4,96,256]{2,1,0:T(8,128)(2,1)S(1)}, bf16[4,96,256]{2,1,0:T(8,128)(2,1)S(1)}, u32[]{:S(2)}, u32[]{:S(2)}) collective-permute-start(bf16[4,96,256]{2,1,0:T(8,128)(2,1)S(1)} %collective-permute-done.2.refs_6_), channel_id=1, source_target_pairs={{0,8},{8,0},{16,24},{24,16},{32,40},{40,32},{48,56},{56,48},{64,72... | collective-permute-start | bytes 589832 | tf_op jit(solution)/shard_map/ppermute | solution.py:49
  44.0 13.7 %copy-start.6 = (bf16[4,96,256]{2,1,0:T(8,128)(2,1)}, bf16[4,96,256]{2,1,0:T(8,128)(2,1)S(1)}, u32[]{:S(2)}) copy-start(bf16[4,96,256]{2,1,0:T(8,128)(2,1)S(1)} %collective-permute-done.4.refs_4_) | copy-start | bytes 589828
  44.0 4.5 %collective-permute-start.5 = (bf16[4,96,256]{2,1,0:T(8,128)(2,1)S(1)}, bf16[4,96,256]{2,1,0:T(8,128)(2,1)S(1)}, u32[]{:S(2)}, u32[]{:S(2)}) collective-permute-start(bf16[4,96,256]{2,1,0:T(8,128)(2,1)S(1)} %collective-permute-done.4.refs_4_), channel_id=1, source_target_pairs={{8,16},{16,8},{24,32},{32,24},{40,48},{48,40},{56,64},{64,56},{72,... | collective-permute-start | bytes 589832 | tf_op jit(solution)/shard_map/ppermute | solution.py:49
  48.4 9.3 %copy-start.7 = (bf16[4,96,256]{2,1,0:T(8,128)(2,1)}, bf16[4,96,256]{2,1,0:T(8,128)(2,1)S(1)}, u32[]{:S(2)}) copy-start(bf16[4,96,256]{2,1,0:T(8,128)(2,1)S(1)} %collective-permute-done.3.refs_3_) | copy-start | bytes 589828
  48.4 9.3 %copy-start.8 = (bf16[4,96,256]{2,1,0:T(8,128)(2,1)}, bf16[4,96,256]{2,1,0:T(8,128)(2,1)S(1)}, u32[]{:S(2)}) copy-start(bf16[4,96,256]{2,1,0:T(8,128)(2,1)S(1)} %collective-permute-done.5.refs_7_) | copy-start | bytes 589828
  48.5 9.2 %collective-permute-start.6 = (bf16[4,96,256]{2,1,0:T(8,128)(2,1)S(1)}, bf16[4,96,256]{2,1,0:T(8,128)(2,1)S(1)}, u32[]{:S(2)}, u32[]{:S(2)}) collective-permute-start(bf16[4,96,256]{2,1,0:T(8,128)(2,1)S(1)} %collective-permute-done.5.refs_7_), channel_id=1, source_target_pairs={{0,8},{8,0},{16,24},{24,16},{32,40},{40,32},{48,56},{56,48},{64,72... | collective-permute-start | bytes 589832 | tf_op jit(solution)/shard_map/ppermute | solution.py:49
  54.6 3.0 %collective-permute-start.7 = (bf16[4,96,256]{2,1,0:T(8,128)(2,1)S(1)}, bf16[4,96,256]{2,1,0:T(8,128)(2,1)S(1)}, u32[]{:S(2)}, u32[]{:S(2)}) collective-permute-start(bf16[4,96,256]{2,1,0:T(8,128)(2,1)S(1)} %collective-permute-done.3.refs_3_), channel_id=1, source_target_pairs={{8,16},{16,8},{24,32},{32,24},{40,48},{48,40},{56,64},{64,56},{72,... | collective-permute-start | bytes 589832 | tf_op jit(solution)/shard_map/ppermute | solution.py:49
  58.4 0.7 copy-start.10
  64.2 7.5 %collective-permute-start.8 = (bf16[128,2304]{1,0:T(8,128)(2,1)}, bf16[128,2304]{1,0:T(8,128)(2,1)S(1)}, u32[]{:S(2)}, u32[]{:S(2)}) collective-permute-start(bf16[128,2304]{1,0:T(8,128)(2,1)} %get-tuple-element.19), channel_id=1, source_target_pairs={{0,1},{1,0},{2,3},{3,2},{4,5},{5,4},{6,7},{7,6},{8,9},{9,8},{10,11... | collective-permute-start | bytes 1769480 | tf_op jit(solution)/shard_map/ppermute | solution.py:36
  73.7 20.2 %all-to-all-start.1 = ((bf16[4,32,2304]{2,1,0:T(8,128)(2,1)}), bf16[4,32,2304]{2,1,0:T(8,128)(2,1)S(1)}, u32[]{:S(2)}, u32[]{:S(2)}) async-start(bf16[4,32,2304]{2,1,0:T(8,128)(2,1)} %bitcast.12), calls=%async_computation.1 | async-start | bytes 1179648 | tf_op jit(solution)/shard_map/all_to_all | solution.py:201
  128.7 15.4 %copy-start.1 = (bf16[8,16,2560]{2,1,0:T(8,128)(2,1)}, bf16[8,16,2560]{2,1,0:T(8,128)(2,1)S(1)}, u32[]{:S(2)}) copy-start(bf16[8,16,2560]{2,1,0:T(8,128)(2,1)S(1)} %all_to_all.26) | copy-start | bytes 1966084
  128.8 15.4 %collective-permute-start.9 = (bf16[128,2304]{1,0:T(8,128)(2,1)S(1)}, bf16[128,2304]{1,0:T(8,128)(2,1)S(1)}, u32[]{:S(2)}, u32[]{:S(2)}) collective-permute-start(bf16[128,2304]{1,0:T(8,128)(2,1)S(1)} %slice.65), channel_id=1, source_target_pairs={{0,1},{1,0},{2,3},{3,2},{4,5},{5,4},{6,7},{7,6},{8,9},{9,8},{10,11... | collective-permute-start | bytes 1769480 | tf_op jit(solution)/shard_map/ppermute | solution.py:36
  136.0 20.8 %all-to-all-start.4 = ((f32[8,1,2304]{2,1,0:T(1,128)}), f32[8,1,2304]{2,1,0:T(1,128)S(1)}, u32[]{:S(2)}, u32[]{:S(2)}) async-start(f32[8,1,2304]{2,1,0:T(1,128)} %broadcast_in_dim.35), calls=%async_computation.4 | async-start | bytes 147456 | tf_op jit(solution)/shard_map/all_to_all | solution.py:244
  144.2 0.8 copy-start.3
  (1 other events, 0.7 us)

commit v5 on v4

--- a/solution.py
+++ b/solution.py
@@ -7,7 +7,7 @@
 from jax.experimental.pallas import tpu as pltpu
 from jax.sharding import PartitionSpec as P
 
-FACTORS = {128: (4, 4, 8), 16: (2, 2, 4)}
+FACTORS = {128: (4, 4, 8), 16: (4, 1, 4)}
 TILE = 8
 
 
@@ -34,6 +34,11 @@
 
 def swapped_core(block):
     return lax.ppermute(block, "lon", [(i, i ^ 1) for i in range(lax.axis_size("lon"))])
+
+
+def passed_along(block, by):
+    count = lax.axis_size("lat")
+    return lax.ppermute(block, "lat", [(i, i + by) for i in range(count) if 0 <= i + by < count])
 
 
 def paired(block, axis, first, loop):
@@ -53,6 +58,14 @@
     copies = jnp.broadcast_to(block, (factors[dim],) + block.shape)
     joined = lax.all_to_all(copies, "lat", 0, 0, axis_index_groups=groups((dim,), factors))
     return joined.reshape(-1, block.shape[1])
+
+
+def doubled(block, mask, after, factors):
+    mask = mask * factors[1] * factors[2]
+    pairs = [(i, i ^ mask) for i in range(lax.axis_size("lat"))]
+    other = lax.ppermute(block, "lat", pairs)
+    block, after = lax.optimization_barrier((block, after))
+    return jnp.concatenate([block, other], axis=0), after
 
 
 def band_kernel(rows_ref, band_ref):
@@ -128,8 +141,6 @@
     cells = rows * cols
     bf16 = jnp.bfloat16
 
-    gathered = spread_over(lax.dynamic_slice_in_dim(weight, core, 1, 0), 1, factors)
-
     offsets = jnp.arange(width) - reach
     validity = jnp.abs(offsets)[None, None, :] <= spans[:, :, None]
     masked = jnp.where(validity[:, :, None, :], basis, jnp.zeros_like(basis))
@@ -140,9 +151,7 @@
             for row in range(rows)
         ],
         axis=1,
-    ).reshape(nbasis * rows, window_rows // rows, rows * window_cols)
-    band_rows = jnp.where(lat % 2 == 0, band_rows[:, ::-1], band_rows)
-    band_rows = band_rows.reshape(nbasis * rows, window_rows * window_cols)
+    ).reshape(nbasis * rows, window_rows * window_cols)
     band = pl.pallas_call(
         band_kernel,
         out_shape=jax.ShapeDtypeStruct((nbasis * rows * TILE, window_rows * window_cols), bf16),
@@ -170,16 +179,15 @@
     left = jnp.where(core == 0, far_edge, near_edge)
     right = jnp.where(core == 0, near_edge, far_edge)
     own = jnp.concatenate([left, fields, right], axis=1)
-    own, gathered = lax.optimization_barrier((own, gathered))
-    near, far = own, own
-    nears, fars = [], []
-    for turn in range(3):
-        if turn == 2:
-            near, far, band, cot = lax.optimization_barrier((near, far, band, cot))
-        near, far = paired(far, "lat", 0, False), paired(near, "lat", 1, False)
-        nears.append(near)
-        fars.append(far)
-    windows = nears[::-1] + [own] + fars
+    windows = {0: own}
+    for by in (3, -3, 2, -2, 1, -1):
+        windows[by] = passed_along(own, by)
+
+    mine = lax.dynamic_slice_in_dim(weight, core, 1, 0)
+    windows[3], mine = lax.optimization_barrier((windows[3], mine))
+    gathered = spread_over(mine, 2, factors)
+    windows[-1], gathered, band, cot = lax.optimization_barrier((windows[-1], gathered, band, cot))
+    pieces = [windows[by] for by in (3, 2, 1, 0, -1, -2, -3)]
 
     features, keep, send = pl.pallas_call(
         lambda *refs: feature_kernel(nbasis, tile_count, *refs),
@@ -191,7 +199,7 @@
         in_specs=vmem(9),
         out_specs=tuple(vmem(3)),
         name="features",
-    )(band, cot, *windows)
+    )(band, cot, *pieces)
 
     f32 = jnp.float32
     length = nbasis * channels
@@ -201,29 +209,29 @@
         return lax.all_to_all(block, "lat", 0, 0, axis_index_groups=groups((dim,), factors))
 
     total = (keep.astype(f32) + swapped_core(send).astype(f32)).astype(bf16)
-    total = jnp.sum(exchanged(total, 1).astype(f32), axis=0).astype(bf16)
-
-    total = total.reshape(zs, ys, length)
-    folded = jnp.concatenate([gathered[:, : length // 2], gathered[:, length // 2 :]], axis=0)
-    folded = jnp.pad(folded, ((0, ys - folded.shape[0]), (0, 0)))
-    folded = jnp.broadcast_to(folded, (zs,) + folded.shape)
-    arrived = exchanged(jnp.concatenate([total, folded], axis=2), 0)
+    total = total.reshape(xs, zs * ys, length)
+    third = length // 3
+    folded = jnp.concatenate([gathered[:, n * third : (n + 1) * third] for n in range(3)], axis=0)
+    folded = jnp.pad(folded, ((0, total.shape[1] - 3 * ys), (0, 0)))
+    folded = jnp.broadcast_to(folded, (xs,) + folded.shape)
+    arrived = exchanged(jnp.concatenate([total, folded], axis=2), 1)
     total = jnp.sum(arrived[:, :, :length].astype(f32), axis=0).astype(bf16)
     gathered = jnp.concatenate(
-        [arrived[:, :xs, length:], arrived[:, xs : 2 * xs, length:]], axis=2
-    ).reshape(zs * xs, length)
-
-    piece = zs * xs
-    column = -(-length // piece // 128) * 128
-    folded = jnp.pad(total, ((0, 0), (0, piece * column - length))).reshape(ys, piece, column)
-    whole = jnp.broadcast_to(gathered, (ys,) + gathered.shape)
-    arrived = exchanged(jnp.concatenate([whole, folded], axis=2), 2)
-    gathered = arrived.reshape(ys * piece, length + column)
-    total = jnp.sum(arrived[:, :, length:].astype(f32), axis=0).reshape(1, -1)[:, :length]
-
-    other_weight = swapped_core(gathered[:, :length])
+        [arrived[:, n * ys : (n + 1) * ys, length:] for n in range(3)], axis=2
+    ).reshape(xs * ys, length)
+
+    total = jnp.sum(exchanged(total, 0).astype(f32), axis=0)
+    gathered, total = doubled(gathered, 1, total, factors)
+    total = jnp.sum(exchanged(total, 2), axis=0)
+    scale = 1.0 / math.sqrt(rows * lax.axis_size("lat") * cols * lax.axis_size("lon"))
+    lon_size = lax.axis_size("lon")
+    spread = jnp.broadcast_to(total * scale, (lon_size,) + total.shape)
+    if zs == 4:
+        gathered, spread = doubled(gathered, 2, spread, factors)
+    other_weight = swapped_core(gathered)
     place = position % half
-    weight_row = 2 * lat_index(place // xs % zs, place % xs, place // piece, factors)
+    from_z = (lat // (xs * ys)) ^ (place // (xs * ys))
+    weight_row = 2 * lat_index(from_z, place // ys % xs, place % ys, factors)
     weight_row = weight_row + (core ^ (position // half))
     weight_order = (weight_row[:, None] == jnp.arange(outs)[None, :]).astype(bf16)
 
@@ -238,9 +246,6 @@
         name="mixing",
     )(features, gathered, other_weight, weight_order)
 
-    scale = 1.0 / math.sqrt(rows * lax.axis_size("lat") * cols * lax.axis_size("lon"))
-    lon_size = lax.axis_size("lon")
-    spread = jnp.broadcast_to(total * scale, (lon_size,) + total.shape)
     arrived = lax.all_to_all(spread, "lon", 0, 0)
     arrived, output = lax.optimization_barrier((arrived, output))
     grad_weight = jnp.sum(arrived.reshape(lon_size // 2, 2, nbasis * channels), axis=0)

time: 159 us -> 159 us (level)
  blocking collectives: 34.5 us -> 14.4 us
  waiting for transfers between devices: 27.3 us -> 39.5 us
  starting transfers between devices: 71 us -> 78.2 us
    ppermute x0 -> x8, starting transfers between devices: none -> 23.5 us  [the longest x6 17.6 us: passed_along(): lax.ppermute(block, 'lat', [(i, i + by) for i in range(count) if 0 <= i +...]
    all_to_all x2 -> x1, blocking collectives: 34.5 us -> 14.4 us  [exchanged(): lax.all_to_all(block, 'lat', 0, 0, axis_index_groups=groups((dim,), facto...]
    ppermute x8 -> x2, starting transfers between devices: 36.9 us -> 21 us  [paired(): return lax.ppermute(block, axis, pairs)]
    all_to_all x1, waiting for transfers between devices: 1.93 us -> 14.7 us  [spread_over(): lax.all_to_all(copies, 'lat', 0, 0, axis_index_groups=groups((dim,), fact...]
    ppermute x0 -> x8, waiting for transfers between devices: none -> 9.23 us  [the longest x2 9.22 us: doubled(): other = lax.ppermute(block, 'lat', pairs)]
    all_to_all x1, starting transfers between devices: 4.01 us -> 9.99 us  [spread_over(): lax.all_to_all(copies, 'lat', 0, 0, axis_index_groups=groups((dim,), fact...]
    ppermute x8 -> x2, waiting for transfers between devices: 5.21 us -> 0.01 us  [paired(): return lax.ppermute(block, axis, pairs)]
    ppermute x2, starting transfers between devices: 12.1 us -> 7.05 us  [swapped_core(): lax.ppermute(block, 'lon', [(i, i ^ 1) for i in range(lax.axis_size('lon'...]
  transfers between devices with their start and end apart: 13 -> 16, of which waited for: 6 -> 6; matrix products, arithmetic and copies ran while one was open for 5% -> 5% of each run, Pallas kernels for 3% -> 3%
where the time goes in v5:
time: 159 us; the launch traced here: 158 us
  starting transfers between devices  78.2 us (49%)
  waiting for transfers between devices  39.5 us (25%)
  blocking collectives  14.4 us (9%)
  Pallas kernels  10.1 us (6%)
  other arithmetic  7.36 us (5%)
  local copies, waits for them, and re-layouts  6.18 us (4%)
    ppermute x2, starting transfers between devices, paired(): return lax.ppermute(block, axis, pairs)  21 us
    ppermute x6, starting transfers between devices, passed_along(): lax.ppermute(block, 'lat', [(i, i + by) for i in range(count) if 0 <= i +...  17.6 us
    all_to_all x1, waiting for transfers between devices, spread_over(): lax.all_to_all(copies, 'lat', 0, 0, axis_index_groups=groups((dim,), fact...  14.7 us
    all_to_all x1, blocking collectives, exchanged(): lax.all_to_all(block, 'lat', 0, 0, axis_index_groups=groups((dim,), facto...  14.4 us
    all_to_all x1, starting transfers between devices, spread_over(): lax.all_to_all(copies, 'lat', 0, 0, axis_index_groups=groups((dim,), fact...  9.99 us
    all_to_all x2, starting transfers between devices, exchanged(): lax.all_to_all(block, 'lat', 0, 0, axis_index_groups=groups((dim,), facto...  9.42 us
    ppermute x2, waiting for transfers between devices, doubled(): other = lax.ppermute(block, 'lat', pairs)  9.22 us
    all_to_all x1, waiting for transfers between devices, shards(): arrived = lax.all_to_all(spread, 'lon', 0, 0)  7.54 us
  transfers between devices with their start and end apart: 16, of which 6 were waited for; matrix products, arithmetic and copies ran while one was open for 5% of the time, Pallas kernels for 3%

profile of v5, /device:TPU:1, one launch (start us, length us, event | category | flops | bytes accessed | tf_op | source)
XLA Modules:
  0.0 157.9 jit_solution(8335060456282111655)
XLA Ops:
  1.5 12.0 %collective-permute-start = (bf16[4,12,256]{2,1,0:T(8,128)(2,1)S(1)}, bf16[4,12,256]{2,1,0:T(8,128)(2,1)S(1)}, u32[]{:S(2)}, u32[]{:S(2)}) collective-permute-start(bf16[4,12,256]{2,1,0:T(8,128)(2,1)S(1)} %get-tuple-element.39), channel_id=1, source_target_pairs={{1,2},{2,1},{3,4},{4,3},{5,6},{6,5},{7,0},{0,7},{9,10},{10,9},{11,... | collective-permute-start | bytes 73736 | tf_op jit(solution)/shard_map/ppermute | solution.py:54
  13.5 9.0 %collective-permute-start.1 = (bf16[4,12,256]{2,1,0:T(8,128)(2,1)S(1)}, bf16[4,12,256]{2,1,0:T(8,128)(2,1)S(1)}, u32[]{:S(2)}, u32[]{:S(2)}) collective-permute-start(bf16[4,12,256]{2,1,0:T(8,128)(2,1)S(1)} %get-tuple-element.40), channel_id=1, source_target_pairs={{0,1},{1,0},{2,3},{3,2},{4,5},{5,4},{6,7},{7,6},{8,9},{9,8},{10,11... | collective-permute-start | bytes 73736 | tf_op jit(solution)/shard_map/ppermute | solution.py:54
  24.7 5.2 %collective-permute-start.3 = (bf16[4,96,256]{2,1,0:T(8,128)(2,1)S(1)}, bf16[4,96,256]{2,1,0:T(8,128)(2,1)S(1)}, u32[]{:S(2)}, u32[]{:S(2)}) collective-permute-start(bf16[4,96,256]{2,1,0:T(8,128)(2,1)S(1)} %pad_maximum_fusion.2.refs_5_), channel_id=1, source_target_pairs={{0,24},{8,32},{16,40},{24,48},{32,56},{40,64},{48,72},{56,80},{64,... | collective-permute-start | bytes 589832 | tf_op jit(solution)/shard_map/ppermute | solution.py:41
  32.2 6.2 %collective-permute-start.4 = (bf16[4,96,256]{2,1,0:T(8,128)(2,1)S(1)}, bf16[4,96,256]{2,1,0:T(8,128)(2,1)S(1)}, u32[]{:S(2)}, u32[]{:S(2)}) collective-permute-start(bf16[4,96,256]{2,1,0:T(8,128)(2,1)S(1)} %pad_maximum_fusion.2.refs_5_), channel_id=1, source_target_pairs={{0,16},{8,24},{16,32},{24,40},{32,48},{40,56},{48,64},{56,72},{64,... | collective-permute-start | bytes 589832 | tf_op jit(solution)/shard_map/ppermute | solution.py:41
  38.4 2.3 %collective-permute-start.5 = (bf16[4,96,256]{2,1,0:T(8,128)(2,1)S(1)}, bf16[4,96,256]{2,1,0:T(8,128)(2,1)S(1)}, u32[]{:S(2)}, u32[]{:S(2)}) collective-permute-start(bf16[4,96,256]{2,1,0:T(8,128)(2,1)S(1)} %pad_maximum_fusion.2.refs_5_), channel_id=1, source_target_pairs={{0,8},{8,16},{16,24},{24,32},{32,40},{40,48},{48,56},{56,64},{64,7... | collective-permute-start | bytes 589832 | tf_op jit(solution)/shard_map/ppermute | solution.py:41
  42.1 1.3 collective-permute-start.7
  45.5 10.0 %all-to-all-start = ((bf16[8,2,1152]{2,1,0:T(2,128)(2,1)}), bf16[8,2,1152]{2,1,0:T(2,128)(2,1)S(1)}, u32[]{:S(2)}, u32[]{:S(2)}) async-start(bf16[8,2,1152]{2,1,0:T(2,128)(2,1)} %reshape.185), calls=%async_computation | async-start | bytes 73728 | tf_op jit(solution)/shard_map/all_to_all | solution.py:59
  56.5 1.9 %shard_map.68.refs_0_ = bf16[288,896]{1,0:T(8,128)(2,1)} custom-call(f32[36,896]{1,0:T(8,128)} %reshape.175.rows_ref), custom_call_target="tpu_custom_call" | custom-call | tf_op jit(solution)/shard_map/pallas_call | solution.py:155
  58.4 14.7 %all-to-all-done = bf16[8,2,1152]{2,1,0:T(2,128)(2,1)S(1)} async-done(((bf16[8,2,1152]{2,1,0:T(2,128)(2,1)}), bf16[8,2,1152]{2,1,0:T(2,128)(2,1)S(1)}, u32[]{:S(2)}, u32[]{:S(2)}) %all-to-all-start) | async-done | bytes 36896 | tf_op jit(solution)/shard_map/all_to_all | solution.py:59
  74.7 5.2 %features.1 = (bf16[9,288,256]{2,1,0:T(8,128)(2,1)}, bf16[128,2304]{1,0:T(8,128)(2,1)}, bf16[128,2304]{1,0:T(8,128)(2,1)}) custom-call(bf16[288,896]{1,0:T(8,128)(2,1)} %shard_map.68.refs_0_, bf16[256,288]{1,0:T(8,128)(2,1)} %convolution_convert_fusion.refs_1_, bf16[4,96,256]{2,1,0:T(8,128)(2,1)} %copy-done.5, bf16[4,96,256]{2,1,0:T(8,128)(2,1)} %copy-done.7, ...), custom_call_target="tpu_custom_call" | custom-call | tf_op jit(solution)/shard_map/features/pallas_call | solution.py:192
  79.9 3.9 %collective-permute-start.8 = (bf16[128,2304]{1,0:T(8,128)(2,1)}, bf16[128,2304]{1,0:T(8,128)(2,1)S(1)}, u32[]{:S(2)}, u32[]{:S(2)}) collective-permute-start(bf16[128,2304]{1,0:T(8,128)(2,1)} %get-tuple-element.23), channel_id=1, source_target_pairs={{0,1},{1,0},{2,3},{3,2},{4,5},{5,4},{6,7},{7,6},{8,9},{9,8},{10,11... | collective-permute-start | bytes 1769480 | tf_op jit(solution)/shard_map/ppermute | solution.py:36
  83.8 1.8 %collective-permute-done.8 = bf16[128,2304]{1,0:T(8,128)(2,1)S(1)} collective-permute-done((bf16[128,2304]{1,0:T(8,128)(2,1)}, bf16[128,2304]{1,0:T(8,128)(2,1)S(1)}, u32[]{:S(2)}, u32[]{:S(2)}) %collective-permute-start.8) | collective-permute-done | bytes 589856 | tf_op jit(solution)/shard_map/ppermute | solution.py:36
  86.9 14.4 %all_to_all.25 = bf16[4,32,3072]{2,1,0:T(8,128)(2,1)S(1)} all-to-all(bf16[4,32,3072]{2,1,0:T(8,128)(2,1)S(1)} %pad_maximum_fusion), channel_id=1, replica_groups={{0,64,128,192},{8,72,136,200},{16,80,144,208},{24,88,152,216},{32,96,16..., dimensions={0} | all-to-all | bytes 1572864 | tf_op jit(solution)/shard_map/all_to_all | solution.py:209
  102.1 3.7 %all-to-all-start.2 = ((bf16[4,8,2304]{2,1,0:T(8,128)(2,1)}), bf16[4,8,2304]{2,1,0:T(8,128)(2,1)S(1)}, u32[]{:S(2)}, u32[]{:S(2)}) async-start(bf16[4,8,2304]{2,1,0:T(8,128)(2,1)} %bitcast.14), calls=%async_computation.2 | async-start | bytes 294912 | tf_op jit(solution)/shard_map/all_to_all | solution.py:209
  105.8 3.4 %collective-permute-start.9 = (bf16[32,2304]{1,0:T(8,128)(2,1)S(1)}, bf16[32,2304]{1,0:T(8,128)(2,1)S(1)}, u32[]{:S(2)}, u32[]{:S(2)}) collective-permute-start(bf16[32,2304]{1,0:T(8,128)(2,1)S(1)} %maximum_bitcast_fusion), channel_id=1, source_target_pairs={{0,256},{8,264},{16,272},{24,280},{32,288},{40,296},{48,304},{56,3... | collective-permute-start | bytes 442376 | tf_op jit(solution)/shard_map/ppermute | solution.py:66
  109.2 1.5 all-to-all-done.2
  111.5 5.7 %all-to-all-start.3 = ((f32[8,1,2304]{2,1,0:T(1,128)}), f32[8,1,2304]{2,1,0:T(1,128)S(1)}, u32[]{:S(2)}, u32[]{:S(2)}) async-start(f32[8,1,2304]{2,1,0:T(1,128)} %copy.43), calls=%async_computation.3 | async-start | bytes 147456 | tf_op jit(solution)/shard_map/all_to_all | solution.py:209
  117.2 2.5 %collective-permute-start.10 = (bf16[64,2304]{1,0:T(8,128)(2,1)S(1)}, bf16[64,2304]{1,0:T(8,128)(2,1)S(1)}, u32[]{:S(2)}, u32[]{:S(2)}) collective-permute-start(bf16[64,2304]{1,0:T(8,128)(2,1)S(1)} %constant_dynamic-update-slice_fusion), channel_id=1, source_target_pairs={{0,512},{8,520},{16,528},{24,536},{32,544},{40,552},{48,560},{56,5... | collective-permute-start | bytes 884744 | tf_op jit(solution)/shard_map/ppermute | solution.py:66
  119.7 4.8 %all-to-all-done.3 = f32[8,1,2304]{2,1,0:T(1,128)S(1)} async-done(((f32[8,1,2304]{2,1,0:T(1,128)}), f32[8,1,2304]{2,1,0:T(1,128)S(1)}, u32[]{:S(2)}, u32[]{:S(2)}) %all-to-all-start.3) | async-done | bytes 73760 | tf_op jit(solution)/shard_map/all_to_all | solution.py:209
  125.3 9.2 %collective-permute-done.10 = bf16[64,2304]{1,0:T(8,128)(2,1)S(1)} collective-permute-done((bf16[64,2304]{1,0:T(8,128)(2,1)S(1)}, bf16[64,2304]{1,0:T(8,128)(2,1)S(1)}, u32[]{:S(2)}, u32[]{:S(2)}) %collective-permute-start.10) | collective-permute-done | bytes 294944 | tf_op jit(solution)/shard_map/ppermute | solution.py:66
  134.5 3.2 %collective-permute-start.11 = (bf16[128,2304]{1,0:T(8,128)(2,1)S(1)}, bf16[128,2304]{1,0:T(8,128)(2,1)S(1)}, u32[]{:S(2)}, u32[]{:S(2)}) collective-permute-start(bf16[128,2304]{1,0:T(8,128)(2,1)S(1)} %constant_dynamic-update-slice_fusion.2.refs_1_), channel_id=1, source_target_pairs={{0,1},{1,0},{2,3},{3,2},{4,5},{5,4},{6,7},{7,6},{8,9},{9,8},{10,11... | collective-permute-start | bytes 1769480 | tf_op jit(solution)/shard_map/ppermute | solution.py:36
  137.7 7.2 %all-to-all-start.4 = ((f32[8,1,2304]{2,1,0:T(1,128)}), f32[8,1,2304]{2,1,0:T(1,128)S(1)}, u32[]{:S(2)}, u32[]{:S(2)}) async-start(f32[8,1,2304]{2,1,0:T(1,128)} %broadcast_in_dim.31), calls=%async_computation.4 | async-start | bytes 147456 | tf_op jit(solution)/shard_map/all_to_all | solution.py:249
  146.5 3.0 %mixing.1 = bf16[4,72,256]{2,1,0:T(8,128)(2,1)} custom-call(bf16[9,288,256]{2,1,0:T(8,128)(2,1)} %get-tuple-element.28.refs_0_, bf16[128,2304]{1,0:T(8,128)(2,1)} %copy-done.1, bf16[128,2304]{1,0:T(8,128)(2,1)} %copy-done.3, bf16[256,256]{1,0:T(8,128)(2,1)} %fusion.refs_3_), custom_call_target="tpu_custom_call" | custom-call | flops 377487360 | bytes 5308416 | tf_op jit(solution)/shard_map/mixing/pallas_call | solution.py:238
  149.5 7.5 %all-to-all-done.4 = f32[8,1,2304]{2,1,0:T(1,128)S(1)} async-done(((f32[8,1,2304]{2,1,0:T(1,128)}), f32[8,1,2304]{2,1,0:T(1,128)S(1)}, u32[]{:S(2)}, u32[]{:S(2)}) %all-to-all-start.4) | async-done | bytes 73760 | tf_op jit(solution)/shard_map/all_to_all | solution.py:249
  (81 shorter events, 17.1 us)
Async XLA Ops:
  0.6 23.8 %copy-start = (bf16[2,2304]{1,0:T(2,128)(2,1)S(1)}, bf16[2,2304]{1,0:T(2,128)(2,1)}, u32[]{:S(2)}) copy-start(bf16[2,2304]{1,0:T(2,128)(2,1)} %param.8) | copy-start | bytes 27652
  1.5 23.1 %collective-permute-start = (bf16[4,12,256]{2,1,0:T(8,128)(2,1)S(1)}, bf16[4,12,256]{2,1,0:T(8,128)(2,1)S(1)}, u32[]{:S(2)}, u32[]{:S(2)}) collective-permute-start(bf16[4,12,256]{2,1,0:T(8,128)(2,1)S(1)} %get-tuple-element.39), channel_id=1, source_target_pairs={{1,2},{2,1},{3,4},{4,3},{5,6},{6,5},{7,0},{0,7},{9,10},{10,9},{11,... | collective-permute-start | bytes 73736 | tf_op jit(solution)/shard_map/ppermute | solution.py:54
  13.5 11.1 %collective-permute-start.1 = (bf16[4,12,256]{2,1,0:T(8,128)(2,1)S(1)}, bf16[4,12,256]{2,1,0:T(8,128)(2,1)S(1)}, u32[]{:S(2)}, u32[]{:S(2)}) collective-permute-start(bf16[4,12,256]{2,1,0:T(8,128)(2,1)S(1)} %get-tuple-element.40), channel_id=1, source_target_pairs={{0,1},{1,0},{2,3},{3,2},{4,5},{5,4},{6,7},{7,6},{8,9},{9,8},{10,11... | collective-permute-start | bytes 73736 | tf_op jit(solution)/shard_map/ppermute | solution.py:54
  22.5 2.0 %copy-start.11 = (bf16[4,72,256]{2,1,0:T(8,128)(2,1)S(1)}, bf16[4,72,256]{2,1,0:T(8,128)(2,1)}, u32[]{:S(2)}) copy-start(bf16[4,72,256]{2,1,0:T(8,128)(2,1)} %param.9) | copy-start | bytes 442372
  23.4 1.3 copy-start.4
  24.7 30.9 %copy-start.2 = (bf16[4,96,256]{2,1,0:T(8,128)(2,1)}, bf16[4,96,256]{2,1,0:T(8,128)(2,1)S(1)}, u32[]{:S(2)}) copy-start(bf16[4,96,256]{2,1,0:T(8,128)(2,1)S(1)} %pad_maximum_fusion.2.refs_5_) | copy-start | bytes 589828
  24.7 17.4 %collective-permute-start.3 = (bf16[4,96,256]{2,1,0:T(8,128)(2,1)S(1)}, bf16[4,96,256]{2,1,0:T(8,128)(2,1)S(1)}, u32[]{:S(2)}, u32[]{:S(2)}) collective-permute-start(bf16[4,96,256]{2,1,0:T(8,128)(2,1)S(1)} %pad_maximum_fusion.2.refs_5_), channel_id=1, source_target_pairs={{0,24},{8,32},{16,40},{24,48},{32,56},{40,64},{48,72},{56,80},{64,... | collective-permute-start | bytes 589832 | tf_op jit(solution)/shard_map/ppermute | solution.py:41
  30.9 42.2 %collective-permute-start.2 = (bf16[4,96,256]{2,1,0:T(8,128)(2,1)S(1)}, bf16[4,96,256]{2,1,0:T(8,128)(2,1)S(1)}, u32[]{:S(2)}, u32[]{:S(2)}) collective-permute-start(bf16[4,96,256]{2,1,0:T(8,128)(2,1)S(1)} %pad_maximum_fusion.2.refs_5_), channel_id=1, source_target_pairs={{8,0},{16,8},{24,16},{32,24},{40,32},{48,40},{56,48},{64,56},{72,6... | collective-permute-start | bytes 589832 | tf_op jit(solution)/shard_map/ppermute | solution.py:41
  32.2 41.0 %collective-permute-start.4 = (bf16[4,96,256]{2,1,0:T(8,128)(2,1)S(1)}, bf16[4,96,256]{2,1,0:T(8,128)(2,1)S(1)}, u32[]{:S(2)}, u32[]{:S(2)}) collective-permute-start(bf16[4,96,256]{2,1,0:T(8,128)(2,1)S(1)} %pad_maximum_fusion.2.refs_5_), channel_id=1, source_target_pairs={{0,16},{8,24},{16,32},{24,40},{32,48},{40,56},{48,64},{56,72},{64,... | collective-permute-start | bytes 589832 | tf_op jit(solution)/shard_map/ppermute | solution.py:41
  38.4 34.8 %collective-permute-start.5 = (bf16[4,96,256]{2,1,0:T(8,128)(2,1)S(1)}, bf16[4,96,256]{2,1,0:T(8,128)(2,1)S(1)}, u32[]{:S(2)}, u32[]{:S(2)}) collective-permute-start(bf16[4,96,256]{2,1,0:T(8,128)(2,1)S(1)} %pad_maximum_fusion.2.refs_5_), channel_id=1, source_target_pairs={{0,8},{8,16},{16,24},{24,32},{32,40},{40,48},{48,56},{56,64},{64,7... | collective-permute-start | bytes 589832 | tf_op jit(solution)/shard_map/ppermute | solution.py:41
  40.8 32.5 %collective-permute-start.6 = (bf16[4,96,256]{2,1,0:T(8,128)(2,1)S(1)}, bf16[4,96,256]{2,1,0:T(8,128)(2,1)S(1)}, u32[]{:S(2)}, u32[]{:S(2)}) collective-permute-start(bf16[4,96,256]{2,1,0:T(8,128)(2,1)S(1)} %pad_maximum_fusion.2.refs_5_), channel_id=1, source_target_pairs={{16,0},{24,8},{32,16},{40,24},{48,32},{56,40},{64,48},{72,56},{80,... | collective-permute-start | bytes 589832 | tf_op jit(solution)/shard_map/ppermute | solution.py:41
  42.1 13.5 %copy-start.5 = (bf16[4,96,256]{2,1,0:T(8,128)(2,1)}, bf16[4,96,256]{2,1,0:T(8,128)(2,1)S(1)}, u32[]{:S(2)}) copy-start(bf16[4,96,256]{2,1,0:T(8,128)(2,1)S(1)} %collective-permute-done.3.refs_2_) | copy-start | bytes 589828
  42.1 31.2 %collective-permute-start.7 = (bf16[4,96,256]{2,1,0:T(8,128)(2,1)S(1)}, bf16[4,96,256]{2,1,0:T(8,128)(2,1)S(1)}, u32[]{:S(2)}, u32[]{:S(2)}) collective-permute-start(bf16[4,96,256]{2,1,0:T(8,128)(2,1)S(1)} %pad_maximum_fusion.2.refs_5_), channel_id=1, source_target_pairs={{24,0},{32,8},{40,16},{48,24},{56,32},{64,40},{72,48},{80,56},{88,... | collective-permute-start | bytes 589832 | tf_op jit(solution)/shard_map/ppermute | solution.py:41
  45.5 27.6 %all-to-all-start = ((bf16[8,2,1152]{2,1,0:T(2,128)(2,1)}), bf16[8,2,1152]{2,1,0:T(2,128)(2,1)S(1)}, u32[]{:S(2)}, u32[]{:S(2)}) async-start(bf16[8,2,1152]{2,1,0:T(2,128)(2,1)} %reshape.185), calls=%async_computation | async-start | bytes 73728 | tf_op jit(solution)/shard_map/all_to_all | solution.py:59
  73.2 0.8 copy-start.9
  79.9 5.7 %collective-permute-start.8 = (bf16[128,2304]{1,0:T(8,128)(2,1)}, bf16[128,2304]{1,0:T(8,128)(2,1)S(1)}, u32[]{:S(2)}, u32[]{:S(2)}) collective-permute-start(bf16[128,2304]{1,0:T(8,128)(2,1)} %get-tuple-element.23), channel_id=1, source_target_pairs={{0,1},{1,0},{2,3},{3,2},{4,5},{5,4},{6,7},{7,6},{8,9},{9,8},{10,11... | collective-permute-start | bytes 1769480 | tf_op jit(solution)/shard_map/ppermute | solution.py:36
  102.1 8.6 %all-to-all-start.2 = ((bf16[4,8,2304]{2,1,0:T(8,128)(2,1)}), bf16[4,8,2304]{2,1,0:T(8,128)(2,1)S(1)}, u32[]{:S(2)}, u32[]{:S(2)}) async-start(bf16[4,8,2304]{2,1,0:T(8,128)(2,1)} %bitcast.14), calls=%async_computation.2 | async-start | bytes 294912 | tf_op jit(solution)/shard_map/all_to_all | solution.py:209
  105.8 11.3 %collective-permute-start.9 = (bf16[32,2304]{1,0:T(8,128)(2,1)S(1)}, bf16[32,2304]{1,0:T(8,128)(2,1)S(1)}, u32[]{:S(2)}, u32[]{:S(2)}) collective-permute-start(bf16[32,2304]{1,0:T(8,128)(2,1)S(1)} %maximum_bitcast_fusion), channel_id=1, source_target_pairs={{0,256},{8,264},{16,272},{24,280},{32,288},{40,296},{48,304},{56,3... | collective-permute-start | bytes 442376 | tf_op jit(solution)/shard_map/ppermute | solution.py:66
  111.5 13.0 %all-to-all-start.3 = ((f32[8,1,2304]{2,1,0:T(1,128)}), f32[8,1,2304]{2,1,0:T(1,128)S(1)}, u32[]{:S(2)}, u32[]{:S(2)}) async-start(f32[8,1,2304]{2,1,0:T(1,128)} %copy.43), calls=%async_computation.3 | async-start | bytes 147456 | tf_op jit(solution)/shard_map/all_to_all | solution.py:209
  117.2 17.3 %collective-permute-start.10 = (bf16[64,2304]{1,0:T(8,128)(2,1)S(1)}, bf16[64,2304]{1,0:T(8,128)(2,1)S(1)}, u32[]{:S(2)}, u32[]{:S(2)}) collective-permute-start(bf16[64,2304]{1,0:T(8,128)(2,1)S(1)} %constant_dynamic-update-slice_fusion), channel_id=1, source_target_pairs={{0,512},{8,520},{16,528},{24,536},{32,544},{40,552},{48,560},{56,5... | collective-permute-start | bytes 884744 | tf_op jit(solution)/shard_map/ppermute | solution.py:66
  134.5 11.2 %copy-start.1 = (bf16[128,2304]{1,0:T(8,128)(2,1)}, bf16[128,2304]{1,0:T(8,128)(2,1)S(1)}, u32[]{:S(2)}) copy-start(bf16[128,2304]{1,0:T(8,128)(2,1)S(1)} %constant_dynamic-update-slice_fusion.2.refs_1_) | copy-start | bytes 1769476
  134.5 11.1 %collective-permute-start.11 = (bf16[128,2304]{1,0:T(8,128)(2,1)S(1)}, bf16[128,2304]{1,0:T(8,128)(2,1)S(1)}, u32[]{:S(2)}, u32[]{:S(2)}) collective-permute-start(bf16[128,2304]{1,0:T(8,128)(2,1)S(1)} %constant_dynamic-update-slice_fusion.2.refs_1_), channel_id=1, source_target_pairs={{0,1},{1,0},{2,3},{3,2},{4,5},{5,4},{6,7},{7,6},{8,9},{9,8},{10,11... | collective-permute-start | bytes 1769480 | tf_op jit(solution)/shard_map/ppermute | solution.py:36
  137.7 19.3 %all-to-all-start.4 = ((f32[8,1,2304]{2,1,0:T(1,128)}), f32[8,1,2304]{2,1,0:T(1,128)S(1)}, u32[]{:S(2)}, u32[]{:S(2)}) async-start(f32[8,1,2304]{2,1,0:T(1,128)} %broadcast_in_dim.31), calls=%async_computation.4 | async-start | bytes 147456 | tf_op jit(solution)/shard_map/all_to_all | solution.py:249
  145.7 0.8 copy-start.3
  (4 other events, 2.9 us)

commit v6 on v5

--- a/solution.py
+++ b/solution.py
@@ -54,18 +54,17 @@
     return lax.ppermute(block, axis, pairs)
 
 
-def spread_over(block, dim, factors):
-    copies = jnp.broadcast_to(block, (factors[dim],) + block.shape)
-    joined = lax.all_to_all(copies, "lat", 0, 0, axis_index_groups=groups((dim,), factors))
+def spread_over(block, dims, factors):
+    members = groups(dims, factors)
+    copies = jnp.broadcast_to(block, (len(members[0]),) + block.shape)
+    joined = lax.all_to_all(copies, "lat", 0, 0, axis_index_groups=members)
     return joined.reshape(-1, block.shape[1])
 
 
-def doubled(block, mask, after, factors):
+def doubled(block, mask, factors):
     mask = mask * factors[1] * factors[2]
     pairs = [(i, i ^ mask) for i in range(lax.axis_size("lat"))]
-    other = lax.ppermute(block, "lat", pairs)
-    block, after = lax.optimization_barrier((block, after))
-    return jnp.concatenate([block, other], axis=0), after
+    return jnp.concatenate([block, lax.ppermute(block, "lat", pairs)], axis=0)
 
 
 def band_kernel(rows_ref, band_ref):
@@ -179,14 +178,13 @@
     left = jnp.where(core == 0, far_edge, near_edge)
     right = jnp.where(core == 0, near_edge, far_edge)
     own = jnp.concatenate([left, fields, right], axis=1)
+    gathered = spread_over(lax.dynamic_slice_in_dim(weight, core, 1, 0), (1, 2), factors)
+    own, gathered = lax.optimization_barrier((own, gathered))
+    gathered = doubled(gathered, 1, factors)
     windows = {0: own}
     for by in (3, -3, 2, -2, 1, -1):
         windows[by] = passed_along(own, by)
-
-    mine = lax.dynamic_slice_in_dim(weight, core, 1, 0)
-    windows[3], mine = lax.optimization_barrier((windows[3], mine))
-    gathered = spread_over(mine, 2, factors)
-    windows[-1], gathered, band, cot = lax.optimization_barrier((windows[-1], gathered, band, cot))
+    windows[-1], band, cot, gathered = lax.optimization_barrier((windows[-1], band, cot, gathered))
     pieces = [windows[by] for by in (3, 2, 1, 0, -1, -2, -3)]
 
     features, keep, send = pl.pallas_call(
@@ -209,26 +207,17 @@
         return lax.all_to_all(block, "lat", 0, 0, axis_index_groups=groups((dim,), factors))
 
     total = (keep.astype(f32) + swapped_core(send).astype(f32)).astype(bf16)
-    total = total.reshape(xs, zs * ys, length)
-    third = length // 3
-    folded = jnp.concatenate([gathered[:, n * third : (n + 1) * third] for n in range(3)], axis=0)
-    folded = jnp.pad(folded, ((0, total.shape[1] - 3 * ys), (0, 0)))
-    folded = jnp.broadcast_to(folded, (xs,) + folded.shape)
-    arrived = exchanged(jnp.concatenate([total, folded], axis=2), 1)
-    total = jnp.sum(arrived[:, :, :length].astype(f32), axis=0).astype(bf16)
-    gathered = jnp.concatenate(
-        [arrived[:, n * ys : (n + 1) * ys, length:] for n in range(3)], axis=2
-    ).reshape(xs * ys, length)
-
+    total, gathered = lax.optimization_barrier((total, gathered))
+    total = jnp.sum(exchanged(total, 1).astype(f32), axis=0).astype(bf16)
+    if zs == 4:
+        gathered = doubled(gathered, 2, factors)
+    total, gathered = lax.optimization_barrier((total, gathered))
     total = jnp.sum(exchanged(total, 0).astype(f32), axis=0)
-    gathered, total = doubled(gathered, 1, total, factors)
+    other_weight = swapped_core(gathered)
     total = jnp.sum(exchanged(total, 2), axis=0)
     scale = 1.0 / math.sqrt(rows * lax.axis_size("lat") * cols * lax.axis_size("lon"))
     lon_size = lax.axis_size("lon")
     spread = jnp.broadcast_to(total * scale, (lon_size,) + total.shape)
-    if zs == 4:
-        gathered, spread = doubled(gathered, 2, spread, factors)
-    other_weight = swapped_core(gathered)
     place = position % half
     from_z = (lat // (xs * ys)) ^ (place // (xs * ys))
     weight_row = 2 * lat_index(from_z, place // ys % xs, place % ys, factors)

time: 159 us -> 168 us (1.057)
  waiting for transfers between devices: 39.5 us -> 59.3 us
  blocking collectives: 14.4 us -> 0 us
  starting transfers between devices: 78.2 us -> 81.5 us
    ppermute x6, waiting for transfers between devices: 0.02 us -> 30.6 us  [passed_along(): lax.ppermute(block, 'lat', [(i, i + by) for i in range(count) if 0 <= i +...]
    all_to_all x1, waiting for transfers between devices: 14.7 us -> 0.01 us  [spread_over(): joined = lax.all_to_all(copies, 'lat', 0, 0, axis_index_groups=members)]
    all_to_all x1 -> x0, blocking collectives: 14.4 us -> none  [exchanged(): lax.all_to_all(block, 'lat', 0, 0, axis_index_groups=groups((dim,), facto...]
    all_to_all x1, starting transfers between devices: 7.17 us -> 10.7 us  [shards(): arrived = lax.all_to_all(spread, 'lon', 0, 0)]
    all_to_all x2 -> x3, waiting for transfers between devices: 6.28 us -> 9.2 us  [exchanged(): lax.all_to_all(block, 'lat', 0, 0, axis_index_groups=groups((dim,), facto...]
    ppermute x2, starting transfers between devices: 7.05 us -> 5.26 us  [swapped_core(): lax.ppermute(block, 'lon', [(i, i ^ 1) for i in range(lax.axis_size('lon'...]
    ppermute x2, starting transfers between devices: 5.88 us -> 7.59 us  [doubled(): return jnp.concatenate([block, lax.ppermute(block, 'lat', pairs)], axis=0)]
    unnamed x29 -> x31, local copies, waits for them, and re-layouts: 3.06 us -> 4.4 us
  transfers between devices with their start and end apart: 16 -> 17, of which waited for: 6 -> 8; matrix products, arithmetic and copies ran while one was open for 5% -> 3% of each run, Pallas kernels for 3% -> 3%
where the time goes in v6:
time: 168 us; the launch traced here: 167 us
  starting transfers between devices  81.5 us (49%)
  waiting for transfers between devices  59.3 us (35%)
  Pallas kernels  10.1 us (6%)
  local copies, waits for them, and re-layouts  7.59 us (5%)
  other arithmetic  6.4 us (4%)
    ppermute x6, waiting for transfers between devices, passed_along(): lax.ppermute(block, 'lat', [(i, i + by) for i in range(count) if 0 <= i +...  30.6 us
    ppermute x2, starting transfers between devices, paired(): return lax.ppermute(block, axis, pairs)  20.2 us
    ppermute x6, starting transfers between devices, passed_along(): lax.ppermute(block, 'lat', [(i, i + by) for i in range(count) if 0 <= i +...  17.1 us
    all_to_all x1, starting transfers between devices, shards(): arrived = lax.all_to_all(spread, 'lon', 0, 0)  10.7 us
    all_to_all x1, starting transfers between devices, spread_over(): joined = lax.all_to_all(copies, 'lat', 0, 0, axis_index_groups=members)  10.5 us
    all_to_all x3, starting transfers between devices, exchanged(): lax.all_to_all(block, 'lat', 0, 0, axis_index_groups=groups((dim,), facto...  10.2 us
    ppermute x2, waiting for transfers between devices, doubled(): return jnp.concatenate([block, lax.ppermute(block, 'lat', pairs)], axis=0)  10.1 us
    all_to_all x3, waiting for transfers between devices, exchanged(): lax.all_to_all(block, 'lat', 0, 0, axis_index_groups=groups((dim,), facto...  9.2 us
  transfers between devices with their start and end apart: 17, of which 8 were waited for; matrix products, arithmetic and copies ran while one was open for 3% of the time, Pallas kernels for 3%

profile of v6, /device:TPU:1, one launch (start us, length us, event | category | flops | bytes accessed | tf_op | source)
XLA Modules:
  0.0 167.0 jit_solution(11028587182018464056)
XLA Ops:
  4.3 10.5 %all-to-all-start = ((bf16[32,2,1152]{2,1,0:T(2,128)(2,1)}), bf16[32,2,1152]{2,1,0:T(2,128)(2,1)S(1)}, u32[]{:S(2)}, u32[]{:S(2)}) async-start(bf16[32,2,1152]{2,1,0:T(2,128)(2,1)} %reshape.181), calls=%async_computation | async-start | bytes 294912 | tf_op jit(solution)/shard_map/all_to_all | solution.py:60
  14.8 11.5 %collective-permute-start = (bf16[4,12,256]{2,1,0:T(8,128)(2,1)S(1)}, bf16[4,12,256]{2,1,0:T(8,128)(2,1)S(1)}, u32[]{:S(2)}, u32[]{:S(2)}) collective-permute-start(bf16[4,12,256]{2,1,0:T(8,128)(2,1)S(1)} %get-tuple-element.36), channel_id=1, source_target_pairs={{1,2},{2,1},{3,4},{4,3},{5,6},{6,5},{7,0},{0,7},{9,10},{10,9},{11,... | collective-permute-start | bytes 73736 | tf_op jit(solution)/shard_map/ppermute | solution.py:54
  26.3 8.7 %collective-permute-start.1 = (bf16[4,12,256]{2,1,0:T(8,128)(2,1)S(1)}, bf16[4,12,256]{2,1,0:T(8,128)(2,1)S(1)}, u32[]{:S(2)}, u32[]{:S(2)}) collective-permute-start(bf16[4,12,256]{2,1,0:T(8,128)(2,1)S(1)} %get-tuple-element.37), channel_id=1, source_target_pairs={{0,1},{1,0},{2,3},{3,2},{4,5},{5,4},{6,7},{7,6},{8,9},{9,8},{10,11... | collective-permute-start | bytes 73736 | tf_op jit(solution)/shard_map/ppermute | solution.py:54
  39.3 3.1 %collective-permute-start.3 = (bf16[32,2304]{1,0:T(8,128)(2,1)S(1)}, bf16[32,2304]{1,0:T(8,128)(2,1)S(1)}, u32[]{:S(2)}, u32[]{:S(2)}) collective-permute-start(bf16[32,2304]{1,0:T(8,128)(2,1)S(1)} %bitcast.29), channel_id=1, source_target_pairs={{0,256},{8,264},{16,272},{24,280},{32,288},{40,296},{48,304},{56,3... | collective-permute-start | bytes 442376 | tf_op jit(solution)/shard_map/ppermute | solution.py:67
  44.7 5.8 %collective-permute-start.4 = (bf16[4,96,256]{2,1,0:T(8,128)(2,1)S(1)}, bf16[4,96,256]{2,1,0:T(8,128)(2,1)S(1)}, u32[]{:S(2)}, u32[]{:S(2)}) collective-permute-start(bf16[4,96,256]{2,1,0:T(8,128)(2,1)S(1)} %pad_maximum_fusion.3.refs_5_), channel_id=1, source_target_pairs={{0,24},{8,32},{16,40},{24,48},{32,56},{40,64},{48,72},{56,80},{64,... | collective-permute-start | bytes 589832 | tf_op jit(solution)/shard_map/ppermute | solution.py:41
  50.5 5.2 %collective-permute-start.5 = (bf16[4,96,256]{2,1,0:T(8,128)(2,1)S(1)}, bf16[4,96,256]{2,1,0:T(8,128)(2,1)S(1)}, u32[]{:S(2)}, u32[]{:S(2)}) collective-permute-start(bf16[4,96,256]{2,1,0:T(8,128)(2,1)S(1)} %pad_maximum_fusion.3.refs_5_), channel_id=1, source_target_pairs={{0,16},{8,24},{16,32},{24,40},{32,48},{40,56},{48,64},{56,72},{64,... | collective-permute-start | bytes 589832 | tf_op jit(solution)/shard_map/ppermute | solution.py:41
  55.8 2.2 %collective-permute-start.6 = (bf16[4,96,256]{2,1,0:T(8,128)(2,1)S(1)}, bf16[4,96,256]{2,1,0:T(8,128)(2,1)S(1)}, u32[]{:S(2)}, u32[]{:S(2)}) collective-permute-start(bf16[4,96,256]{2,1,0:T(8,128)(2,1)S(1)} %pad_maximum_fusion.3.refs_5_), channel_id=1, source_target_pairs={{0,8},{8,16},{16,24},{24,32},{32,40},{40,48},{48,56},{56,64},{64,7... | collective-permute-start | bytes 589832 | tf_op jit(solution)/shard_map/ppermute | solution.py:41
  60.6 6.2 %collective-permute-done.5.refs_3_ = bf16[4,96,256]{2,1,0:T(8,128)(2,1)S(1)} collective-permute-done((bf16[4,96,256]{2,1,0:T(8,128)(2,1)S(1)}, bf16[4,96,256]{2,1,0:T(8,128)(2,1)S(1)}, u32[]{:S(2)}, u32[]{:S(2)}) %collective-permute-start.5) | collective-permute-done | bytes 196640 | tf_op jit(solution)/shard_map/ppermute | solution.py:41
  66.8 8.5 %collective-permute-done.6.refs_4_ = bf16[4,96,256]{2,1,0:T(8,128)(2,1)S(1)} collective-permute-done((bf16[4,96,256]{2,1,0:T(8,128)(2,1)S(1)}, bf16[4,96,256]{2,1,0:T(8,128)(2,1)S(1)}, u32[]{:S(2)}, u32[]{:S(2)}) %collective-permute-start.6) | collective-permute-done | bytes 196640 | tf_op jit(solution)/shard_map/ppermute | solution.py:41
  75.3 15.9 %collective-permute-done.7.refs_7_ = bf16[4,96,256]{2,1,0:T(8,128)(2,1)S(1)} collective-permute-done((bf16[4,96,256]{2,1,0:T(8,128)(2,1)S(1)}, bf16[4,96,256]{2,1,0:T(8,128)(2,1)S(1)}, u32[]{:S(2)}, u32[]{:S(2)}) %collective-permute-start.7) | collective-permute-done | bytes 196640 | tf_op jit(solution)/shard_map/ppermute | solution.py:41
  92.6 5.1 %features.1 = (bf16[9,288,256]{2,1,0:T(8,128)(2,1)}, bf16[128,2304]{1,0:T(8,128)(2,1)}, bf16[128,2304]{1,0:T(8,128)(2,1)}) custom-call(bf16[288,896]{1,0:T(8,128)(2,1)} %shard_map.68.refs_0_, bf16[256,288]{1,0:T(8,128)(2,1)} %convolution_convert_fusion.refs_1_, bf16[4,96,256]{2,1,0:T(8,128)(2,1)} %copy-done.7, bf16[4,96,256]{2,1,0:T(8,128)(2,1)} %copy-done.8, ...), custom_call_target="tpu_custom_call" | custom-call | tf_op jit(solution)/shard_map/features/pallas_call | solution.py:190
  97.7 2.4 %collective-permute-start.9 = (bf16[128,2304]{1,0:T(8,128)(2,1)}, bf16[128,2304]{1,0:T(8,128)(2,1)S(1)}, u32[]{:S(2)}, u32[]{:S(2)}) collective-permute-start(bf16[128,2304]{1,0:T(8,128)(2,1)} %get-tuple-element.23), channel_id=1, source_target_pairs={{0,1},{1,0},{2,3},{3,2},{4,5},{5,4},{6,7},{7,6},{8,9},{9,8},{10,11... | collective-permute-start | bytes 1769480 | tf_op jit(solution)/shard_map/ppermute | solution.py:36
  102.0 2.0 %add_convert_fusion = bf16[128,2304]{1,0:T(8,128)(2,1)} fusion(bf16[128,2304]{1,0:T(8,128)(2,1)S(1)} %collective-permute-done.9, bf16[128,2304]{1,0:T(8,128)(2,1)} %get-tuple-element.22), kind=kLoop, calls=%fused_computation | loop fusion | flops 1179648 | bytes 1769472 | tf_op jit(solution)/shard_map/convert_element_type | solution.py:209
  104.0 4.5 %collective-permute-start.10 = (bf16[64,2304]{1,0:T(8,128)(2,1)S(1)}, bf16[64,2304]{1,0:T(8,128)(2,1)S(1)}, u32[]{:S(2)}, u32[]{:S(2)}) collective-permute-start(bf16[64,2304]{1,0:T(8,128)(2,1)S(1)} %pad_maximum_fusion.2), channel_id=1, source_target_pairs={{0,512},{8,520},{16,528},{24,536},{32,544},{40,552},{48,560},{56,5... | collective-permute-start | bytes 884744 | tf_op jit(solution)/shard_map/ppermute | solution.py:67
  108.5 3.5 %all-to-all-start.1 = ((bf16[4,32,2304]{2,1,0:T(8,128)(2,1)}), bf16[4,32,2304]{2,1,0:T(8,128)(2,1)S(1)}, u32[]{:S(2)}, u32[]{:S(2)}) async-start(bf16[4,32,2304]{2,1,0:T(8,128)(2,1)} %bitcast.12), calls=%async_computation.1 | async-start | bytes 1179648 | tf_op jit(solution)/shard_map/all_to_all | solution.py:207
  112.0 10.1 %collective-permute-done.10 = bf16[64,2304]{1,0:T(8,128)(2,1)S(1)} collective-permute-done((bf16[64,2304]{1,0:T(8,128)(2,1)S(1)}, bf16[64,2304]{1,0:T(8,128)(2,1)S(1)}, u32[]{:S(2)}, u32[]{:S(2)}) %collective-permute-start.10) | collective-permute-done | bytes 294944 | tf_op jit(solution)/shard_map/ppermute | solution.py:67
  123.0 3.3 %all-to-all-start.2 = ((bf16[4,8,2304]{2,1,0:T(8,128)(2,1)}), bf16[4,8,2304]{2,1,0:T(8,128)(2,1)S(1)}, u32[]{:S(2)}, u32[]{:S(2)}) async-start(bf16[4,8,2304]{2,1,0:T(8,128)(2,1)} %bitcast.13), calls=%async_computation.2 | async-start | bytes 294912 | tf_op jit(solution)/shard_map/all_to_all | solution.py:207
  126.3 2.8 %collective-permute-start.11 = (bf16[128,2304]{1,0:T(8,128)(2,1)S(1)}, bf16[128,2304]{1,0:T(8,128)(2,1)S(1)}, u32[]{:S(2)}, u32[]{:S(2)}) collective-permute-start(bf16[128,2304]{1,0:T(8,128)(2,1)S(1)} %pad_maximum_fusion.1.refs_1_), channel_id=1, source_target_pairs={{0,1},{1,0},{2,3},{3,2},{4,5},{5,4},{6,7},{7,6},{8,9},{9,8},{10,11... | collective-permute-start | bytes 1769480 | tf_op jit(solution)/shard_map/ppermute | solution.py:36
  129.1 2.0 %all-to-all-done.2 = bf16[4,8,2304]{2,1,0:T(8,128)(2,1)S(1)} async-done(((bf16[4,8,2304]{2,1,0:T(8,128)(2,1)}), bf16[4,8,2304]{2,1,0:T(8,128)(2,1)S(1)}, u32[]{:S(2)}, u32[]{:S(2)}) %all-to-all-start.2) | async-done | bytes 147488 | tf_op jit(solution)/shard_map/all_to_all | solution.py:207
  131.9 3.4 %all-to-all-start.3 = ((f32[8,1,2304]{2,1,0:T(1,128)}), f32[8,1,2304]{2,1,0:T(1,128)S(1)}, u32[]{:S(2)}, u32[]{:S(2)}) async-start(f32[8,1,2304]{2,1,0:T(1,128)} %copy.43), calls=%async_computation.3 | async-start | bytes 147456 | tf_op jit(solution)/shard_map/all_to_all | solution.py:207
  135.3 7.2 %all-to-all-done.3 = f32[8,1,2304]{2,1,0:T(1,128)S(1)} async-done(((f32[8,1,2304]{2,1,0:T(1,128)}), f32[8,1,2304]{2,1,0:T(1,128)S(1)}, u32[]{:S(2)}, u32[]{:S(2)}) %all-to-all-start.3) | async-done | bytes 73760 | tf_op jit(solution)/shard_map/all_to_all | solution.py:207
  143.2 10.7 %all-to-all-start.4 = ((f32[8,1,2304]{2,1,0:T(1,128)}), f32[8,1,2304]{2,1,0:T(1,128)S(1)}, u32[]{:S(2)}, u32[]{:S(2)}) async-start(f32[8,1,2304]{2,1,0:T(1,128)} %broadcast_in_dim.27), calls=%async_computation.4 | async-start | bytes 147456 | tf_op jit(solution)/shard_map/all_to_all | solution.py:238
  155.4 3.0 %mixing.1 = bf16[4,72,256]{2,1,0:T(8,128)(2,1)} custom-call(bf16[9,288,256]{2,1,0:T(8,128)(2,1)} %get-tuple-element.28.refs_0_, bf16[128,2304]{1,0:T(8,128)(2,1)} %copy-done.1, bf16[128,2304]{1,0:T(8,128)(2,1)} %copy-done.3, bf16[256,256]{1,0:T(8,128)(2,1)} %fusion.refs_3_), custom_call_target="tpu_custom_call" | custom-call | flops 377487360 | bytes 5308416 | tf_op jit(solution)/shard_map/mixing/pallas_call | solution.py:227
  158.5 7.6 %all-to-all-done.4 = f32[8,1,2304]{2,1,0:T(1,128)S(1)} async-done(((f32[8,1,2304]{2,1,0:T(1,128)}), f32[8,1,2304]{2,1,0:T(1,128)S(1)}, u32[]{:S(2)}, u32[]{:S(2)}) %all-to-all-start.4) | async-done | bytes 73760 | tf_op jit(solution)/shard_map/all_to_all | solution.py:238
  (77 shorter events, 20.6 us)
Async XLA Ops:
  0.7 34.4 %copy-start.13 = (s32[4,25]{1,0:T(4,128)S(1)}, s32[4,25]{1,0:T(4,128)}, u32[]{:S(2)}) copy-start(s32[4,25]{1,0:T(4,128)} %param.7) | copy-start | bytes 1204
  0.7 34.5 %copy-start.5 = (bf16[4,25,9,25]{3,0,2,1:T(4,128)(2,1)S(1)}, bf16[4,25,9,25]{3,0,2,1:T(4,128)(2,1)}, u32[]{:S(2)}) copy-start(bf16[4,25,9,25]{3,0,2,1:T(4,128)(2,1)} %param.6) | copy-start | bytes 135004
  4.3 34.9 %all-to-all-start = ((bf16[32,2,1152]{2,1,0:T(2,128)(2,1)}), bf16[32,2,1152]{2,1,0:T(2,128)(2,1)S(1)}, u32[]{:S(2)}, u32[]{:S(2)}) async-start(bf16[32,2,1152]{2,1,0:T(2,128)(2,1)} %reshape.181), calls=%async_computation | async-start | bytes 294912 | tf_op jit(solution)/shard_map/all_to_all | solution.py:60
  14.8 24.3 %collective-permute-start = (bf16[4,12,256]{2,1,0:T(8,128)(2,1)S(1)}, bf16[4,12,256]{2,1,0:T(8,128)(2,1)S(1)}, u32[]{:S(2)}, u32[]{:S(2)}) collective-permute-start(bf16[4,12,256]{2,1,0:T(8,128)(2,1)S(1)} %get-tuple-element.36), channel_id=1, source_target_pairs={{1,2},{2,1},{3,4},{4,3},{5,6},{6,5},{7,0},{0,7},{9,10},{10,9},{11,... | collective-permute-start | bytes 73736 | tf_op jit(solution)/shard_map/ppermute | solution.py:54
  26.3 12.8 %collective-permute-start.1 = (bf16[4,12,256]{2,1,0:T(8,128)(2,1)S(1)}, bf16[4,12,256]{2,1,0:T(8,128)(2,1)S(1)}, u32[]{:S(2)}, u32[]{:S(2)}) collective-permute-start(bf16[4,12,256]{2,1,0:T(8,128)(2,1)S(1)} %get-tuple-element.37), channel_id=1, source_target_pairs={{0,1},{1,0},{2,3},{3,2},{4,5},{5,4},{6,7},{7,6},{8,9},{9,8},{10,11... | collective-permute-start | bytes 73736 | tf_op jit(solution)/shard_map/ppermute | solution.py:54
  39.2 52.1 %copy-start.2 = (bf16[4,96,256]{2,1,0:T(8,128)(2,1)}, bf16[4,96,256]{2,1,0:T(8,128)(2,1)S(1)}, u32[]{:S(2)}) copy-start(bf16[4,96,256]{2,1,0:T(8,128)(2,1)S(1)} %pad_maximum_fusion.3.refs_5_) | copy-start | bytes 589828
  39.3 18.6 %collective-permute-start.3 = (bf16[32,2304]{1,0:T(8,128)(2,1)S(1)}, bf16[32,2304]{1,0:T(8,128)(2,1)S(1)}, u32[]{:S(2)}, u32[]{:S(2)}) collective-permute-start(bf16[32,2304]{1,0:T(8,128)(2,1)S(1)} %bitcast.29), channel_id=1, source_target_pairs={{0,256},{8,264},{16,272},{24,280},{32,288},{40,296},{48,304},{56,3... | collective-permute-start | bytes 442376 | tf_op jit(solution)/shard_map/ppermute | solution.py:67
  42.4 16.8 %collective-permute-start.2 = (bf16[4,96,256]{2,1,0:T(8,128)(2,1)S(1)}, bf16[4,96,256]{2,1,0:T(8,128)(2,1)S(1)}, u32[]{:S(2)}, u32[]{:S(2)}) collective-permute-start(bf16[4,96,256]{2,1,0:T(8,128)(2,1)S(1)} %pad_maximum_fusion.3.refs_5_), channel_id=1, source_target_pairs={{8,0},{16,8},{24,16},{32,24},{40,32},{48,40},{56,48},{64,56},{72,6... | collective-permute-start | bytes 589832 | tf_op jit(solution)/shard_map/ppermute | solution.py:41
  44.7 15.9 %collective-permute-start.4 = (bf16[4,96,256]{2,1,0:T(8,128)(2,1)S(1)}, bf16[4,96,256]{2,1,0:T(8,128)(2,1)S(1)}, u32[]{:S(2)}, u32[]{:S(2)}) collective-permute-start(bf16[4,96,256]{2,1,0:T(8,128)(2,1)S(1)} %pad_maximum_fusion.3.refs_5_), channel_id=1, source_target_pairs={{0,24},{8,32},{16,40},{24,48},{32,56},{40,64},{48,72},{56,80},{64,... | collective-permute-start | bytes 589832 | tf_op jit(solution)/shard_map/ppermute | solution.py:41
  50.5 16.3 %collective-permute-start.5 = (bf16[4,96,256]{2,1,0:T(8,128)(2,1)S(1)}, bf16[4,96,256]{2,1,0:T(8,128)(2,1)S(1)}, u32[]{:S(2)}, u32[]{:S(2)}) collective-permute-start(bf16[4,96,256]{2,1,0:T(8,128)(2,1)S(1)} %pad_maximum_fusion.3.refs_5_), channel_id=1, source_target_pairs={{0,16},{8,24},{16,32},{24,40},{32,48},{40,56},{48,64},{56,72},{64,... | collective-permute-start | bytes 589832 | tf_op jit(solution)/shard_map/ppermute | solution.py:41
  55.8 19.5 %collective-permute-start.6 = (bf16[4,96,256]{2,1,0:T(8,128)(2,1)S(1)}, bf16[4,96,256]{2,1,0:T(8,128)(2,1)S(1)}, u32[]{:S(2)}, u32[]{:S(2)}) collective-permute-start(bf16[4,96,256]{2,1,0:T(8,128)(2,1)S(1)} %pad_maximum_fusion.3.refs_5_), channel_id=1, source_target_pairs={{0,8},{8,16},{16,24},{24,32},{32,40},{40,48},{48,56},{56,64},{64,7... | collective-permute-start | bytes 589832 | tf_op jit(solution)/shard_map/ppermute | solution.py:41
  58.0 33.2 %collective-permute-start.7 = (bf16[4,96,256]{2,1,0:T(8,128)(2,1)S(1)}, bf16[4,96,256]{2,1,0:T(8,128)(2,1)S(1)}, u32[]{:S(2)}, u32[]{:S(2)}) collective-permute-start(bf16[4,96,256]{2,1,0:T(8,128)(2,1)S(1)} %pad_maximum_fusion.3.refs_5_), channel_id=1, source_target_pairs={{16,0},{24,8},{32,16},{40,24},{48,32},{56,40},{64,48},{72,56},{80,... | collective-permute-start | bytes 589832 | tf_op jit(solution)/shard_map/ppermute | solution.py:41
  59.3 31.9 %copy-start.6 = (bf16[4,96,256]{2,1,0:T(8,128)(2,1)}, bf16[4,96,256]{2,1,0:T(8,128)(2,1)S(1)}, u32[]{:S(2)}) copy-start(bf16[4,96,256]{2,1,0:T(8,128)(2,1)S(1)} %collective-permute-done.2.refs_6_) | copy-start | bytes 589828
  59.3 31.9 %collective-permute-start.8 = (bf16[4,96,256]{2,1,0:T(8,128)(2,1)S(1)}, bf16[4,96,256]{2,1,0:T(8,128)(2,1)S(1)}, u32[]{:S(2)}, u32[]{:S(2)}) collective-permute-start(bf16[4,96,256]{2,1,0:T(8,128)(2,1)S(1)} %pad_maximum_fusion.3.refs_5_), channel_id=1, source_target_pairs={{24,0},{32,8},{40,16},{48,24},{56,32},{64,40},{72,48},{80,56},{88,... | collective-permute-start | bytes 589832 | tf_op jit(solution)/shard_map/ppermute | solution.py:41
  60.6 30.6 %copy-start.7 = (bf16[4,96,256]{2,1,0:T(8,128)(2,1)}, bf16[4,96,256]{2,1,0:T(8,128)(2,1)S(1)}, u32[]{:S(2)}) copy-start(bf16[4,96,256]{2,1,0:T(8,128)(2,1)S(1)} %collective-permute-done.4.refs_2_) | copy-start | bytes 589828
  66.8 24.4 %copy-start.8 = (bf16[4,96,256]{2,1,0:T(8,128)(2,1)}, bf16[4,96,256]{2,1,0:T(8,128)(2,1)S(1)}, u32[]{:S(2)}) copy-start(bf16[4,96,256]{2,1,0:T(8,128)(2,1)S(1)} %collective-permute-done.5.refs_3_) | copy-start | bytes 589828
  97.7 4.3 %collective-permute-start.9 = (bf16[128,2304]{1,0:T(8,128)(2,1)}, bf16[128,2304]{1,0:T(8,128)(2,1)S(1)}, u32[]{:S(2)}, u32[]{:S(2)}) collective-permute-start(bf16[128,2304]{1,0:T(8,128)(2,1)} %get-tuple-element.23), channel_id=1, source_target_pairs={{0,1},{1,0},{2,3},{3,2},{4,5},{5,4},{6,7},{7,6},{8,9},{9,8},{10,11... | collective-permute-start | bytes 1769480 | tf_op jit(solution)/shard_map/ppermute | solution.py:36
  104.0 18.0 %collective-permute-start.10 = (bf16[64,2304]{1,0:T(8,128)(2,1)S(1)}, bf16[64,2304]{1,0:T(8,128)(2,1)S(1)}, u32[]{:S(2)}, u32[]{:S(2)}) collective-permute-start(bf16[64,2304]{1,0:T(8,128)(2,1)S(1)} %pad_maximum_fusion.2), channel_id=1, source_target_pairs={{0,512},{8,520},{16,528},{24,536},{32,544},{40,552},{48,560},{56,5... | collective-permute-start | bytes 884744 | tf_op jit(solution)/shard_map/ppermute | solution.py:67
  108.5 13.6 %all-to-all-start.1 = ((bf16[4,32,2304]{2,1,0:T(8,128)(2,1)}), bf16[4,32,2304]{2,1,0:T(8,128)(2,1)S(1)}, u32[]{:S(2)}, u32[]{:S(2)}) async-start(bf16[4,32,2304]{2,1,0:T(8,128)(2,1)} %bitcast.12), calls=%async_computation.1 | async-start | bytes 1179648 | tf_op jit(solution)/shard_map/all_to_all | solution.py:207
  122.1 32.5 %copy-start.1 = (bf16[128,2304]{1,0:T(8,128)(2,1)}, bf16[128,2304]{1,0:T(8,128)(2,1)S(1)}, u32[]{:S(2)}) copy-start(bf16[128,2304]{1,0:T(8,128)(2,1)S(1)} %pad_maximum_fusion.1.refs_1_) | copy-start | bytes 1769476
  123.0 8.2 %all-to-all-start.2 = ((bf16[4,8,2304]{2,1,0:T(8,128)(2,1)}), bf16[4,8,2304]{2,1,0:T(8,128)(2,1)S(1)}, u32[]{:S(2)}, u32[]{:S(2)}) async-start(bf16[4,8,2304]{2,1,0:T(8,128)(2,1)} %bitcast.13), calls=%async_computation.2 | async-start | bytes 294912 | tf_op jit(solution)/shard_map/all_to_all | solution.py:207
  126.3 28.3 %collective-permute-start.11 = (bf16[128,2304]{1,0:T(8,128)(2,1)S(1)}, bf16[128,2304]{1,0:T(8,128)(2,1)S(1)}, u32[]{:S(2)}, u32[]{:S(2)}) collective-permute-start(bf16[128,2304]{1,0:T(8,128)(2,1)S(1)} %pad_maximum_fusion.1.refs_1_), channel_id=1, source_target_pairs={{0,1},{1,0},{2,3},{3,2},{4,5},{5,4},{6,7},{7,6},{8,9},{9,8},{10,11... | collective-permute-start | bytes 1769480 | tf_op jit(solution)/shard_map/ppermute | solution.py:36
  131.9 10.6 %all-to-all-start.3 = ((f32[8,1,2304]{2,1,0:T(1,128)}), f32[8,1,2304]{2,1,0:T(1,128)S(1)}, u32[]{:S(2)}, u32[]{:S(2)}) async-start(f32[8,1,2304]{2,1,0:T(1,128)} %copy.43), calls=%async_computation.3 | async-start | bytes 147456 | tf_op jit(solution)/shard_map/all_to_all | solution.py:207
  143.2 22.9 %all-to-all-start.4 = ((f32[8,1,2304]{2,1,0:T(1,128)}), f32[8,1,2304]{2,1,0:T(1,128)S(1)}, u32[]{:S(2)}, u32[]{:S(2)}) async-start(f32[8,1,2304]{2,1,0:T(1,128)} %broadcast_in_dim.27), calls=%async_computation.4 | async-start | bytes 147456 | tf_op jit(solution)/shard_map/all_to_all | solution.py:238
  (7 other events, 33.9 us)

commit v7 on v4

--- a/solution.py
+++ b/solution.py
@@ -7,7 +7,7 @@
 from jax.experimental.pallas import tpu as pltpu
 from jax.sharding import PartitionSpec as P
 
-FACTORS = {128: (4, 4, 8), 16: (2, 2, 4)}
+FACTORS = {128: (4, 4, 8), 16: (4, 1, 4)}
 TILE = 8
 
 
@@ -34,6 +34,11 @@
 
 def swapped_core(block):
     return lax.ppermute(block, "lon", [(i, i ^ 1) for i in range(lax.axis_size("lon"))])
+
+
+def passed_along(block, by):
+    count = lax.axis_size("lat")
+    return lax.ppermute(block, "lat", [(i, i + by) for i in range(count) if 0 <= i + by < count])
 
 
 def paired(block, axis, first, loop):
@@ -47,12 +52,6 @@
             high = 0
         pairs += [(low, high), (high, low)]
     return lax.ppermute(block, axis, pairs)
-
-
-def spread_over(block, dim, factors):
-    copies = jnp.broadcast_to(block, (factors[dim],) + block.shape)
-    joined = lax.all_to_all(copies, "lat", 0, 0, axis_index_groups=groups((dim,), factors))
-    return joined.reshape(-1, block.shape[1])
 
 
 def band_kernel(rows_ref, band_ref):
@@ -128,8 +127,6 @@
     cells = rows * cols
     bf16 = jnp.bfloat16
 
-    gathered = spread_over(lax.dynamic_slice_in_dim(weight, core, 1, 0), 1, factors)
-
     offsets = jnp.arange(width) - reach
     validity = jnp.abs(offsets)[None, None, :] <= spans[:, :, None]
     masked = jnp.where(validity[:, :, None, :], basis, jnp.zeros_like(basis))
@@ -140,9 +137,7 @@
             for row in range(rows)
         ],
         axis=1,
-    ).reshape(nbasis * rows, window_rows // rows, rows * window_cols)
-    band_rows = jnp.where(lat % 2 == 0, band_rows[:, ::-1], band_rows)
-    band_rows = band_rows.reshape(nbasis * rows, window_rows * window_cols)
+    ).reshape(nbasis * rows, window_rows * window_cols)
     band = pl.pallas_call(
         band_kernel,
         out_shape=jax.ShapeDtypeStruct((nbasis * rows * TILE, window_rows * window_cols), bf16),
@@ -170,16 +165,12 @@
     left = jnp.where(core == 0, far_edge, near_edge)
     right = jnp.where(core == 0, near_edge, far_edge)
     own = jnp.concatenate([left, fields, right], axis=1)
-    own, gathered = lax.optimization_barrier((own, gathered))
-    near, far = own, own
-    nears, fars = [], []
-    for turn in range(3):
-        if turn == 2:
-            near, far, band, cot = lax.optimization_barrier((near, far, band, cot))
-        near, far = paired(far, "lat", 0, False), paired(near, "lat", 1, False)
-        nears.append(near)
-        fars.append(far)
-    windows = nears[::-1] + [own] + fars
+    windows = {0: own}
+    for by in (3, -3, 2, -2, 1, -1):
+        windows[by] = passed_along(own, by)
+
+    windows[-1], band, cot = lax.optimization_barrier((windows[-1], band, cot))
+    pieces = [windows[by] for by in (3, 2, 1, 0, -1, -2, -3)]
 
     features, keep, send = pl.pallas_call(
         lambda *refs: feature_kernel(nbasis, tile_count, *refs),
@@ -191,7 +182,7 @@
         in_specs=vmem(9),
         out_specs=tuple(vmem(3)),
         name="features",
-    )(band, cot, *windows)
+    )(band, cot, *pieces)
 
     f32 = jnp.float32
     length = nbasis * channels
@@ -201,7 +192,15 @@
         return lax.all_to_all(block, "lat", 0, 0, axis_index_groups=groups((dim,), factors))
 
     total = (keep.astype(f32) + swapped_core(send).astype(f32)).astype(bf16)
-    total = jnp.sum(exchanged(total, 1).astype(f32), axis=0).astype(bf16)
+    count = zs * ys
+    column = -(-length // count // 128) * 128
+    mine = lax.dynamic_slice_in_dim(weight, core, 1, 0)
+    folded = jnp.pad(mine, ((0, 0), (0, count * column - length))).reshape(1, count, column)
+    folded = jnp.broadcast_to(folded, (xs, count, column))
+    total = total.reshape(xs, count, length)
+    arrived = exchanged(jnp.concatenate([total, folded], axis=2), 1)
+    total = jnp.sum(arrived[:, :, :length].astype(f32), axis=0).astype(bf16)
+    gathered = arrived[:, :, length:].reshape(xs, count * column)[:, :length]
 
     total = total.reshape(zs, ys, length)
     folded = jnp.concatenate([gathered[:, : length // 2], gathered[:, length // 2 :]], axis=0)

time: 159 us -> 160 us (level)
  starting transfers between devices: 71 us -> 54.5 us
  waiting for transfers between devices: 27.3 us -> 40.8 us
  blocking collectives: 34.5 us -> 41.3 us
    ppermute x0 -> x6, waiting for transfers between devices: none -> 30.3 us  [passed_along(): lax.ppermute(block, 'lat', [(i, i + by) for i in range(count) if 0 <= i +...]
    ppermute x0 -> x6, starting transfers between devices: none -> 17.6 us  [passed_along(): lax.ppermute(block, 'lat', [(i, i + by) for i in range(count) if 0 <= i +...]
    ppermute x8 -> x2, starting transfers between devices: 36.9 us -> 21 us  [paired(): return lax.ppermute(block, axis, pairs)]
    all_to_all x2 -> x0, starting transfers between devices: 14.6 us -> none  [the longest x1 10.6 us: exchanged(): lax.all_to_all(block, 'lat', 0, 0, axis_index_groups=groups((dim,), facto...]
    all_to_all x2 -> x0, waiting for transfers between devices: 11.5 us -> none  [the longest x1 9.57 us: exchanged(): lax.all_to_all(block, 'lat', 0, 0, axis_index_groups=groups((dim,), facto...]
    all_to_all x2 -> x3, blocking collectives: 34.5 us -> 41.3 us  [exchanged(): lax.all_to_all(block, 'lat', 0, 0, axis_index_groups=groups((dim,), facto...]
    ppermute x8 -> x2, waiting for transfers between devices: 5.21 us -> 0.01 us  [paired(): return lax.ppermute(block, axis, pairs)]
    ppermute x2, starting transfers between devices: 12.1 us -> 8.87 us  [swapped_core(): lax.ppermute(block, 'lon', [(i, i ^ 1) for i in range(lax.axis_size('lon'...]
  transfers between devices with their start and end apart: 13 -> 11, of which waited for: 6 -> 5; matrix products, arithmetic and copies ran while one was open for 5% -> 3% of each run, Pallas kernels for 3% -> 3%
where the time goes in v7:
time: 160 us; the launch traced here: 159 us
  starting transfers between devices  54.5 us (34%)
  blocking collectives  41.3 us (26%)
  waiting for transfers between devices  40.8 us (25%)
  Pallas kernels  10.1 us (6%)
  other arithmetic  5.79 us (4%)
  local copies, waits for them, and re-layouts  5.02 us (3%)
    all_to_all x3, blocking collectives, exchanged(): lax.all_to_all(block, 'lat', 0, 0, axis_index_groups=groups((dim,), facto...  41.3 us
    ppermute x6, waiting for transfers between devices, passed_along(): lax.ppermute(block, 'lat', [(i, i + by) for i in range(count) if 0 <= i +...  30.3 us
    ppermute x2, starting transfers between devices, paired(): return lax.ppermute(block, axis, pairs)  21 us
    ppermute x6, starting transfers between devices, passed_along(): lax.ppermute(block, 'lat', [(i, i + by) for i in range(count) if 0 <= i +...  17.6 us
    ppermute x2, starting transfers between devices, swapped_core(): lax.ppermute(block, 'lon', [(i, i ^ 1) for i in range(lax.axis_size('lon'...  8.87 us
    all_to_all x1, waiting for transfers between devices, shards(): arrived = lax.all_to_all(spread, 'lon', 0, 0)  8.75 us
    all_to_all x1, starting transfers between devices, shards(): arrived = lax.all_to_all(spread, 'lon', 0, 0)  6.92 us
    pallas_call x1, Pallas kernels, shards(): pl.pallas_call(lambda *refs: feature_kernel(nbasis, tile_count, *refs), o...  5.13 us
  transfers between devices with their start and end apart: 11, of which 5 were waited for; matrix products, arithmetic and copies ran while one was open for 3% of the time, Pallas kernels for 3%

profile of v7, /device:TPU:1, one launch (start us, length us, event | category | flops | bytes accessed | tf_op | source)
XLA Modules:
  0.0 159.4 jit_solution(9442785443085160903)
XLA Ops:
  1.5 12.0 %collective-permute-start = (bf16[4,12,256]{2,1,0:T(8,128)(2,1)S(1)}, bf16[4,12,256]{2,1,0:T(8,128)(2,1)S(1)}, u32[]{:S(2)}, u32[]{:S(2)}) collective-permute-start(bf16[4,12,256]{2,1,0:T(8,128)(2,1)S(1)} %get-tuple-element.24), channel_id=1, source_target_pairs={{1,2},{2,1},{3,4},{4,3},{5,6},{6,5},{7,0},{0,7},{9,10},{10,9},{11,... | collective-permute-start | bytes 73736 | tf_op jit(solution)/shard_map/ppermute | solution.py:54
  13.5 9.0 %collective-permute-start.1 = (bf16[4,12,256]{2,1,0:T(8,128)(2,1)S(1)}, bf16[4,12,256]{2,1,0:T(8,128)(2,1)S(1)}, u32[]{:S(2)}, u32[]{:S(2)}) collective-permute-start(bf16[4,12,256]{2,1,0:T(8,128)(2,1)S(1)} %get-tuple-element.25), channel_id=1, source_target_pairs={{0,1},{1,0},{2,3},{3,2},{4,5},{5,4},{6,7},{7,6},{8,9},{9,8},{10,11... | collective-permute-start | bytes 73736 | tf_op jit(solution)/shard_map/ppermute | solution.py:54
  23.3 1.0 convert_bitcast_fusion
  25.4 1.3 collective-permute-start.2
  27.7 1.9 %shard_map.68.refs_0_ = bf16[288,896]{1,0:T(8,128)(2,1)} custom-call(f32[36,896]{1,0:T(8,128)} %reshape.175.rows_ref), custom_call_target="tpu_custom_call" | custom-call | tf_op jit(solution)/shard_map/pallas_call | solution.py:141
  29.6 6.0 %collective-permute-start.3 = (bf16[4,96,256]{2,1,0:T(8,128)(2,1)S(1)}, bf16[4,96,256]{2,1,0:T(8,128)(2,1)S(1)}, u32[]{:S(2)}, u32[]{:S(2)}) collective-permute-start(bf16[4,96,256]{2,1,0:T(8,128)(2,1)S(1)} %pad_maximum_fusion.4.refs_5_), channel_id=1, source_target_pairs={{0,24},{8,32},{16,40},{24,48},{32,56},{40,64},{48,72},{56,80},{64,... | collective-permute-start | bytes 589832 | tf_op jit(solution)/shard_map/ppermute | solution.py:41
  35.6 5.4 %collective-permute-start.4 = (bf16[4,96,256]{2,1,0:T(8,128)(2,1)S(1)}, bf16[4,96,256]{2,1,0:T(8,128)(2,1)S(1)}, u32[]{:S(2)}, u32[]{:S(2)}) collective-permute-start(bf16[4,96,256]{2,1,0:T(8,128)(2,1)S(1)} %pad_maximum_fusion.4.refs_5_), channel_id=1, source_target_pairs={{0,16},{8,24},{16,32},{24,40},{32,48},{40,56},{48,64},{56,72},{64,... | collective-permute-start | bytes 589832 | tf_op jit(solution)/shard_map/ppermute | solution.py:41
  41.0 2.3 %collective-permute-start.5 = (bf16[4,96,256]{2,1,0:T(8,128)(2,1)S(1)}, bf16[4,96,256]{2,1,0:T(8,128)(2,1)S(1)}, u32[]{:S(2)}, u32[]{:S(2)}) collective-permute-start(bf16[4,96,256]{2,1,0:T(8,128)(2,1)S(1)} %pad_maximum_fusion.4.refs_5_), channel_id=1, source_target_pairs={{0,8},{8,16},{16,24},{24,32},{32,40},{40,48},{48,56},{56,64},{64,7... | collective-permute-start | bytes 589832 | tf_op jit(solution)/shard_map/ppermute | solution.py:41
  43.4 1.3 collective-permute-start.6
  44.7 1.3 collective-permute-start.7
  47.0 5.4 %collective-permute-done.4.refs_3_ = bf16[4,96,256]{2,1,0:T(8,128)(2,1)S(1)} collective-permute-done((bf16[4,96,256]{2,1,0:T(8,128)(2,1)S(1)}, bf16[4,96,256]{2,1,0:T(8,128)(2,1)S(1)}, u32[]{:S(2)}, u32[]{:S(2)}) %collective-permute-start.4) | collective-permute-done | bytes 196640 | tf_op jit(solution)/shard_map/ppermute | solution.py:41
  52.3 8.4 %collective-permute-done.5.refs_4_ = bf16[4,96,256]{2,1,0:T(8,128)(2,1)S(1)} collective-permute-done((bf16[4,96,256]{2,1,0:T(8,128)(2,1)S(1)}, bf16[4,96,256]{2,1,0:T(8,128)(2,1)S(1)}, u32[]{:S(2)}, u32[]{:S(2)}) %collective-permute-start.5) | collective-permute-done | bytes 196640 | tf_op jit(solution)/shard_map/ppermute | solution.py:41
  60.7 16.5 %collective-permute-done.6.refs_7_ = bf16[4,96,256]{2,1,0:T(8,128)(2,1)S(1)} collective-permute-done((bf16[4,96,256]{2,1,0:T(8,128)(2,1)S(1)}, bf16[4,96,256]{2,1,0:T(8,128)(2,1)S(1)}, u32[]{:S(2)}, u32[]{:S(2)}) %collective-permute-start.6) | collective-permute-done | bytes 196640 | tf_op jit(solution)/shard_map/ppermute | solution.py:41
  78.6 5.1 %features.1 = (bf16[9,288,256]{2,1,0:T(8,128)(2,1)}, bf16[128,2304]{1,0:T(8,128)(2,1)}, bf16[128,2304]{1,0:T(8,128)(2,1)}) custom-call(bf16[288,896]{1,0:T(8,128)(2,1)} %shard_map.68.refs_0_, bf16[256,288]{1,0:T(8,128)(2,1)} %convolution_convert_fusion.refs_1_, bf16[4,96,256]{2,1,0:T(8,128)(2,1)} %copy-done.6, bf16[4,96,256]{2,1,0:T(8,128)(2,1)} %copy-done.7, ...), custom_call_target="tpu_custom_call" | custom-call | tf_op jit(solution)/shard_map/features/pallas_call | solution.py:175
  83.7 2.4 %collective-permute-start.8 = (bf16[128,2304]{1,0:T(8,128)(2,1)}, bf16[128,2304]{1,0:T(8,128)(2,1)S(1)}, u32[]{:S(2)}, u32[]{:S(2)}) collective-permute-start(bf16[128,2304]{1,0:T(8,128)(2,1)} %get-tuple-element.14), channel_id=1, source_target_pairs={{0,1},{1,0},{2,3},{3,2},{4,5},{5,4},{6,7},{7,6},{8,9},{9,8},{10,11... | collective-permute-start | bytes 1769480 | tf_op jit(solution)/shard_map/ppermute | solution.py:36
  86.3 1.7 %collective-permute-done.8 = bf16[128,2304]{1,0:T(8,128)(2,1)S(1)} collective-permute-done((bf16[128,2304]{1,0:T(8,128)(2,1)}, bf16[128,2304]{1,0:T(8,128)(2,1)S(1)}, u32[]{:S(2)}, u32[]{:S(2)}) %collective-permute-start.8) | collective-permute-done | bytes 589856 | tf_op jit(solution)/shard_map/ppermute | solution.py:36
  88.0 1.2 add_convert_fusion
  89.3 12.7 %all_to_all.20 = bf16[4,32,2432]{2,1,0:T(8,128)(2,1)S(1)} all-to-all(bf16[4,32,2432]{2,1,0:T(8,128)(2,1)S(1)} %pad_maximum_fusion.1), channel_id=1, replica_groups={{0,64,128,192},{8,72,136,200},{16,80,144,208},{24,88,152,216},{32,96,16..., dimensions={0} | all-to-all | bytes 1245184 | tf_op jit(solution)/shard_map/all_to_all | solution.py:192
  102.2 9.5 %all_to_all.21 = bf16[4,8,3456]{2,1,0:T(8,128)(2,1)S(1)} all-to-all(bf16[4,8,3456]{2,1,0:T(8,128)(2,1)S(1)} %pad_maximum_fusion.3), channel_id=1, replica_groups={{0,256,512,768},{8,264,520,776},{16,272,528,784},{24,280,536,792},{32,2..., dimensions={0} | all-to-all | bytes 442368 | tf_op jit(solution)/shard_map/all_to_all | solution.py:192
  111.9 19.1 %all_to_all.22 = bf16[8,16,2560]{2,1,0:T(8,128)(2,1)S(1)} all-to-all(bf16[8,16,2560]{2,1,0:T(8,128)(2,1)S(1)} %pad_maximum_fusion), channel_id=1, replica_groups={{0,8,16,24,32,40,48,56},{64,72,80,88,96,104,112,120},{128,136,144,152,1..., dimensions={0} | all-to-all | bytes 1310720 | tf_op jit(solution)/shard_map/all_to_all | solution.py:192
  131.1 6.4 %collective-permute-start.9 = (bf16[128,2304]{1,0:T(8,128)(2,1)S(1)}, bf16[128,2304]{1,0:T(8,128)(2,1)S(1)}, u32[]{:S(2)}, u32[]{:S(2)}) collective-permute-start(bf16[128,2304]{1,0:T(8,128)(2,1)S(1)} %slice.80), channel_id=1, source_target_pairs={{0,1},{1,0},{2,3},{3,2},{4,5},{5,4},{6,7},{7,6},{8,9},{9,8},{10,11... | collective-permute-start | bytes 1769480 | tf_op jit(solution)/shard_map/ppermute | solution.py:36
  138.3 6.9 %all-to-all-start.3 = ((f32[8,1,2304]{2,1,0:T(1,128)}), f32[8,1,2304]{2,1,0:T(1,128)S(1)}, u32[]{:S(2)}, u32[]{:S(2)}) async-start(f32[8,1,2304]{2,1,0:T(1,128)} %broadcast_in_dim.40), calls=%async_computation.3 | async-start | bytes 147456 | tf_op jit(solution)/shard_map/all_to_all | solution.py:243
  146.8 3.0 %mixing.1 = bf16[4,72,256]{2,1,0:T(8,128)(2,1)} custom-call(bf16[9,288,256]{2,1,0:T(8,128)(2,1)} %get-tuple-element.15.refs_0_, bf16[128,2560]{1,0:T(8,128)(2,1)} %bitcast.40, bf16[128,2304]{1,0:T(8,128)(2,1)} %copy-done.3, bf16[256,256]{1,0:T(8,128)(2,1)} %fusion.refs_3_), custom_call_target="tpu_custom_call" | custom-call | flops 377487360 | bytes 5308416 | tf_op jit(solution)/shard_map/mixing/pallas_call | solution.py:229
  149.8 8.7 %all-to-all-done.3 = f32[8,1,2304]{2,1,0:T(1,128)S(1)} async-done(((f32[8,1,2304]{2,1,0:T(1,128)}), f32[8,1,2304]{2,1,0:T(1,128)S(1)}, u32[]{:S(2)}, u32[]{:S(2)}) %all-to-all-start.3) | async-done | bytes 73760 | tf_op jit(solution)/shard_map/all_to_all | solution.py:243
  (73 shorter events, 9.6 us)
Async XLA Ops:
  0.6 85.6 %copy-start = (bf16[2,2304]{1,0:T(2,128)(2,1)S(1)}, bf16[2,2304]{1,0:T(2,128)(2,1)}, u32[]{:S(2)}) copy-start(bf16[2,2304]{1,0:T(2,128)(2,1)} %param.8) | copy-start | bytes 27652
  1.5 23.8 %collective-permute-start = (bf16[4,12,256]{2,1,0:T(8,128)(2,1)S(1)}, bf16[4,12,256]{2,1,0:T(8,128)(2,1)S(1)}, u32[]{:S(2)}, u32[]{:S(2)}) collective-permute-start(bf16[4,12,256]{2,1,0:T(8,128)(2,1)S(1)} %get-tuple-element.24), channel_id=1, source_target_pairs={{1,2},{2,1},{3,4},{4,3},{5,6},{6,5},{7,0},{0,7},{9,10},{10,9},{11,... | collective-permute-start | bytes 73736 | tf_op jit(solution)/shard_map/ppermute | solution.py:54
  13.5 11.8 %collective-permute-start.1 = (bf16[4,12,256]{2,1,0:T(8,128)(2,1)S(1)}, bf16[4,12,256]{2,1,0:T(8,128)(2,1)S(1)}, u32[]{:S(2)}, u32[]{:S(2)}) collective-permute-start(bf16[4,12,256]{2,1,0:T(8,128)(2,1)S(1)} %get-tuple-element.25), channel_id=1, source_target_pairs={{0,1},{1,0},{2,3},{3,2},{4,5},{5,4},{6,7},{7,6},{8,9},{9,8},{10,11... | collective-permute-start | bytes 73736 | tf_op jit(solution)/shard_map/ppermute | solution.py:54
  24.3 0.9 copy-start.11
  24.3 1.0 copy-start.4
  25.4 19.3 %copy-start.2 = (bf16[4,96,256]{2,1,0:T(8,128)(2,1)}, bf16[4,96,256]{2,1,0:T(8,128)(2,1)S(1)}, u32[]{:S(2)}) copy-start(bf16[4,96,256]{2,1,0:T(8,128)(2,1)S(1)} %pad_maximum_fusion.4.refs_5_) | copy-start | bytes 589828
  25.4 19.3 %collective-permute-start.2 = (bf16[4,96,256]{2,1,0:T(8,128)(2,1)S(1)}, bf16[4,96,256]{2,1,0:T(8,128)(2,1)S(1)}, u32[]{:S(2)}, u32[]{:S(2)}) collective-permute-start(bf16[4,96,256]{2,1,0:T(8,128)(2,1)S(1)} %pad_maximum_fusion.4.refs_5_), channel_id=1, source_target_pairs={{8,0},{16,8},{24,16},{32,24},{40,32},{48,40},{56,48},{64,56},{72,6... | collective-permute-start | bytes 589832 | tf_op jit(solution)/shard_map/ppermute | solution.py:41
  29.6 17.4 %collective-permute-start.3 = (bf16[4,96,256]{2,1,0:T(8,128)(2,1)S(1)}, bf16[4,96,256]{2,1,0:T(8,128)(2,1)S(1)}, u32[]{:S(2)}, u32[]{:S(2)}) collective-permute-start(bf16[4,96,256]{2,1,0:T(8,128)(2,1)S(1)} %pad_maximum_fusion.4.refs_5_), channel_id=1, source_target_pairs={{0,24},{8,32},{16,40},{24,48},{32,56},{40,64},{48,72},{56,80},{64,... | collective-permute-start | bytes 589832 | tf_op jit(solution)/shard_map/ppermute | solution.py:41
  35.6 16.7 %collective-permute-start.4 = (bf16[4,96,256]{2,1,0:T(8,128)(2,1)S(1)}, bf16[4,96,256]{2,1,0:T(8,128)(2,1)S(1)}, u32[]{:S(2)}, u32[]{:S(2)}) collective-permute-start(bf16[4,96,256]{2,1,0:T(8,128)(2,1)S(1)} %pad_maximum_fusion.4.refs_5_), channel_id=1, source_target_pairs={{0,16},{8,24},{16,32},{24,40},{32,48},{40,56},{48,64},{56,72},{64,... | collective-permute-start | bytes 589832 | tf_op jit(solution)/shard_map/ppermute | solution.py:41
  41.0 19.7 %collective-permute-start.5 = (bf16[4,96,256]{2,1,0:T(8,128)(2,1)S(1)}, bf16[4,96,256]{2,1,0:T(8,128)(2,1)S(1)}, u32[]{:S(2)}, u32[]{:S(2)}) collective-permute-start(bf16[4,96,256]{2,1,0:T(8,128)(2,1)S(1)} %pad_maximum_fusion.4.refs_5_), channel_id=1, source_target_pairs={{0,8},{8,16},{16,24},{24,32},{32,40},{40,48},{48,56},{56,64},{64,7... | collective-permute-start | bytes 589832 | tf_op jit(solution)/shard_map/ppermute | solution.py:41
  43.4 33.9 %collective-permute-start.6 = (bf16[4,96,256]{2,1,0:T(8,128)(2,1)S(1)}, bf16[4,96,256]{2,1,0:T(8,128)(2,1)S(1)}, u32[]{:S(2)}, u32[]{:S(2)}) collective-permute-start(bf16[4,96,256]{2,1,0:T(8,128)(2,1)S(1)} %pad_maximum_fusion.4.refs_5_), channel_id=1, source_target_pairs={{16,0},{24,8},{32,16},{40,24},{48,32},{56,40},{64,48},{72,56},{80,... | collective-permute-start | bytes 589832 | tf_op jit(solution)/shard_map/ppermute | solution.py:41
  44.7 32.6 %copy-start.5 = (bf16[4,96,256]{2,1,0:T(8,128)(2,1)}, bf16[4,96,256]{2,1,0:T(8,128)(2,1)S(1)}, u32[]{:S(2)}) copy-start(bf16[4,96,256]{2,1,0:T(8,128)(2,1)S(1)} %collective-permute-done.2.refs_6_) | copy-start | bytes 589828
  44.7 32.5 %collective-permute-start.7 = (bf16[4,96,256]{2,1,0:T(8,128)(2,1)S(1)}, bf16[4,96,256]{2,1,0:T(8,128)(2,1)S(1)}, u32[]{:S(2)}, u32[]{:S(2)}) collective-permute-start(bf16[4,96,256]{2,1,0:T(8,128)(2,1)S(1)} %pad_maximum_fusion.4.refs_5_), channel_id=1, source_target_pairs={{24,0},{32,8},{40,16},{48,24},{56,32},{64,40},{72,48},{80,56},{88,... | collective-permute-start | bytes 589832 | tf_op jit(solution)/shard_map/ppermute | solution.py:41
  46.9 30.3 %copy-start.6 = (bf16[4,96,256]{2,1,0:T(8,128)(2,1)}, bf16[4,96,256]{2,1,0:T(8,128)(2,1)S(1)}, u32[]{:S(2)}) copy-start(bf16[4,96,256]{2,1,0:T(8,128)(2,1)S(1)} %collective-permute-done.3.refs_2_) | copy-start | bytes 589828
  52.3 24.9 %copy-start.7 = (bf16[4,96,256]{2,1,0:T(8,128)(2,1)}, bf16[4,96,256]{2,1,0:T(8,128)(2,1)S(1)}, u32[]{:S(2)}) copy-start(bf16[4,96,256]{2,1,0:T(8,128)(2,1)S(1)} %collective-permute-done.4.refs_3_) | copy-start | bytes 589828
  60.7 16.5 %copy-start.8 = (bf16[4,96,256]{2,1,0:T(8,128)(2,1)}, bf16[4,96,256]{2,1,0:T(8,128)(2,1)S(1)}, u32[]{:S(2)}) copy-start(bf16[4,96,256]{2,1,0:T(8,128)(2,1)S(1)} %collective-permute-done.5.refs_4_) | copy-start | bytes 589828
  77.2 0.7 copy-start.9
  77.9 0.7 copy-start.10
  83.7 4.3 %collective-permute-start.8 = (bf16[128,2304]{1,0:T(8,128)(2,1)}, bf16[128,2304]{1,0:T(8,128)(2,1)S(1)}, u32[]{:S(2)}, u32[]{:S(2)}) collective-permute-start(bf16[128,2304]{1,0:T(8,128)(2,1)} %get-tuple-element.14), channel_id=1, source_target_pairs={{0,1},{1,0},{2,3},{3,2},{4,5},{5,4},{6,7},{7,6},{8,9},{9,8},{10,11... | collective-permute-start | bytes 1769480 | tf_op jit(solution)/shard_map/ppermute | solution.py:36
  131.0 14.9 %copy-start.1 = (bf16[8,16,2560]{2,1,0:T(8,128)(2,1)}, bf16[8,16,2560]{2,1,0:T(8,128)(2,1)S(1)}, u32[]{:S(2)}) copy-start(bf16[8,16,2560]{2,1,0:T(8,128)(2,1)S(1)} %all_to_all.22) | copy-start | bytes 1966084
  131.1 14.9 %collective-permute-start.9 = (bf16[128,2304]{1,0:T(8,128)(2,1)S(1)}, bf16[128,2304]{1,0:T(8,128)(2,1)S(1)}, u32[]{:S(2)}, u32[]{:S(2)}) collective-permute-start(bf16[128,2304]{1,0:T(8,128)(2,1)S(1)} %slice.80), channel_id=1, source_target_pairs={{0,1},{1,0},{2,3},{3,2},{4,5},{5,4},{6,7},{7,6},{8,9},{9,8},{10,11... | collective-permute-start | bytes 1769480 | tf_op jit(solution)/shard_map/ppermute | solution.py:36
  138.3 20.3 %all-to-all-start.3 = ((f32[8,1,2304]{2,1,0:T(1,128)}), f32[8,1,2304]{2,1,0:T(1,128)S(1)}, u32[]{:S(2)}, u32[]{:S(2)}) async-start(f32[8,1,2304]{2,1,0:T(1,128)} %broadcast_in_dim.40), calls=%async_computation.3 | async-start | bytes 147456 | tf_op jit(solution)/shard_map/all_to_all | solution.py:243
  145.9 0.8 copy-start.3

commit v8 on v4

--- a/solution.py
+++ b/solution.py
@@ -7,7 +7,7 @@
 from jax.experimental.pallas import tpu as pltpu
 from jax.sharding import PartitionSpec as P
 
-FACTORS = {128: (4, 4, 8), 16: (2, 2, 4)}
+FACTORS = {128: (4, 4, 8), 16: (4, 1, 4)}
 TILE = 8
 
 
@@ -47,12 +47,6 @@
             high = 0
         pairs += [(low, high), (high, low)]
     return lax.ppermute(block, axis, pairs)
-
-
-def spread_over(block, dim, factors):
-    copies = jnp.broadcast_to(block, (factors[dim],) + block.shape)
-    joined = lax.all_to_all(copies, "lat", 0, 0, axis_index_groups=groups((dim,), factors))
-    return joined.reshape(-1, block.shape[1])
 
 
 def band_kernel(rows_ref, band_ref):
@@ -128,8 +122,6 @@
     cells = rows * cols
     bf16 = jnp.bfloat16
 
-    gathered = spread_over(lax.dynamic_slice_in_dim(weight, core, 1, 0), 1, factors)
-
     offsets = jnp.arange(width) - reach
     validity = jnp.abs(offsets)[None, None, :] <= spans[:, :, None]
     masked = jnp.where(validity[:, :, None, :], basis, jnp.zeros_like(basis))
@@ -170,12 +162,11 @@
     left = jnp.where(core == 0, far_edge, near_edge)
     right = jnp.where(core == 0, near_edge, far_edge)
     own = jnp.concatenate([left, fields, right], axis=1)
-    own, gathered = lax.optimization_barrier((own, gathered))
     near, far = own, own
     nears, fars = [], []
     for turn in range(3):
         if turn == 2:
-            near, far, band, cot = lax.optimization_barrier((near, far, band, cot))
+            near, band, cot = lax.optimization_barrier((near, band, cot))
         near, far = paired(far, "lat", 0, False), paired(near, "lat", 1, False)
         nears.append(near)
         fars.append(far)
@@ -201,7 +192,15 @@
         return lax.all_to_all(block, "lat", 0, 0, axis_index_groups=groups((dim,), factors))
 
     total = (keep.astype(f32) + swapped_core(send).astype(f32)).astype(bf16)
-    total = jnp.sum(exchanged(total, 1).astype(f32), axis=0).astype(bf16)
+    count = zs * ys
+    column = -(-length // count // 128) * 128
+    mine = lax.dynamic_slice_in_dim(weight, core, 1, 0)
+    folded = jnp.pad(mine, ((0, 0), (0, count * column - length))).reshape(1, count, column)
+    folded = jnp.broadcast_to(folded, (xs, count, column))
+    total = total.reshape(xs, count, length)
+    arrived = exchanged(jnp.concatenate([total, folded], axis=2), 1)
+    total = jnp.sum(arrived[:, :, :length].astype(f32), axis=0).astype(bf16)
+    gathered = arrived[:, :, length:].reshape(xs, count * column)[:, :length]
 
     total = total.reshape(zs, ys, length)
     folded = jnp.concatenate([gathered[:, : length // 2], gathered[:, length // 2 :]], axis=0)

time: 159 us -> 144 us (0.906)
  starting transfers between devices: 71 us -> 55.5 us
  blocking collectives: 34.5 us -> 48.2 us
  waiting for transfers between devices: 27.3 us -> 17.5 us
    all_to_all x2 -> x0, starting transfers between devices: 14.6 us -> none  [the longest x1 10.6 us: exchanged(): lax.all_to_all(block, 'lat', 0, 0, axis_index_groups=groups((dim,), facto...]
    all_to_all x2 -> x3, blocking collectives: 34.5 us -> 48.2 us  [exchanged(): lax.all_to_all(block, 'lat', 0, 0, axis_index_groups=groups((dim,), facto...]
    all_to_all x2 -> x0, waiting for transfers between devices: 11.5 us -> none  [the longest x1 9.57 us: exchanged(): lax.all_to_all(block, 'lat', 0, 0, axis_index_groups=groups((dim,), facto...]
    ppermute x8, waiting for transfers between devices: 5.21 us -> 7.13 us  [paired(): return lax.ppermute(block, axis, pairs)]
    unnamed x31 -> x30, local copies, waits for them, and re-layouts: 3.58 us -> 2.87 us
  transfers between devices with their start and end apart: 13 -> 11, of which waited for: 6 -> 4; matrix products, arithmetic and copies ran while one was open for 5% -> 4% of each run, Pallas kernels for 3% -> 3%
where the time goes in v8:
time: 144 us; the launch traced here: 143 us
  starting transfers between devices  55.5 us (39%)
  blocking collectives  48.2 us (33%)
  waiting for transfers between devices  17.5 us (12%)
  Pallas kernels  10.1 us (7%)
  other arithmetic  5.81 us (4%)
  local copies, waits for them, and re-layouts  4.18 us (3%)
    all_to_all x3, blocking collectives, exchanged(): lax.all_to_all(block, 'lat', 0, 0, axis_index_groups=groups((dim,), facto...  48.2 us
    ppermute x8, starting transfers between devices, paired(): return lax.ppermute(block, axis, pairs)  38.2 us
    ppermute x2, starting transfers between devices, swapped_core(): lax.ppermute(block, 'lon', [(i, i ^ 1) for i in range(lax.axis_size('lon'...  11 us
    all_to_all x1, waiting for transfers between devices, shards(): arrived = lax.all_to_all(spread, 'lon', 0, 0)  8.68 us
    ppermute x8, waiting for transfers between devices, paired(): return lax.ppermute(block, axis, pairs)  7.13 us
    all_to_all x1, starting transfers between devices, shards(): arrived = lax.all_to_all(spread, 'lon', 0, 0)  6.38 us
    pallas_call x1, Pallas kernels, shards(): pl.pallas_call(lambda *refs: feature_kernel(nbasis, tile_count, *refs), o...  5.13 us
    pallas_call x1, Pallas kernels, shards(): pl.pallas_call(lambda *refs: output_kernel(tile_count, *refs), out_shape=...  3.03 us
  transfers between devices with their start and end apart: 11, of which 4 were waited for; matrix products, arithmetic and copies ran while one was open for 4% of the time, Pallas kernels for 3%

profile of v8, /device:TPU:1, one launch (start us, length us, event | category | flops | bytes accessed | tf_op | source)
XLA Modules:
  0.0 143.5 jit_solution(13814389971956453526)
XLA Ops:
  0.7 0.8 broadcast_select_fusion.4
  1.5 12.0 %collective-permute-start = (bf16[4,12,256]{2,1,0:T(8,128)(2,1)S(1)}, bf16[4,12,256]{2,1,0:T(8,128)(2,1)S(1)}, u32[]{:S(2)}, u32[]{:S(2)}) collective-permute-start(bf16[4,12,256]{2,1,0:T(8,128)(2,1)S(1)} %get-tuple-element.24), channel_id=1, source_target_pairs={{1,2},{2,1},{3,4},{4,3},{5,6},{6,5},{7,0},{0,7},{9,10},{10,9},{11,... | collective-permute-start | bytes 73736 | tf_op jit(solution)/shard_map/ppermute | solution.py:49
  13.5 9.0 %collective-permute-start.1 = (bf16[4,12,256]{2,1,0:T(8,128)(2,1)S(1)}, bf16[4,12,256]{2,1,0:T(8,128)(2,1)S(1)}, u32[]{:S(2)}, u32[]{:S(2)}) collective-permute-start(bf16[4,12,256]{2,1,0:T(8,128)(2,1)S(1)} %get-tuple-element.25), channel_id=1, source_target_pairs={{0,1},{1,0},{2,3},{3,2},{4,5},{5,4},{6,7},{7,6},{8,9},{9,8},{10,11... | collective-permute-start | bytes 73736 | tf_op jit(solution)/shard_map/ppermute | solution.py:49
  22.5 0.8 broadcast_compare_fusion
  23.3 1.0 convert_bitcast_fusion
  26.2 5.7 %collective-permute-start.4 = (bf16[4,96,256]{2,1,0:T(8,128)(2,1)S(1)}, bf16[4,96,256]{2,1,0:T(8,128)(2,1)S(1)}, u32[]{:S(2)}, u32[]{:S(2)}) collective-permute-start(bf16[4,96,256]{2,1,0:T(8,128)(2,1)S(1)} %pad_maximum_fusion.4.refs_5_), channel_id=1, source_target_pairs={{0,8},{8,0},{16,24},{24,16},{32,40},{40,32},{48,56},{56,48},{64,72... | collective-permute-start | bytes 589832 | tf_op jit(solution)/shard_map/ppermute | solution.py:49
  32.6 1.9 %shard_map.68.refs_0_ = bf16[288,896]{1,0:T(8,128)(2,1)} custom-call(f32[36,896]{1,0:T(8,128)} %bitcast.48), custom_call_target="tpu_custom_call" | custom-call | tf_op jit(solution)/shard_map/pallas_call | solution.py:138
  34.6 2.5 %collective-permute-start.3 = (bf16[4,96,256]{2,1,0:T(8,128)(2,1)S(1)}, bf16[4,96,256]{2,1,0:T(8,128)(2,1)S(1)}, u32[]{:S(2)}, u32[]{:S(2)}) collective-permute-start(bf16[4,96,256]{2,1,0:T(8,128)(2,1)S(1)} %collective-permute-done.2.refs_6_), channel_id=1, source_target_pairs={{0,8},{8,0},{16,24},{24,16},{32,40},{40,32},{48,56},{56,48},{64,72... | collective-permute-start | bytes 589832 | tf_op jit(solution)/shard_map/ppermute | solution.py:49
  37.8 1.0 convolution_convert_fusion.refs_1_
  38.8 3.6 %collective-permute-done.3.refs_3_ = bf16[4,96,256]{2,1,0:T(8,128)(2,1)S(1)} collective-permute-done((bf16[4,96,256]{2,1,0:T(8,128)(2,1)S(1)}, bf16[4,96,256]{2,1,0:T(8,128)(2,1)S(1)}, u32[]{:S(2)}, u32[]{:S(2)}) %collective-permute-start.3) | collective-permute-done | bytes 196640 | tf_op jit(solution)/shard_map/ppermute | solution.py:49
  43.1 6.9 %collective-permute-start.6 = (bf16[4,96,256]{2,1,0:T(8,128)(2,1)S(1)}, bf16[4,96,256]{2,1,0:T(8,128)(2,1)S(1)}, u32[]{:S(2)}, u32[]{:S(2)}) collective-permute-start(bf16[4,96,256]{2,1,0:T(8,128)(2,1)S(1)} %collective-permute-done.5.refs_7_), channel_id=1, source_target_pairs={{0,8},{8,0},{16,24},{24,16},{32,40},{40,32},{48,56},{56,48},{64,72... | collective-permute-start | bytes 589832 | tf_op jit(solution)/shard_map/ppermute | solution.py:49
  50.1 3.5 %collective-permute-done.6.refs_2_ = bf16[4,96,256]{2,1,0:T(8,128)(2,1)S(1)} collective-permute-done((bf16[4,96,256]{2,1,0:T(8,128)(2,1)S(1)}, bf16[4,96,256]{2,1,0:T(8,128)(2,1)S(1)}, u32[]{:S(2)}, u32[]{:S(2)}) %collective-permute-start.6) | collective-permute-done | bytes 196640 | tf_op jit(solution)/shard_map/ppermute | solution.py:49
  54.3 5.1 %features.1 = (bf16[9,288,256]{2,1,0:T(8,128)(2,1)}, bf16[128,2304]{1,0:T(8,128)(2,1)}, bf16[128,2304]{1,0:T(8,128)(2,1)}) custom-call(bf16[288,896]{1,0:T(8,128)(2,1)} %shard_map.68.refs_0_, bf16[256,288]{1,0:T(8,128)(2,1)} %convolution_convert_fusion.refs_1_, bf16[4,96,256]{2,1,0:T(8,128)(2,1)} %copy-done.10, bf16[4,96,256]{2,1,0:T(8,128)(2,1)} %copy-done.7, ...), custom_call_target="tpu_custom_call" | custom-call | tf_op jit(solution)/shard_map/features/pallas_call | solution.py:175
  59.4 4.3 %collective-permute-start.8 = (bf16[128,2304]{1,0:T(8,128)(2,1)}, bf16[128,2304]{1,0:T(8,128)(2,1)S(1)}, u32[]{:S(2)}, u32[]{:S(2)}) collective-permute-start(bf16[128,2304]{1,0:T(8,128)(2,1)} %get-tuple-element.14), channel_id=1, source_target_pairs={{0,1},{1,0},{2,3},{3,2},{4,5},{5,4},{6,7},{7,6},{8,9},{9,8},{10,11... | collective-permute-start | bytes 1769480 | tf_op jit(solution)/shard_map/ppermute | solution.py:36
  63.7 1.7 %collective-permute-done.8 = bf16[128,2304]{1,0:T(8,128)(2,1)S(1)} collective-permute-done((bf16[128,2304]{1,0:T(8,128)(2,1)}, bf16[128,2304]{1,0:T(8,128)(2,1)S(1)}, u32[]{:S(2)}, u32[]{:S(2)}) %collective-permute-start.8) | collective-permute-done | bytes 589856 | tf_op jit(solution)/shard_map/ppermute | solution.py:36
  65.5 1.2 add_convert_fusion
  66.7 15.9 %all_to_all.20 = bf16[4,32,2432]{2,1,0:T(8,128)(2,1)S(1)} all-to-all(bf16[4,32,2432]{2,1,0:T(8,128)(2,1)S(1)} %pad_maximum_fusion.1), channel_id=1, replica_groups={{0,64,128,192},{8,72,136,200},{16,80,144,208},{24,88,152,216},{32,96,16..., dimensions={0} | all-to-all | bytes 1245184 | tf_op jit(solution)/shard_map/all_to_all | solution.py:192
  82.8 13.2 %all_to_all.21 = bf16[4,8,3456]{2,1,0:T(8,128)(2,1)S(1)} all-to-all(bf16[4,8,3456]{2,1,0:T(8,128)(2,1)S(1)} %pad_maximum_fusion.3), channel_id=1, replica_groups={{0,256,512,768},{8,264,520,776},{16,272,528,784},{24,280,536,792},{32,2..., dimensions={0} | all-to-all | bytes 442368 | tf_op jit(solution)/shard_map/all_to_all | solution.py:192
  96.3 19.1 %all_to_all.22 = bf16[8,16,2560]{2,1,0:T(8,128)(2,1)S(1)} all-to-all(bf16[8,16,2560]{2,1,0:T(8,128)(2,1)S(1)} %pad_maximum_fusion), channel_id=1, replica_groups={{0,8,16,24,32,40,48,56},{64,72,80,88,96,104,112,120},{128,136,144,152,1..., dimensions={0} | all-to-all | bytes 1310720 | tf_op jit(solution)/shard_map/all_to_all | solution.py:192
  115.4 6.7 %collective-permute-start.9 = (bf16[128,2304]{1,0:T(8,128)(2,1)S(1)}, bf16[128,2304]{1,0:T(8,128)(2,1)S(1)}, u32[]{:S(2)}, u32[]{:S(2)}) collective-permute-start(bf16[128,2304]{1,0:T(8,128)(2,1)S(1)} %slice.80), channel_id=1, source_target_pairs={{0,1},{1,0},{2,3},{3,2},{4,5},{5,4},{6,7},{7,6},{8,9},{9,8},{10,11... | collective-permute-start | bytes 1769480 | tf_op jit(solution)/shard_map/ppermute | solution.py:36
  122.9 6.4 %all-to-all-start.3 = ((f32[8,1,2304]{2,1,0:T(1,128)}), f32[8,1,2304]{2,1,0:T(1,128)S(1)}, u32[]{:S(2)}, u32[]{:S(2)}) async-start(f32[8,1,2304]{2,1,0:T(1,128)} %broadcast_in_dim.40), calls=%async_computation.3 | async-start | bytes 147456 | tf_op jit(solution)/shard_map/all_to_all | solution.py:243
  130.0 0.8 copy-done.3
  130.9 3.0 %mixing.1 = bf16[4,72,256]{2,1,0:T(8,128)(2,1)} custom-call(bf16[9,288,256]{2,1,0:T(8,128)(2,1)} %get-tuple-element.15.refs_0_, bf16[128,2560]{1,0:T(8,128)(2,1)} %bitcast.43, bf16[128,2304]{1,0:T(8,128)(2,1)} %copy-done.3, bf16[256,256]{1,0:T(8,128)(2,1)} %fusion.refs_3_), custom_call_target="tpu_custom_call" | custom-call | flops 377487360 | bytes 5308416 | tf_op jit(solution)/shard_map/mixing/pallas_call | solution.py:229
  133.9 8.7 %all-to-all-done.3 = f32[8,1,2304]{2,1,0:T(1,128)S(1)} async-done(((f32[8,1,2304]{2,1,0:T(1,128)}), f32[8,1,2304]{2,1,0:T(1,128)S(1)}, u32[]{:S(2)}, u32[]{:S(2)}) %all-to-all-start.3) | async-done | bytes 73760 | tf_op jit(solution)/shard_map/all_to_all | solution.py:243
  (77 shorter events, 7.4 us)
Async XLA Ops:
  0.6 63.0 %copy-start = (bf16[2,2304]{1,0:T(2,128)(2,1)S(1)}, bf16[2,2304]{1,0:T(2,128)(2,1)}, u32[]{:S(2)}) copy-start(bf16[2,2304]{1,0:T(2,128)(2,1)} %param.8) | copy-start | bytes 27652
  1.5 23.4 %collective-permute-start = (bf16[4,12,256]{2,1,0:T(8,128)(2,1)S(1)}, bf16[4,12,256]{2,1,0:T(8,128)(2,1)S(1)}, u32[]{:S(2)}, u32[]{:S(2)}) collective-permute-start(bf16[4,12,256]{2,1,0:T(8,128)(2,1)S(1)} %get-tuple-element.24), channel_id=1, source_target_pairs={{1,2},{2,1},{3,4},{4,3},{5,6},{6,5},{7,0},{0,7},{9,10},{10,9},{11,... | collective-permute-start | bytes 73736 | tf_op jit(solution)/shard_map/ppermute | solution.py:49
  13.5 11.3 %collective-permute-start.1 = (bf16[4,12,256]{2,1,0:T(8,128)(2,1)S(1)}, bf16[4,12,256]{2,1,0:T(8,128)(2,1)S(1)}, u32[]{:S(2)}, u32[]{:S(2)}) collective-permute-start(bf16[4,12,256]{2,1,0:T(8,128)(2,1)S(1)} %get-tuple-element.25), channel_id=1, source_target_pairs={{0,1},{1,0},{2,3},{3,2},{4,5},{5,4},{6,7},{7,6},{8,9},{9,8},{10,11... | collective-permute-start | bytes 73736 | tf_op jit(solution)/shard_map/ppermute | solution.py:49
  24.5 0.9 copy-start.4
  24.8 9.8 %copy-start.11 = (bf16[4,72,256]{2,1,0:T(8,128)(2,1)S(1)}, bf16[4,72,256]{2,1,0:T(8,128)(2,1)}, u32[]{:S(2)}) copy-start(bf16[4,72,256]{2,1,0:T(8,128)(2,1)} %param.9) | copy-start | bytes 442372
  25.5 28.1 %copy-start.2 = (bf16[4,96,256]{2,1,0:T(8,128)(2,1)}, bf16[4,96,256]{2,1,0:T(8,128)(2,1)S(1)}, u32[]{:S(2)}) copy-start(bf16[4,96,256]{2,1,0:T(8,128)(2,1)S(1)} %pad_maximum_fusion.4.refs_5_) | copy-start | bytes 589828
  25.5 9.1 %collective-permute-start.2 = (bf16[4,96,256]{2,1,0:T(8,128)(2,1)S(1)}, bf16[4,96,256]{2,1,0:T(8,128)(2,1)S(1)}, u32[]{:S(2)}, u32[]{:S(2)}) collective-permute-start(bf16[4,96,256]{2,1,0:T(8,128)(2,1)S(1)} %pad_maximum_fusion.4.refs_5_), channel_id=1, source_target_pairs={{8,16},{16,8},{24,32},{32,24},{40,48},{48,40},{56,64},{64,56},{72,... | collective-permute-start | bytes 589832 | tf_op jit(solution)/shard_map/ppermute | solution.py:49
  26.2 10.9 %collective-permute-start.4 = (bf16[4,96,256]{2,1,0:T(8,128)(2,1)S(1)}, bf16[4,96,256]{2,1,0:T(8,128)(2,1)S(1)}, u32[]{:S(2)}, u32[]{:S(2)}) collective-permute-start(bf16[4,96,256]{2,1,0:T(8,128)(2,1)S(1)} %pad_maximum_fusion.4.refs_5_), channel_id=1, source_target_pairs={{0,8},{8,0},{16,24},{24,16},{32,40},{40,32},{48,56},{56,48},{64,72... | collective-permute-start | bytes 589832 | tf_op jit(solution)/shard_map/ppermute | solution.py:49
  34.6 18.9 %copy-start.5 = (bf16[4,96,256]{2,1,0:T(8,128)(2,1)}, bf16[4,96,256]{2,1,0:T(8,128)(2,1)S(1)}, u32[]{:S(2)}) copy-start(bf16[4,96,256]{2,1,0:T(8,128)(2,1)S(1)} %collective-permute-done.2.refs_6_) | copy-start | bytes 589828
  34.6 7.8 %collective-permute-start.3 = (bf16[4,96,256]{2,1,0:T(8,128)(2,1)S(1)}, bf16[4,96,256]{2,1,0:T(8,128)(2,1)S(1)}, u32[]{:S(2)}, u32[]{:S(2)}) collective-permute-start(bf16[4,96,256]{2,1,0:T(8,128)(2,1)S(1)} %collective-permute-done.2.refs_6_), channel_id=1, source_target_pairs={{0,8},{8,0},{16,24},{24,16},{32,40},{40,32},{48,56},{56,48},{64,72... | collective-permute-start | bytes 589832 | tf_op jit(solution)/shard_map/ppermute | solution.py:49
  37.1 16.4 %copy-start.6 = (bf16[4,96,256]{2,1,0:T(8,128)(2,1)}, bf16[4,96,256]{2,1,0:T(8,128)(2,1)S(1)}, u32[]{:S(2)}) copy-start(bf16[4,96,256]{2,1,0:T(8,128)(2,1)S(1)} %collective-permute-done.4.refs_4_) | copy-start | bytes 589828
  37.1 6.0 %collective-permute-start.5 = (bf16[4,96,256]{2,1,0:T(8,128)(2,1)S(1)}, bf16[4,96,256]{2,1,0:T(8,128)(2,1)S(1)}, u32[]{:S(2)}, u32[]{:S(2)}) collective-permute-start(bf16[4,96,256]{2,1,0:T(8,128)(2,1)S(1)} %collective-permute-done.4.refs_4_), channel_id=1, source_target_pairs={{8,16},{16,8},{24,32},{32,24},{40,48},{48,40},{56,64},{64,56},{72,... | collective-permute-start | bytes 589832 | tf_op jit(solution)/shard_map/ppermute | solution.py:49
  42.4 11.1 %copy-start.7 = (bf16[4,96,256]{2,1,0:T(8,128)(2,1)}, bf16[4,96,256]{2,1,0:T(8,128)(2,1)S(1)}, u32[]{:S(2)}) copy-start(bf16[4,96,256]{2,1,0:T(8,128)(2,1)S(1)} %collective-permute-done.3.refs_3_) | copy-start | bytes 589828
  42.4 7.6 %collective-permute-start.7 = (bf16[4,96,256]{2,1,0:T(8,128)(2,1)S(1)}, bf16[4,96,256]{2,1,0:T(8,128)(2,1)S(1)}, u32[]{:S(2)}, u32[]{:S(2)}) collective-permute-start(bf16[4,96,256]{2,1,0:T(8,128)(2,1)S(1)} %collective-permute-done.3.refs_3_), channel_id=1, source_target_pairs={{8,16},{16,8},{24,32},{32,24},{40,48},{48,40},{56,64},{64,56},{72,... | collective-permute-start | bytes 589832 | tf_op jit(solution)/shard_map/ppermute | solution.py:49
  43.1 10.5 %copy-start.8 = (bf16[4,96,256]{2,1,0:T(8,128)(2,1)}, bf16[4,96,256]{2,1,0:T(8,128)(2,1)S(1)}, u32[]{:S(2)}) copy-start(bf16[4,96,256]{2,1,0:T(8,128)(2,1)S(1)} %collective-permute-done.5.refs_7_) | copy-start | bytes 589828
  43.1 10.4 %collective-permute-start.6 = (bf16[4,96,256]{2,1,0:T(8,128)(2,1)S(1)}, bf16[4,96,256]{2,1,0:T(8,128)(2,1)S(1)}, u32[]{:S(2)}, u32[]{:S(2)}) collective-permute-start(bf16[4,96,256]{2,1,0:T(8,128)(2,1)S(1)} %collective-permute-done.5.refs_7_), channel_id=1, source_target_pairs={{0,8},{8,0},{16,24},{24,16},{32,40},{40,32},{48,56},{56,48},{64,72... | collective-permute-start | bytes 589832 | tf_op jit(solution)/shard_map/ppermute | solution.py:49
  50.1 3.5 %copy-start.9 = (bf16[4,96,256]{2,1,0:T(8,128)(2,1)}, bf16[4,96,256]{2,1,0:T(8,128)(2,1)S(1)}, u32[]{:S(2)}) copy-start(bf16[4,96,256]{2,1,0:T(8,128)(2,1)S(1)} %collective-permute-done.7.refs_8_) | copy-start | bytes 589828
  53.6 0.7 copy-start.10
  59.4 6.1 %collective-permute-start.8 = (bf16[128,2304]{1,0:T(8,128)(2,1)}, bf16[128,2304]{1,0:T(8,128)(2,1)S(1)}, u32[]{:S(2)}, u32[]{:S(2)}) collective-permute-start(bf16[128,2304]{1,0:T(8,128)(2,1)} %get-tuple-element.14), channel_id=1, source_target_pairs={{0,1},{1,0},{2,3},{3,2},{4,5},{5,4},{6,7},{7,6},{8,9},{9,8},{10,11... | collective-permute-start | bytes 1769480 | tf_op jit(solution)/shard_map/ppermute | solution.py:36
  115.4 14.7 %copy-start.1 = (bf16[8,16,2560]{2,1,0:T(8,128)(2,1)}, bf16[8,16,2560]{2,1,0:T(8,128)(2,1)S(1)}, u32[]{:S(2)}) copy-start(bf16[8,16,2560]{2,1,0:T(8,128)(2,1)S(1)} %all_to_all.22) | copy-start | bytes 1966084
  115.4 14.6 %collective-permute-start.9 = (bf16[128,2304]{1,0:T(8,128)(2,1)S(1)}, bf16[128,2304]{1,0:T(8,128)(2,1)S(1)}, u32[]{:S(2)}, u32[]{:S(2)}) collective-permute-start(bf16[128,2304]{1,0:T(8,128)(2,1)S(1)} %slice.80), channel_id=1, source_target_pairs={{0,1},{1,0},{2,3},{3,2},{4,5},{5,4},{6,7},{7,6},{8,9},{9,8},{10,11... | collective-permute-start | bytes 1769480 | tf_op jit(solution)/shard_map/ppermute | solution.py:36
  122.9 19.7 %all-to-all-start.3 = ((f32[8,1,2304]{2,1,0:T(1,128)}), f32[8,1,2304]{2,1,0:T(1,128)S(1)}, u32[]{:S(2)}, u32[]{:S(2)}) async-start(f32[8,1,2304]{2,1,0:T(1,128)} %broadcast_in_dim.40), calls=%async_computation.3 | async-start | bytes 147456 | tf_op jit(solution)/shard_map/all_to_all | solution.py:243
  130.0 0.8 copy-start.3

commit v9 on v8

--- a/solution.py
+++ b/solution.py
@@ -187,9 +187,10 @@
     f32 = jnp.float32
     length = nbasis * channels
 
-    def exchanged(block, dim):
-        block = block.reshape(factors[dim], -1, block.shape[-1])
-        return lax.all_to_all(block, "lat", 0, 0, axis_index_groups=groups((dim,), factors))
+    def exchanged(block, dims):
+        members = groups(dims, factors)
+        block = block.reshape(len(members[0]), -1, block.shape[-1])
+        return lax.all_to_all(block, "lat", 0, 0, axis_index_groups=members)
 
     total = (keep.astype(f32) + swapped_core(send).astype(f32)).astype(bf16)
     count = zs * ys
@@ -198,31 +199,25 @@
     folded = jnp.pad(mine, ((0, 0), (0, count * column - length))).reshape(1, count, column)
     folded = jnp.broadcast_to(folded, (xs, count, column))
     total = total.reshape(xs, count, length)
-    arrived = exchanged(jnp.concatenate([total, folded], axis=2), 1)
+    arrived = exchanged(jnp.concatenate([total, folded], axis=2), (1,))
     total = jnp.sum(arrived[:, :, :length].astype(f32), axis=0).astype(bf16)
     gathered = arrived[:, :, length:].reshape(xs, count * column)[:, :length]
 
-    total = total.reshape(zs, ys, length)
-    folded = jnp.concatenate([gathered[:, : length // 2], gathered[:, length // 2 :]], axis=0)
-    folded = jnp.pad(folded, ((0, ys - folded.shape[0]), (0, 0)))
-    folded = jnp.broadcast_to(folded, (zs,) + folded.shape)
-    arrived = exchanged(jnp.concatenate([total, folded], axis=2), 0)
-    total = jnp.sum(arrived[:, :, :length].astype(f32), axis=0).astype(bf16)
-    gathered = jnp.concatenate(
-        [arrived[:, :xs, length:], arrived[:, xs : 2 * xs, length:]], axis=2
-    ).reshape(zs * xs, length)
-
-    piece = zs * xs
-    column = -(-length // piece // 128) * 128
-    folded = jnp.pad(total, ((0, 0), (0, piece * column - length))).reshape(ys, piece, column)
-    whole = jnp.broadcast_to(gathered, (ys,) + gathered.shape)
-    arrived = exchanged(jnp.concatenate([whole, folded], axis=2), 2)
-    gathered = arrived.reshape(ys * piece, length + column)
+    count = zs * ys
+    column = -(-length // xs // 128) * 128
+    whole = jnp.broadcast_to(gathered, (count,) + gathered.shape)
+    total = jnp.pad(total, ((0, 0), (0, xs * column - length))).reshape(count, xs, column)
+    arrived = exchanged(jnp.concatenate([whole, total], axis=2), (0, 2))
     total = jnp.sum(arrived[:, :, length:].astype(f32), axis=0).reshape(1, -1)[:, :length]
-
-    other_weight = swapped_core(gathered[:, :length])
+    scale = 1.0 / math.sqrt(rows * lax.axis_size("lat") * cols * lax.axis_size("lon"))
+    lon_size = lax.axis_size("lon")
+    spread = jnp.broadcast_to(total * scale, (lon_size,) + total.shape)
+    arrived, spread = lax.optimization_barrier((arrived, spread))
+    gathered = arrived.reshape(count * xs, length + column)
+
+    other_weight = swapped_core(gathered)
     place = position % half
-    weight_row = 2 * lat_index(place // xs % zs, place % xs, place // piece, factors)
+    weight_row = 2 * lat_index(place // (xs * ys), place % xs, place // xs % ys, factors)
     weight_row = weight_row + (core ^ (position // half))
     weight_order = (weight_row[:, None] == jnp.arange(outs)[None, :]).astype(bf16)
 
@@ -237,9 +232,6 @@
         name="mixing",
     )(features, gathered, other_weight, weight_order)
 
-    scale = 1.0 / math.sqrt(rows * lax.axis_size("lat") * cols * lax.axis_size("lon"))
-    lon_size = lax.axis_size("lon")
-    spread = jnp.broadcast_to(total * scale, (lon_size,) + total.shape)
     arrived = lax.all_to_all(spread, "lon", 0, 0)
     arrived, output = lax.optimization_barrier((arrived, output))
     grad_weight = jnp.sum(arrived.reshape(lon_size // 2, 2, nbasis * channels), axis=0)

time: 144 us -> 139 us (0.965)
  blocking collectives: 48.2 us -> 44.3 us
  starting transfers between devices: 55.5 us -> 53.5 us
    all_to_all x3 -> x2, blocking collectives: 48.2 us -> 44.3 us  [exchanged(): return lax.all_to_all(block, 'lat', 0, 0, axis_index_groups=members)]
    ppermute x2, starting transfers between devices: 11 us -> 8.91 us  [swapped_core(): lax.ppermute(block, 'lon', [(i, i ^ 1) for i in range(lax.axis_size('lon'...]
  transfers between devices with their start and end apart: 11 -> 11, of which waited for: 4 -> 4; matrix products, arithmetic and copies ran while one was open for 4% -> 3% of each run, Pallas kernels for 3% -> 4%
where the time goes in v9:
time: 139 us; the launch traced here: 138 us
  starting transfers between devices  53.5 us (38%)
  blocking collectives  44.3 us (32%)
  waiting for transfers between devices  17.6 us (13%)
  Pallas kernels  10.2 us (7%)
  other arithmetic  6.07 us (4%)
  local copies, waits for them, and re-layouts  4.43 us (3%)
    all_to_all x2, blocking collectives, exchanged(): return lax.all_to_all(block, 'lat', 0, 0, axis_index_groups=members)  44.3 us
    ppermute x8, starting transfers between devices, paired(): return lax.ppermute(block, axis, pairs)  38.2 us
    ppermute x2, starting transfers between devices, swapped_core(): lax.ppermute(block, 'lon', [(i, i ^ 1) for i in range(lax.axis_size('lon'...  8.91 us
    all_to_all x1, waiting for transfers between devices, shards(): arrived = lax.all_to_all(spread, 'lon', 0, 0)  8.76 us
    ppermute x8, waiting for transfers between devices, paired(): return lax.ppermute(block, axis, pairs)  7.12 us
    all_to_all x1, starting transfers between devices, shards(): arrived = lax.all_to_all(spread, 'lon', 0, 0)  6.39 us
    pallas_call x1, Pallas kernels, shards(): pl.pallas_call(lambda *refs: feature_kernel(nbasis, tile_count, *refs), o...  5.14 us
    pallas_call x1, Pallas kernels, shards(): pl.pallas_call(lambda *refs: output_kernel(tile_count, *refs), out_shape=...  3.12 us
  transfers between devices with their start and end apart: 11, of which 4 were waited for; matrix products, arithmetic and copies ran while one was open for 3% of the time, Pallas kernels for 4%

profile of v9, /device:TPU:1, one launch (start us, length us, event | category | flops | bytes accessed | tf_op | source)
XLA Modules:
  0.0 138.2 jit_solution(3572498269350176797)
XLA Ops:
  0.7 0.8 broadcast_select_fusion.4
  1.5 12.0 %collective-permute-start = (bf16[4,12,256]{2,1,0:T(8,128)(2,1)S(1)}, bf16[4,12,256]{2,1,0:T(8,128)(2,1)S(1)}, u32[]{:S(2)}, u32[]{:S(2)}) collective-permute-start(bf16[4,12,256]{2,1,0:T(8,128)(2,1)S(1)} %get-tuple-element.26), channel_id=1, source_target_pairs={{1,2},{2,1},{3,4},{4,3},{5,6},{6,5},{7,0},{0,7},{9,10},{10,9},{11,... | collective-permute-start | bytes 73736 | tf_op jit(solution)/shard_map/ppermute | solution.py:49
  13.5 9.0 %collective-permute-start.1 = (bf16[4,12,256]{2,1,0:T(8,128)(2,1)S(1)}, bf16[4,12,256]{2,1,0:T(8,128)(2,1)S(1)}, u32[]{:S(2)}, u32[]{:S(2)}) collective-permute-start(bf16[4,12,256]{2,1,0:T(8,128)(2,1)S(1)} %get-tuple-element.27), channel_id=1, source_target_pairs={{0,1},{1,0},{2,3},{3,2},{4,5},{5,4},{6,7},{7,6},{8,9},{9,8},{10,11... | collective-permute-start | bytes 73736 | tf_op jit(solution)/shard_map/ppermute | solution.py:49
  22.5 0.8 broadcast_compare_fusion
  23.3 1.0 convert_bitcast_fusion
  26.2 5.7 %collective-permute-start.4 = (bf16[4,96,256]{2,1,0:T(8,128)(2,1)S(1)}, bf16[4,96,256]{2,1,0:T(8,128)(2,1)S(1)}, u32[]{:S(2)}, u32[]{:S(2)}) collective-permute-start(bf16[4,96,256]{2,1,0:T(8,128)(2,1)S(1)} %pad_maximum_fusion.3.refs_5_), channel_id=1, source_target_pairs={{0,8},{8,0},{16,24},{24,16},{32,40},{40,32},{48,56},{56,48},{64,72... | collective-permute-start | bytes 589832 | tf_op jit(solution)/shard_map/ppermute | solution.py:49
  32.6 1.9 %shard_map.68.refs_0_ = bf16[288,896]{1,0:T(8,128)(2,1)} custom-call(f32[36,896]{1,0:T(8,128)} %bitcast.39), custom_call_target="tpu_custom_call" | custom-call | tf_op jit(solution)/shard_map/pallas_call | solution.py:138
  34.6 2.5 %collective-permute-start.3 = (bf16[4,96,256]{2,1,0:T(8,128)(2,1)S(1)}, bf16[4,96,256]{2,1,0:T(8,128)(2,1)S(1)}, u32[]{:S(2)}, u32[]{:S(2)}) collective-permute-start(bf16[4,96,256]{2,1,0:T(8,128)(2,1)S(1)} %collective-permute-done.2.refs_6_), channel_id=1, source_target_pairs={{0,8},{8,0},{16,24},{24,16},{32,40},{40,32},{48,56},{56,48},{64,72... | collective-permute-start | bytes 589832 | tf_op jit(solution)/shard_map/ppermute | solution.py:49
  37.8 1.0 convolution_convert_fusion.refs_1_
  38.8 3.6 %collective-permute-done.3.refs_3_ = bf16[4,96,256]{2,1,0:T(8,128)(2,1)S(1)} collective-permute-done((bf16[4,96,256]{2,1,0:T(8,128)(2,1)S(1)}, bf16[4,96,256]{2,1,0:T(8,128)(2,1)S(1)}, u32[]{:S(2)}, u32[]{:S(2)}) %collective-permute-start.3) | collective-permute-done | bytes 196640 | tf_op jit(solution)/shard_map/ppermute | solution.py:49
  43.1 6.9 %collective-permute-start.6 = (bf16[4,96,256]{2,1,0:T(8,128)(2,1)S(1)}, bf16[4,96,256]{2,1,0:T(8,128)(2,1)S(1)}, u32[]{:S(2)}, u32[]{:S(2)}) collective-permute-start(bf16[4,96,256]{2,1,0:T(8,128)(2,1)S(1)} %collective-permute-done.5.refs_7_), channel_id=1, source_target_pairs={{0,8},{8,0},{16,24},{24,16},{32,40},{40,32},{48,56},{56,48},{64,72... | collective-permute-start | bytes 589832 | tf_op jit(solution)/shard_map/ppermute | solution.py:49
  50.1 3.5 %collective-permute-done.6.refs_2_ = bf16[4,96,256]{2,1,0:T(8,128)(2,1)S(1)} collective-permute-done((bf16[4,96,256]{2,1,0:T(8,128)(2,1)S(1)}, bf16[4,96,256]{2,1,0:T(8,128)(2,1)S(1)}, u32[]{:S(2)}, u32[]{:S(2)}) %collective-permute-start.6) | collective-permute-done | bytes 196640 | tf_op jit(solution)/shard_map/ppermute | solution.py:49
  54.2 5.1 %features.1 = (bf16[9,288,256]{2,1,0:T(8,128)(2,1)}, bf16[128,2304]{1,0:T(8,128)(2,1)}, bf16[128,2304]{1,0:T(8,128)(2,1)}) custom-call(bf16[288,896]{1,0:T(8,128)(2,1)} %shard_map.68.refs_0_, bf16[256,288]{1,0:T(8,128)(2,1)} %convolution_convert_fusion.refs_1_, bf16[4,96,256]{2,1,0:T(8,128)(2,1)} %copy-done.10, bf16[4,96,256]{2,1,0:T(8,128)(2,1)} %copy-done.7, ...), custom_call_target="tpu_custom_call" | custom-call | tf_op jit(solution)/shard_map/features/pallas_call | solution.py:175
  59.4 4.2 %collective-permute-start.8 = (bf16[128,2304]{1,0:T(8,128)(2,1)}, bf16[128,2304]{1,0:T(8,128)(2,1)S(1)}, u32[]{:S(2)}, u32[]{:S(2)}) collective-permute-start(bf16[128,2304]{1,0:T(8,128)(2,1)} %get-tuple-element.16), channel_id=1, source_target_pairs={{0,1},{1,0},{2,3},{3,2},{4,5},{5,4},{6,7},{7,6},{8,9},{9,8},{10,11... | collective-permute-start | bytes 1769480 | tf_op jit(solution)/shard_map/ppermute | solution.py:36
  63.7 1.7 %collective-permute-done.8 = bf16[128,2304]{1,0:T(8,128)(2,1)S(1)} collective-permute-done((bf16[128,2304]{1,0:T(8,128)(2,1)}, bf16[128,2304]{1,0:T(8,128)(2,1)S(1)}, u32[]{:S(2)}, u32[]{:S(2)}) %collective-permute-start.8) | collective-permute-done | bytes 589856 | tf_op jit(solution)/shard_map/ppermute | solution.py:36
  65.5 1.2 add_convert_fusion
  66.7 15.9 %all_to_all.15 = bf16[4,32,2432]{2,1,0:T(8,128)(2,1)S(1)} all-to-all(bf16[4,32,2432]{2,1,0:T(8,128)(2,1)S(1)} %pad_maximum_fusion.1), channel_id=1, replica_groups={{0,64,128,192},{8,72,136,200},{16,80,144,208},{24,88,152,216},{32,96,16..., dimensions={0} | all-to-all | bytes 1245184 | tf_op jit(solution)/shard_map/all_to_all | solution.py:193
  83.3 28.4 %all_to_all.16 = bf16[32,4,2944]{2,1,0:T(4,128)(2,1)S(1)} all-to-all(bf16[32,4,2944]{2,1,0:T(4,128)(2,1)S(1)} %pad_maximum_fusion), channel_id=1, replica_groups={{0,8,16,24,32,40,48,56,256,264,272,280,288,296,304,312,512,520,528,536,..., dimensions={0} | all-to-all | bytes 1507328 | tf_op jit(solution)/shard_map/all_to_all | solution.py:193
  112.7 4.7 %collective-permute-start.9 = (bf16[128,2944]{1,0:T(8,128)(2,1)S(1)}, bf16[128,2944]{1,0:T(8,128)(2,1)S(1)}, u32[]{:S(2)}, u32[]{:S(2)}) collective-permute-start(bf16[128,2944]{1,0:T(8,128)(2,1)S(1)} %reshape.180.refs_1_), channel_id=1, source_target_pairs={{0,1},{1,0},{2,3},{3,2},{4,5},{5,4},{6,7},{7,6},{8,9},{9,8},{10,11... | collective-permute-start | bytes 2261000 | tf_op jit(solution)/shard_map/ppermute | solution.py:36
  117.4 6.4 %all-to-all-start.2 = ((f32[8,1,2304]{2,1,0:T(1,128)}), f32[8,1,2304]{2,1,0:T(1,128)S(1)}, u32[]{:S(2)}, u32[]{:S(2)}) async-start(f32[8,1,2304]{2,1,0:T(1,128)} %broadcast_in_dim.36), calls=%async_computation.2 | async-start | bytes 147456 | tf_op jit(solution)/shard_map/all_to_all | solution.py:235
  123.8 0.8 fusion.refs_3_
  124.5 0.9 copy-done.3
  125.4 3.1 %mixing.1 = bf16[4,72,256]{2,1,0:T(8,128)(2,1)} custom-call(bf16[9,288,256]{2,1,0:T(8,128)(2,1)} %get-tuple-element.18.refs_0_, bf16[128,2944]{1,0:T(8,128)(2,1)} %copy-done.1, bf16[128,2944]{1,0:T(8,128)(2,1)} %copy-done.3, bf16[256,256]{1,0:T(8,128)(2,1)} %fusion.refs_3_), custom_call_target="tpu_custom_call" | custom-call | flops 377487360 | bytes 5308416 | tf_op jit(solution)/shard_map/mixing/pallas_call | solution.py:224
  128.5 8.8 %all-to-all-done.2 = f32[8,1,2304]{2,1,0:T(1,128)S(1)} async-done(((f32[8,1,2304]{2,1,0:T(1,128)}), f32[8,1,2304]{2,1,0:T(1,128)S(1)}, u32[]{:S(2)}, u32[]{:S(2)}) %all-to-all-start.2) | async-done | bytes 73760 | tf_op jit(solution)/shard_map/all_to_all | solution.py:235
  (69 shorter events, 7.2 us)
Async XLA Ops:
  0.6 63.0 %copy-start = (bf16[2,2304]{1,0:T(2,128)(2,1)S(1)}, bf16[2,2304]{1,0:T(2,128)(2,1)}, u32[]{:S(2)}) copy-start(bf16[2,2304]{1,0:T(2,128)(2,1)} %param.8) | copy-start | bytes 27652
  1.5 23.4 %collective-permute-start = (bf16[4,12,256]{2,1,0:T(8,128)(2,1)S(1)}, bf16[4,12,256]{2,1,0:T(8,128)(2,1)S(1)}, u32[]{:S(2)}, u32[]{:S(2)}) collective-permute-start(bf16[4,12,256]{2,1,0:T(8,128)(2,1)S(1)} %get-tuple-element.26), channel_id=1, source_target_pairs={{1,2},{2,1},{3,4},{4,3},{5,6},{6,5},{7,0},{0,7},{9,10},{10,9},{11,... | collective-permute-start | bytes 73736 | tf_op jit(solution)/shard_map/ppermute | solution.py:49
  13.5 11.3 %collective-permute-start.1 = (bf16[4,12,256]{2,1,0:T(8,128)(2,1)S(1)}, bf16[4,12,256]{2,1,0:T(8,128)(2,1)S(1)}, u32[]{:S(2)}, u32[]{:S(2)}) collective-permute-start(bf16[4,12,256]{2,1,0:T(8,128)(2,1)S(1)} %get-tuple-element.27), channel_id=1, source_target_pairs={{0,1},{1,0},{2,3},{3,2},{4,5},{5,4},{6,7},{7,6},{8,9},{9,8},{10,11... | collective-permute-start | bytes 73736 | tf_op jit(solution)/shard_map/ppermute | solution.py:49
  24.5 0.9 copy-start.4
  24.8 9.8 %copy-start.11 = (bf16[4,72,256]{2,1,0:T(8,128)(2,1)S(1)}, bf16[4,72,256]{2,1,0:T(8,128)(2,1)}, u32[]{:S(2)}) copy-start(bf16[4,72,256]{2,1,0:T(8,128)(2,1)} %param.9) | copy-start | bytes 442372
  25.5 28.1 %copy-start.2 = (bf16[4,96,256]{2,1,0:T(8,128)(2,1)}, bf16[4,96,256]{2,1,0:T(8,128)(2,1)S(1)}, u32[]{:S(2)}) copy-start(bf16[4,96,256]{2,1,0:T(8,128)(2,1)S(1)} %pad_maximum_fusion.3.refs_5_) | copy-start | bytes 589828
  25.5 9.1 %collective-permute-start.2 = (bf16[4,96,256]{2,1,0:T(8,128)(2,1)S(1)}, bf16[4,96,256]{2,1,0:T(8,128)(2,1)S(1)}, u32[]{:S(2)}, u32[]{:S(2)}) collective-permute-start(bf16[4,96,256]{2,1,0:T(8,128)(2,1)S(1)} %pad_maximum_fusion.3.refs_5_), channel_id=1, source_target_pairs={{8,16},{16,8},{24,32},{32,24},{40,48},{48,40},{56,64},{64,56},{72,... | collective-permute-start | bytes 589832 | tf_op jit(solution)/shard_map/ppermute | solution.py:49
  26.2 10.9 %collective-permute-start.4 = (bf16[4,96,256]{2,1,0:T(8,128)(2,1)S(1)}, bf16[4,96,256]{2,1,0:T(8,128)(2,1)S(1)}, u32[]{:S(2)}, u32[]{:S(2)}) collective-permute-start(bf16[4,96,256]{2,1,0:T(8,128)(2,1)S(1)} %pad_maximum_fusion.3.refs_5_), channel_id=1, source_target_pairs={{0,8},{8,0},{16,24},{24,16},{32,40},{40,32},{48,56},{56,48},{64,72... | collective-permute-start | bytes 589832 | tf_op jit(solution)/shard_map/ppermute | solution.py:49
  34.6 18.9 %copy-start.5 = (bf16[4,96,256]{2,1,0:T(8,128)(2,1)}, bf16[4,96,256]{2,1,0:T(8,128)(2,1)S(1)}, u32[]{:S(2)}) copy-start(bf16[4,96,256]{2,1,0:T(8,128)(2,1)S(1)} %collective-permute-done.2.refs_6_) | copy-start | bytes 589828
  34.6 7.8 %collective-permute-start.3 = (bf16[4,96,256]{2,1,0:T(8,128)(2,1)S(1)}, bf16[4,96,256]{2,1,0:T(8,128)(2,1)S(1)}, u32[]{:S(2)}, u32[]{:S(2)}) collective-permute-start(bf16[4,96,256]{2,1,0:T(8,128)(2,1)S(1)} %collective-permute-done.2.refs_6_), channel_id=1, source_target_pairs={{0,8},{8,0},{16,24},{24,16},{32,40},{40,32},{48,56},{56,48},{64,72... | collective-permute-start | bytes 589832 | tf_op jit(solution)/shard_map/ppermute | solution.py:49
  37.1 16.4 %copy-start.6 = (bf16[4,96,256]{2,1,0:T(8,128)(2,1)}, bf16[4,96,256]{2,1,0:T(8,128)(2,1)S(1)}, u32[]{:S(2)}) copy-start(bf16[4,96,256]{2,1,0:T(8,128)(2,1)S(1)} %collective-permute-done.4.refs_4_) | copy-start | bytes 589828
  37.1 5.9 %collective-permute-start.5 = (bf16[4,96,256]{2,1,0:T(8,128)(2,1)S(1)}, bf16[4,96,256]{2,1,0:T(8,128)(2,1)S(1)}, u32[]{:S(2)}, u32[]{:S(2)}) collective-permute-start(bf16[4,96,256]{2,1,0:T(8,128)(2,1)S(1)} %collective-permute-done.4.refs_4_), channel_id=1, source_target_pairs={{8,16},{16,8},{24,32},{32,24},{40,48},{48,40},{56,64},{64,56},{72,... | collective-permute-start | bytes 589832 | tf_op jit(solution)/shard_map/ppermute | solution.py:49
  42.4 11.1 %copy-start.7 = (bf16[4,96,256]{2,1,0:T(8,128)(2,1)}, bf16[4,96,256]{2,1,0:T(8,128)(2,1)S(1)}, u32[]{:S(2)}) copy-start(bf16[4,96,256]{2,1,0:T(8,128)(2,1)S(1)} %collective-permute-done.3.refs_3_) | copy-start | bytes 589828
  42.4 7.6 %collective-permute-start.7 = (bf16[4,96,256]{2,1,0:T(8,128)(2,1)S(1)}, bf16[4,96,256]{2,1,0:T(8,128)(2,1)S(1)}, u32[]{:S(2)}, u32[]{:S(2)}) collective-permute-start(bf16[4,96,256]{2,1,0:T(8,128)(2,1)S(1)} %collective-permute-done.3.refs_3_), channel_id=1, source_target_pairs={{8,16},{16,8},{24,32},{32,24},{40,48},{48,40},{56,64},{64,56},{72,... | collective-permute-start | bytes 589832 | tf_op jit(solution)/shard_map/ppermute | solution.py:49
  43.1 10.5 %copy-start.8 = (bf16[4,96,256]{2,1,0:T(8,128)(2,1)}, bf16[4,96,256]{2,1,0:T(8,128)(2,1)S(1)}, u32[]{:S(2)}) copy-start(bf16[4,96,256]{2,1,0:T(8,128)(2,1)S(1)} %collective-permute-done.5.refs_7_) | copy-start | bytes 589828
  43.1 10.4 %collective-permute-start.6 = (bf16[4,96,256]{2,1,0:T(8,128)(2,1)S(1)}, bf16[4,96,256]{2,1,0:T(8,128)(2,1)S(1)}, u32[]{:S(2)}, u32[]{:S(2)}) collective-permute-start(bf16[4,96,256]{2,1,0:T(8,128)(2,1)S(1)} %collective-permute-done.5.refs_7_), channel_id=1, source_target_pairs={{0,8},{8,0},{16,24},{24,16},{32,40},{40,32},{48,56},{56,48},{64,72... | collective-permute-start | bytes 589832 | tf_op jit(solution)/shard_map/ppermute | solution.py:49
  50.0 3.5 %copy-start.9 = (bf16[4,96,256]{2,1,0:T(8,128)(2,1)}, bf16[4,96,256]{2,1,0:T(8,128)(2,1)S(1)}, u32[]{:S(2)}) copy-start(bf16[4,96,256]{2,1,0:T(8,128)(2,1)S(1)} %collective-permute-done.7.refs_8_) | copy-start | bytes 589828
  53.6 0.7 copy-start.10
  59.4 6.1 %collective-permute-start.8 = (bf16[128,2304]{1,0:T(8,128)(2,1)}, bf16[128,2304]{1,0:T(8,128)(2,1)S(1)}, u32[]{:S(2)}, u32[]{:S(2)}) collective-permute-start(bf16[128,2304]{1,0:T(8,128)(2,1)} %get-tuple-element.16), channel_id=1, source_target_pairs={{0,1},{1,0},{2,3},{3,2},{4,5},{5,4},{6,7},{7,6},{8,9},{9,8},{10,11... | collective-permute-start | bytes 1769480 | tf_op jit(solution)/shard_map/ppermute | solution.py:36
  112.7 11.9 %copy-start.1 = (bf16[128,2944]{1,0:T(8,128)(2,1)}, bf16[128,2944]{1,0:T(8,128)(2,1)S(1)}, u32[]{:S(2)}) copy-start(bf16[128,2944]{1,0:T(8,128)(2,1)S(1)} %reshape.180.refs_1_) | copy-start | bytes 2260996
  112.7 11.8 %collective-permute-start.9 = (bf16[128,2944]{1,0:T(8,128)(2,1)S(1)}, bf16[128,2944]{1,0:T(8,128)(2,1)S(1)}, u32[]{:S(2)}, u32[]{:S(2)}) collective-permute-start(bf16[128,2944]{1,0:T(8,128)(2,1)S(1)} %reshape.180.refs_1_), channel_id=1, source_target_pairs={{0,1},{1,0},{2,3},{3,2},{4,5},{5,4},{6,7},{7,6},{8,9},{9,8},{10,11... | collective-permute-start | bytes 2261000 | tf_op jit(solution)/shard_map/ppermute | solution.py:36
  117.4 19.9 %all-to-all-start.2 = ((f32[8,1,2304]{2,1,0:T(1,128)}), f32[8,1,2304]{2,1,0:T(1,128)S(1)}, u32[]{:S(2)}, u32[]{:S(2)}) async-start(f32[8,1,2304]{2,1,0:T(1,128)} %broadcast_in_dim.36), calls=%async_computation.2 | async-start | bytes 147456 | tf_op jit(solution)/shard_map/all_to_all | solution.py:235
  124.5 0.9 copy-start.3

commit v10 on v9

--- a/solution.py
+++ b/solution.py
@@ -60,20 +60,24 @@
         band_ref[start * TILE : (start + 2) * TILE, :] = both
 
 
-def feature_kernel(nbasis, tile_count, *refs):
-    band_ref, cot_ref = refs[0], refs[1]
-    window_refs = refs[2:9]
-    features_ref, keep_ref, send_ref = refs[9:]
-    rows = window_refs[0].shape[0]
-    reach = band_ref.shape[1] // (7 * rows)
+def feature_kernel(nbasis, tile_count, core_ref, band_ref, cot_ref, near_ref, far_ref, *refs):
+    piece_refs = refs[:7]
+    features_ref, keep_ref, send_ref, window_ref = refs[7:]
+    rows, cols, _ = piece_refs[0].shape
+    window_rows = window_ref.shape[0]
+    reach = near_ref.shape[1]
+    span = band_ref.shape[1] // window_rows
     per_tile = rows * TILE
+    first = core_ref[0] == 0
+    for row in range(window_rows):
+        near, far = near_ref[row], far_ref[row]
+        window_ref[row, :reach, :] = jnp.where(first, far, near)
+        window_ref[row, reach : reach + cols, :] = piece_refs[row // rows][row % rows]
+        window_ref[row, reach + cols :, :] = jnp.where(first, near, far)
     band = band_ref[...]
     for tile in range(tile_count):
-        pieces = []
-        for ref in window_refs:
-            for row in range(rows):
-                pieces.append(ref[row, tile * TILE : tile * TILE + reach, :])
-        window = jnp.concatenate(pieces, axis=0)
+        window = window_ref[:, tile * TILE : tile * TILE + span, :]
+        window = window.reshape(window_rows * span, window.shape[2])
         summed = dot(band, window, ((1,), (0,))).astype(jnp.bfloat16)
         for k in range(nbasis):
             features_ref[k, tile * per_tile : (tile + 1) * per_tile, :] = summed[
@@ -156,13 +160,7 @@
     cot_cells = jnp.transpose(cotangent.reshape(rows, tile_count, TILE, outs), (1, 0, 2, 3))
     cot = dot(cot_order, cot_cells.reshape(cells, outs), ((1,), (1,))).astype(bf16)
 
-    low, high = fields[:, :reach], fields[:, cols - reach :]
-    near_edge = paired(jnp.where(core == 0, high, low), "lon", 0, True)
-    far_edge = paired(jnp.where(core == 0, low, high), "lon", 1, True)
-    left = jnp.where(core == 0, far_edge, near_edge)
-    right = jnp.where(core == 0, near_edge, far_edge)
-    own = jnp.concatenate([left, fields, right], axis=1)
-    near, far = own, own
+    near, far = fields, fields
     nears, fars = [], []
     for turn in range(3):
         if turn == 2:
@@ -170,7 +168,11 @@
         near, far = paired(far, "lat", 0, False), paired(near, "lat", 1, False)
         nears.append(near)
         fars.append(far)
-    windows = nears[::-1] + [own] + fars
+    pieces = nears[::-1] + [fields] + fars
+    low = jnp.concatenate([piece[:, :reach] for piece in pieces], axis=0)
+    high = jnp.concatenate([piece[:, cols - reach :] for piece in pieces], axis=0)
+    far_edge = paired(jnp.where(core == 0, low, high), "lon", 1, True)
+    near_edge = paired(jnp.where(core == 0, high, low), "lon", 0, True)
 
     features, keep, send = pl.pallas_call(
         lambda *refs: feature_kernel(nbasis, tile_count, *refs),
@@ -179,10 +181,11 @@
             jax.ShapeDtypeStruct((half, nbasis * channels), bf16),
             jax.ShapeDtypeStruct((half, nbasis * channels), bf16),
         ),
-        in_specs=vmem(9),
+        in_specs=[pl.BlockSpec(memory_space=pltpu.SMEM)] + vmem(11),
         out_specs=tuple(vmem(3)),
+        scratch_shapes=[pltpu.VMEM((window_rows, cols + 2 * reach, channels), bf16)],
         name="features",
-    )(band, cot, *windows)
+    )(core.reshape(1).astype(jnp.int32), band, cot, near_edge, far_edge, *pieces)
 
     f32 = jnp.float32
     length = nbasis * channels

time: 139 us -> 150 us (1.079)
  blocking collectives: 44.3 us -> 55.1 us
  waiting for transfers between devices: 17.6 us -> 22.5 us
  starting transfers between devices: 53.5 us -> 48.9 us
    all_to_all x2, blocking collectives: 44.3 us -> 55.1 us  [exchanged(): return lax.all_to_all(block, 'lat', 0, 0, axis_index_groups=members)]
    ppermute x8, starting transfers between devices: 38.2 us -> 33.4 us  [paired(): return lax.ppermute(block, axis, pairs)]
    ppermute x8, waiting for transfers between devices: 7.12 us -> 11.7 us  [paired(): return lax.ppermute(block, axis, pairs)]
    all_to_all x1, starting transfers between devices: 6.39 us -> 8.88 us  [shards(): arrived = lax.all_to_all(spread, 'lon', 0, 0)]
    ppermute x2, starting transfers between devices: 8.91 us -> 6.57 us  [swapped_core(): lax.ppermute(block, 'lon', [(i, i ^ 1) for i in range(lax.axis_size('lon'...]
    unnamed x29 -> x35, local copies, waits for them, and re-layouts: 2.88 us -> 3.15 us
  transfers between devices with their start and end apart: 11 -> 11, of which waited for: 4 -> 5; matrix products, arithmetic and copies ran while one was open for 3% -> 4% of each run, Pallas kernels for 4% -> 3%
where the time goes in v10:
time: 150 us; the launch traced here: 149 us
  blocking collectives  55.1 us (37%)
  starting transfers between devices  48.9 us (33%)
  waiting for transfers between devices  22.5 us (15%)
  Pallas kernels  10.2 us (7%)
  other arithmetic  5.24 us (3%)
  local copies, waits for them, and re-layouts  4.72 us (3%)
    all_to_all x2, blocking collectives, exchanged(): return lax.all_to_all(block, 'lat', 0, 0, axis_index_groups=members)  55.1 us
    ppermute x8, starting transfers between devices, paired(): return lax.ppermute(block, axis, pairs)  33.4 us
    ppermute x8, waiting for transfers between devices, paired(): return lax.ppermute(block, axis, pairs)  11.7 us
    all_to_all x1, starting transfers between devices, shards(): arrived = lax.all_to_all(spread, 'lon', 0, 0)  8.88 us
    all_to_all x1, waiting for transfers between devices, shards(): arrived = lax.all_to_all(spread, 'lon', 0, 0)  8.74 us
    ppermute x2, starting transfers between devices, swapped_core(): lax.ppermute(block, 'lon', [(i, i ^ 1) for i in range(lax.axis_size('lon'...  6.57 us
    pallas_call x1, Pallas kernels, shards(): pl.pallas_call(lambda *refs: feature_kernel(nbasis, tile_count, *refs), o...  5.21 us
    unnamed x35, local copies, waits for them, and re-layouts  3.15 us
  transfers between devices with their start and end apart: 11, of which 5 were waited for; matrix products, arithmetic and copies ran while one was open for 4% of the time, Pallas kernels for 3%

profile of v10, /device:TPU:1, one launch (start us, length us, event | category | flops | bytes accessed | tf_op | source)
XLA Modules:
  0.0 148.7 jit_solution(18204059166314717369)
XLA Ops:
  0.6 4.0 %collective-permute-start.2 = (bf16[4,72,256]{2,1,0:T(8,128)(2,1)}, bf16[4,72,256]{2,1,0:T(8,128)(2,1)S(1)}, u32[]{:S(2)}, u32[]{:S(2)}) collective-permute-start(bf16[4,72,256]{2,1,0:T(8,128)(2,1)} %refs_8_.1), channel_id=1, source_target_pairs={{0,8},{8,0},{16,24},{24,16},{32,40},{40,32},{48,56},{56,48},{64,72... | collective-permute-start | bytes 442376 | tf_op jit(solution)/shard_map/ppermute | solution.py:49
  5.4 0.8 broadcast_compare_fusion
  6.2 1.0 convert_bitcast_fusion
  9.1 1.9 %shard_map.68.refs_1_ = bf16[288,896]{1,0:T(8,128)(2,1)} custom-call(f32[36,896]{1,0:T(8,128)} %bitcast.40), custom_call_target="tpu_custom_call" | custom-call | tf_op jit(solution)/shard_map/pallas_call | solution.py:142
  11.1 7.0 %collective-permute-start.1 = (bf16[4,72,256]{2,1,0:T(8,128)(2,1)S(1)}, bf16[4,72,256]{2,1,0:T(8,128)(2,1)S(1)}, u32[]{:S(2)}, u32[]{:S(2)}) collective-permute-start(bf16[4,72,256]{2,1,0:T(8,128)(2,1)S(1)} %collective-permute-done.refs_9_), channel_id=1, source_target_pairs={{0,8},{8,0},{16,24},{24,16},{32,40},{40,32},{48,56},{56,48},{64,72... | collective-permute-start | bytes 442376 | tf_op jit(solution)/shard_map/ppermute | solution.py:49
  18.1 1.9 %collective-permute-start.4 = (bf16[4,72,256]{2,1,0:T(8,128)(2,1)S(1)}, bf16[4,72,256]{2,1,0:T(8,128)(2,1)S(1)}, u32[]{:S(2)}, u32[]{:S(2)}) collective-permute-start(bf16[4,72,256]{2,1,0:T(8,128)(2,1)S(1)} %collective-permute-done.3.refs_10_), channel_id=1, source_target_pairs={{0,8},{8,0},{16,24},{24,16},{32,40},{40,32},{48,56},{56,48},{64,72... | collective-permute-start | bytes 442376 | tf_op jit(solution)/shard_map/ppermute | solution.py:49
  20.0 0.9 convolution_convert_fusion.refs_2_
  21.0 0.8 collective-permute-done.1.refs_6_
  22.4 1.6 %collective-permute-done.4.refs_5_ = bf16[4,72,256]{2,1,0:T(8,128)(2,1)S(1)} collective-permute-done((bf16[4,72,256]{2,1,0:T(8,128)(2,1)S(1)}, bf16[4,72,256]{2,1,0:T(8,128)(2,1)S(1)}, u32[]{:S(2)}, u32[]{:S(2)}) %collective-permute-start.4) | collective-permute-done | bytes 147488 | tf_op jit(solution)/shard_map/ppermute | solution.py:49
  24.1 0.8 slice_dynamic-update-slice_fusion.12
  25.0 16.5 %collective-permute-start.6 = (bf16[28,12,256]{2,1,0:T(8,128)(2,1)S(1)}, bf16[28,12,256]{2,1,0:T(8,128)(2,1)S(1)}, u32[]{:S(2)}, u32[]{:S(2)}) collective-permute-start(bf16[28,12,256]{2,1,0:T(8,128)(2,1)S(1)} %get-tuple-element.27), channel_id=1, source_target_pairs={{0,1},{1,0},{2,3},{3,2},{4,5},{5,4},{6,7},{7,6},{8,9},{9,8},{10,11... | collective-permute-start | bytes 516104 | tf_op jit(solution)/shard_map/ppermute | solution.py:49
  41.5 1.9 %collective-permute-start.7 = (bf16[28,12,256]{2,1,0:T(8,128)(2,1)S(1)}, bf16[28,12,256]{2,1,0:T(8,128)(2,1)S(1)}, u32[]{:S(2)}, u32[]{:S(2)}) collective-permute-start(bf16[28,12,256]{2,1,0:T(8,128)(2,1)S(1)} %get-tuple-element.26), channel_id=1, source_target_pairs={{1,2},{2,1},{3,4},{4,3},{5,6},{6,5},{7,0},{0,7},{9,10},{10,9},{11,... | collective-permute-start | bytes 516104 | tf_op jit(solution)/shard_map/ppermute | solution.py:49
  43.5 9.3 %collective-permute-done.7.refs_4_ = bf16[28,12,256]{2,1,0:T(8,128)(2,1)S(1)} collective-permute-done((bf16[28,12,256]{2,1,0:T(8,128)(2,1)S(1)}, bf16[28,12,256]{2,1,0:T(8,128)(2,1)S(1)}, u32[]{:S(2)}, u32[]{:S(2)}) %collective-permute-start.7) | collective-permute-done | bytes 172064 | tf_op jit(solution)/shard_map/ppermute | solution.py:49
  53.4 5.2 %features.1 = (bf16[9,288,256]{2,1,0:T(8,128)(2,1)}, bf16[128,2304]{1,0:T(8,128)(2,1)}, bf16[128,2304]{1,0:T(8,128)(2,1)}) custom-call(s32[1]{0:T(128)} %bitcast.refs_0_, bf16[288,896]{1,0:T(8,128)(2,1)} %shard_map.68.refs_1_, bf16[256,288]{1,0:T(8,128)(2,1)} %convolution_convert_fusion.refs_2_, bf16[28,12,256]{2,1,0:T(8,128)(2,1)} %copy-done.9, ...), custom_call_target="tpu_custom_call" | custom-call | tf_op jit(solution)/shard_map/features/pallas_call | solution.py:177
  58.6 1.9 %collective-permute-start.8 = (bf16[128,2304]{1,0:T(8,128)(2,1)}, bf16[128,2304]{1,0:T(8,128)(2,1)S(1)}, u32[]{:S(2)}, u32[]{:S(2)}) collective-permute-start(bf16[128,2304]{1,0:T(8,128)(2,1)} %get-tuple-element.16), channel_id=1, source_target_pairs={{0,1},{1,0},{2,3},{3,2},{4,5},{5,4},{6,7},{7,6},{8,9},{9,8},{10,11... | collective-permute-start | bytes 1769480 | tf_op jit(solution)/shard_map/ppermute | solution.py:36
  60.7 2.1 %collective-permute-done.8 = bf16[128,2304]{1,0:T(8,128)(2,1)S(1)} collective-permute-done((bf16[128,2304]{1,0:T(8,128)(2,1)}, bf16[128,2304]{1,0:T(8,128)(2,1)S(1)}, u32[]{:S(2)}, u32[]{:S(2)}) %collective-permute-start.8) | collective-permute-done | bytes 589856 | tf_op jit(solution)/shard_map/ppermute | solution.py:36
  62.7 1.2 add_convert_fusion
  64.0 27.5 %all_to_all.15 = bf16[4,32,2432]{2,1,0:T(8,128)(2,1)S(1)} all-to-all(bf16[4,32,2432]{2,1,0:T(8,128)(2,1)S(1)} %pad_maximum_fusion.1), channel_id=1, replica_groups={{0,64,128,192},{8,72,136,200},{16,80,144,208},{24,88,152,216},{32,96,16..., dimensions={0} | all-to-all | bytes 1245184 | tf_op jit(solution)/shard_map/all_to_all | solution.py:196
  92.3 27.5 %all_to_all.16 = bf16[32,4,2944]{2,1,0:T(4,128)(2,1)S(1)} all-to-all(bf16[32,4,2944]{2,1,0:T(4,128)(2,1)S(1)} %pad_maximum_fusion), channel_id=1, replica_groups={{0,8,16,24,32,40,48,56,256,264,272,280,288,296,304,312,512,520,528,536,..., dimensions={0} | all-to-all | bytes 1507328 | tf_op jit(solution)/shard_map/all_to_all | solution.py:196
  120.8 4.7 %collective-permute-start.9 = (bf16[128,2944]{1,0:T(8,128)(2,1)S(1)}, bf16[128,2944]{1,0:T(8,128)(2,1)S(1)}, u32[]{:S(2)}, u32[]{:S(2)}) collective-permute-start(bf16[128,2944]{1,0:T(8,128)(2,1)S(1)} %reshape.184.refs_1_), channel_id=1, source_target_pairs={{0,1},{1,0},{2,3},{3,2},{4,5},{5,4},{6,7},{7,6},{8,9},{9,8},{10,11... | collective-permute-start | bytes 2261000 | tf_op jit(solution)/shard_map/ppermute | solution.py:36
  125.5 8.9 %all-to-all-start.2 = ((f32[8,1,2304]{2,1,0:T(1,128)}), f32[8,1,2304]{2,1,0:T(1,128)S(1)}, u32[]{:S(2)}, u32[]{:S(2)}) async-start(f32[8,1,2304]{2,1,0:T(1,128)} %broadcast_in_dim.36), calls=%async_computation.2 | async-start | bytes 147456 | tf_op jit(solution)/shard_map/all_to_all | solution.py:238
  135.1 0.9 copy-done.2
  136.0 3.1 %mixing.1 = bf16[4,72,256]{2,1,0:T(8,128)(2,1)} custom-call(bf16[9,288,256]{2,1,0:T(8,128)(2,1)} %get-tuple-element.18.refs_0_, bf16[128,2944]{1,0:T(8,128)(2,1)} %copy-done.1, bf16[128,2944]{1,0:T(8,128)(2,1)} %copy-done.2, bf16[256,256]{1,0:T(8,128)(2,1)} %fusion.refs_3_), custom_call_target="tpu_custom_call" | custom-call | flops 377487360 | bytes 5308416 | tf_op jit(solution)/shard_map/mixing/pallas_call | solution.py:227
  139.1 8.7 %all-to-all-done.2 = f32[8,1,2304]{2,1,0:T(1,128)S(1)} async-done(((f32[8,1,2304]{2,1,0:T(1,128)}), f32[8,1,2304]{2,1,0:T(1,128)S(1)}, u32[]{:S(2)}, u32[]{:S(2)}) %all-to-all-start.2) | async-done | bytes 73760 | tf_op jit(solution)/shard_map/all_to_all | solution.py:238
  (74 shorter events, 7.3 us)
Async XLA Ops:
  0.6 59.9 %copy-start = (bf16[2,2304]{1,0:T(2,128)(2,1)S(1)}, bf16[2,2304]{1,0:T(2,128)(2,1)}, u32[]{:S(2)}) copy-start(bf16[2,2304]{1,0:T(2,128)(2,1)} %param.8) | copy-start | bytes 27652
  0.6 7.0 %collective-permute-start.2 = (bf16[4,72,256]{2,1,0:T(8,128)(2,1)}, bf16[4,72,256]{2,1,0:T(8,128)(2,1)S(1)}, u32[]{:S(2)}, u32[]{:S(2)}) collective-permute-start(bf16[4,72,256]{2,1,0:T(8,128)(2,1)} %refs_8_.1), channel_id=1, source_target_pairs={{0,8},{8,0},{16,24},{24,16},{32,40},{40,32},{48,56},{56,48},{64,72... | collective-permute-start | bytes 442376 | tf_op jit(solution)/shard_map/ppermute | solution.py:49
  4.7 6.4 %collective-permute-start = (bf16[4,72,256]{2,1,0:T(8,128)(2,1)}, bf16[4,72,256]{2,1,0:T(8,128)(2,1)S(1)}, u32[]{:S(2)}, u32[]{:S(2)}) collective-permute-start(bf16[4,72,256]{2,1,0:T(8,128)(2,1)} %refs_8_.1), channel_id=1, source_target_pairs={{8,16},{16,8},{24,32},{32,24},{40,48},{48,40},{56,64},{64,56},{72,... | collective-permute-start | bytes 442376 | tf_op jit(solution)/shard_map/ppermute | solution.py:49
  7.4 3.6 %copy-start.11 = (bf16[4,72,256]{2,1,0:T(8,128)(2,1)S(1)}, bf16[4,72,256]{2,1,0:T(8,128)(2,1)}, u32[]{:S(2)}) copy-start(bf16[4,72,256]{2,1,0:T(8,128)(2,1)} %param.9) | copy-start | bytes 442372
  7.7 16.4 %copy-start.3 = (bf16[4,72,256]{2,1,0:T(8,128)(2,1)}, bf16[4,72,256]{2,1,0:T(8,128)(2,1)S(1)}, u32[]{:S(2)}) copy-start(bf16[4,72,256]{2,1,0:T(8,128)(2,1)S(1)} %collective-permute-done.2.refs_7_) | copy-start | bytes 442372
  7.7 10.4 %collective-permute-start.3 = (bf16[4,72,256]{2,1,0:T(8,128)(2,1)S(1)}, bf16[4,72,256]{2,1,0:T(8,128)(2,1)S(1)}, u32[]{:S(2)}, u32[]{:S(2)}) collective-permute-start(bf16[4,72,256]{2,1,0:T(8,128)(2,1)S(1)} %collective-permute-done.2.refs_7_), channel_id=1, source_target_pairs={{8,16},{16,8},{24,32},{32,24},{40,48},{48,40},{56,64},{64,56},{72,... | collective-permute-start | bytes 442376 | tf_op jit(solution)/shard_map/ppermute | solution.py:49
  11.1 41.7 %copy-start.4 = (bf16[4,72,256]{2,1,0:T(8,128)(2,1)}, bf16[4,72,256]{2,1,0:T(8,128)(2,1)S(1)}, u32[]{:S(2)}) copy-start(bf16[4,72,256]{2,1,0:T(8,128)(2,1)S(1)} %collective-permute-done.refs_9_) | copy-start | bytes 442372
  11.1 10.7 %collective-permute-start.1 = (bf16[4,72,256]{2,1,0:T(8,128)(2,1)S(1)}, bf16[4,72,256]{2,1,0:T(8,128)(2,1)S(1)}, u32[]{:S(2)}, u32[]{:S(2)}) collective-permute-start(bf16[4,72,256]{2,1,0:T(8,128)(2,1)S(1)} %collective-permute-done.refs_9_), channel_id=1, source_target_pairs={{0,8},{8,0},{16,24},{24,16},{32,40},{40,32},{48,56},{56,48},{64,72... | collective-permute-start | bytes 442376 | tf_op jit(solution)/shard_map/ppermute | solution.py:49
  18.1 34.7 %copy-start.5 = (bf16[4,72,256]{2,1,0:T(8,128)(2,1)}, bf16[4,72,256]{2,1,0:T(8,128)(2,1)S(1)}, u32[]{:S(2)}) copy-start(bf16[4,72,256]{2,1,0:T(8,128)(2,1)S(1)} %collective-permute-done.3.refs_10_) | copy-start | bytes 442372
  18.1 5.9 %collective-permute-start.4 = (bf16[4,72,256]{2,1,0:T(8,128)(2,1)S(1)}, bf16[4,72,256]{2,1,0:T(8,128)(2,1)S(1)}, u32[]{:S(2)}, u32[]{:S(2)}) collective-permute-start(bf16[4,72,256]{2,1,0:T(8,128)(2,1)S(1)} %collective-permute-done.3.refs_10_), channel_id=1, source_target_pairs={{0,8},{8,0},{16,24},{24,16},{32,40},{40,32},{48,56},{56,48},{64,72... | collective-permute-start | bytes 442376 | tf_op jit(solution)/shard_map/ppermute | solution.py:49
  21.7 31.0 %copy-start.6 = (bf16[4,72,256]{2,1,0:T(8,128)(2,1)}, bf16[4,72,256]{2,1,0:T(8,128)(2,1)S(1)}, u32[]{:S(2)}) copy-start(bf16[4,72,256]{2,1,0:T(8,128)(2,1)S(1)} %collective-permute-done.1.refs_6_) | copy-start | bytes 442372
  21.7 3.1 %collective-permute-start.5 = (bf16[4,72,256]{2,1,0:T(8,128)(2,1)S(1)}, bf16[4,72,256]{2,1,0:T(8,128)(2,1)S(1)}, u32[]{:S(2)}, u32[]{:S(2)}) collective-permute-start(bf16[4,72,256]{2,1,0:T(8,128)(2,1)S(1)} %collective-permute-done.1.refs_6_), channel_id=1, source_target_pairs={{8,16},{16,8},{24,32},{32,24},{40,48},{48,40},{56,64},{64,56},{72,... | collective-permute-start | bytes 442376 | tf_op jit(solution)/shard_map/ppermute | solution.py:49
  24.0 28.8 %copy-start.7 = (bf16[4,72,256]{2,1,0:T(8,128)(2,1)}, bf16[4,72,256]{2,1,0:T(8,128)(2,1)S(1)}, u32[]{:S(2)}) copy-start(bf16[4,72,256]{2,1,0:T(8,128)(2,1)S(1)} %collective-permute-done.4.refs_5_) | copy-start | bytes 442372
  24.9 27.9 %copy-start.8 = (bf16[4,72,256]{2,1,0:T(8,128)(2,1)}, bf16[4,72,256]{2,1,0:T(8,128)(2,1)S(1)}, u32[]{:S(2)}) copy-start(bf16[4,72,256]{2,1,0:T(8,128)(2,1)S(1)} %collective-permute-done.5.refs_11_) | copy-start | bytes 442372
  25.0 18.5 %collective-permute-start.6 = (bf16[28,12,256]{2,1,0:T(8,128)(2,1)S(1)}, bf16[28,12,256]{2,1,0:T(8,128)(2,1)S(1)}, u32[]{:S(2)}, u32[]{:S(2)}) collective-permute-start(bf16[28,12,256]{2,1,0:T(8,128)(2,1)S(1)} %get-tuple-element.27), channel_id=1, source_target_pairs={{0,1},{1,0},{2,3},{3,2},{4,5},{5,4},{6,7},{7,6},{8,9},{9,8},{10,11... | collective-permute-start | bytes 516104 | tf_op jit(solution)/shard_map/ppermute | solution.py:49
  41.5 11.2 %collective-permute-start.7 = (bf16[28,12,256]{2,1,0:T(8,128)(2,1)S(1)}, bf16[28,12,256]{2,1,0:T(8,128)(2,1)S(1)}, u32[]{:S(2)}, u32[]{:S(2)}) collective-permute-start(bf16[28,12,256]{2,1,0:T(8,128)(2,1)S(1)} %get-tuple-element.26), channel_id=1, source_target_pairs={{1,2},{2,1},{3,4},{4,3},{5,6},{6,5},{7,0},{0,7},{9,10},{10,9},{11,... | collective-permute-start | bytes 516104 | tf_op jit(solution)/shard_map/ppermute | solution.py:49
  43.5 9.3 %copy-start.9 = (bf16[28,12,256]{2,1,0:T(8,128)(2,1)}, bf16[28,12,256]{2,1,0:T(8,128)(2,1)S(1)}, u32[]{:S(2)}) copy-start(bf16[28,12,256]{2,1,0:T(8,128)(2,1)S(1)} %collective-permute-done.6.refs_3_) | copy-start | bytes 516100
  52.8 0.7 copy-start.10
  58.6 4.1 %collective-permute-start.8 = (bf16[128,2304]{1,0:T(8,128)(2,1)}, bf16[128,2304]{1,0:T(8,128)(2,1)S(1)}, u32[]{:S(2)}, u32[]{:S(2)}) collective-permute-start(bf16[128,2304]{1,0:T(8,128)(2,1)} %get-tuple-element.16), channel_id=1, source_target_pairs={{0,1},{1,0},{2,3},{3,2},{4,5},{5,4},{6,7},{7,6},{8,9},{9,8},{10,11... | collective-permute-start | bytes 1769480 | tf_op jit(solution)/shard_map/ppermute | solution.py:36
  120.8 14.3 %copy-start.1 = (bf16[128,2944]{1,0:T(8,128)(2,1)}, bf16[128,2944]{1,0:T(8,128)(2,1)S(1)}, u32[]{:S(2)}) copy-start(bf16[128,2944]{1,0:T(8,128)(2,1)S(1)} %reshape.184.refs_1_) | copy-start | bytes 2260996
  120.8 14.3 %collective-permute-start.9 = (bf16[128,2944]{1,0:T(8,128)(2,1)S(1)}, bf16[128,2944]{1,0:T(8,128)(2,1)S(1)}, u32[]{:S(2)}, u32[]{:S(2)}) collective-permute-start(bf16[128,2944]{1,0:T(8,128)(2,1)S(1)} %reshape.184.refs_1_), channel_id=1, source_target_pairs={{0,1},{1,0},{2,3},{3,2},{4,5},{5,4},{6,7},{7,6},{8,9},{9,8},{10,11... | collective-permute-start | bytes 2261000 | tf_op jit(solution)/shard_map/ppermute | solution.py:36
  125.5 22.4 %all-to-all-start.2 = ((f32[8,1,2304]{2,1,0:T(1,128)}), f32[8,1,2304]{2,1,0:T(1,128)S(1)}, u32[]{:S(2)}, u32[]{:S(2)}) async-start(f32[8,1,2304]{2,1,0:T(1,128)} %broadcast_in_dim.36), calls=%async_computation.2 | async-start | bytes 147456 | tf_op jit(solution)/shard_map/all_to_all | solution.py:238
  135.1 0.9 copy-start.2
